TPU v7x, 32 devices: a whole 2x2x4 slice. The times are simulated.
32 devices in a mesh: dp: 16 (over z, x, core), sp: 2 (over y).
Axes of the slice: x: 2, y: 2, z: 4, core: 2. Of those that a mesh axis runs over, the one named last changes fastest.
Arguments:
- tokens: bfloat16 [2, 32768, 1024], P(None, ('dp', 'sp')), may hold values from -6 to 6
- doc_lengths: int32 [16, 2, 4], P('dp'), may hold values from 0 to 2048, as said below
- out_cotangent: bfloat16 [2, 32768, 1024], P(None, ('dp', 'sp')), may hold values from -6 to 6
- in_gain: bfloat16 [1024], P(('dp', 'sp')), may hold values from 0.099609375 to 1.8984375
- in_bias: bfloat16 [1024], P(('dp', 'sp')), may hold values from -3 to 3
- qkv_weight: bfloat16 [1024, 3072], P(('dp', 'sp')), may hold values from -0.1875 to 0.1875
- q_bias: bfloat16 [1024], P(('dp', 'sp')), may hold values from -3 to 3
- v_bias: bfloat16 [1024], P(('dp', 'sp')), may hold values from -3 to 3
- head_scale: bfloat16 [16], P('sp'), may hold values from 0.5 to 2
- attn_gain: bfloat16 [1024], P(('dp', 'sp')), may hold values from 0.099609375 to 1.8984375
- attn_bias: bfloat16 [1024], P(('dp', 'sp')), may hold values from -3 to 3
- out_weight: bfloat16 [1024, 1024], P(('dp', 'sp')), may hold values from -0.1875 to 0.1875
- out_bias: bfloat16 [1024], P(('dp', 'sp')), may hold values from -3 to 3
- ffn_gain: bfloat16 [1024], P(('dp', 'sp')), may hold values from 0.099609375 to 1.8984375
- ffn_bias: bfloat16 [1024], P(('dp', 'sp')), may hold values from -3 to 3
- fc1_weight: bfloat16 [1024, 4096], P(('dp', 'sp')), may hold values from -0.1875 to 0.1875
- fc1_bias: bfloat16 [4096], P(('dp', 'sp')), may hold values from -3 to 3
- mid_gain: bfloat16 [4096], P(('dp', 'sp')), may hold values from 0.099609375 to 1.8984375
- mid_bias: bfloat16 [4096], P(('dp', 'sp')), may hold values from -3 to 3
- fc2_weight: bfloat16 [4096, 1024], P(('dp', 'sp')), may hold values from -0.09375 to 0.09375
- fc2_bias: bfloat16 [1024], P(('dp', 'sp')), may hold values from -3 to 3
Outputs:
- layer_out: bfloat16 [2, 32768, 1024], P(None, ('dp', 'sp'))
- input_grad: float32 [2, 32768, 1024], P(None, ('dp', 'sp'))
- in_gain_grad: float32 [1024], P(('dp', 'sp'))
- in_bias_grad: float32 [1024], P(('dp', 'sp'))
- qkv_weight_grad: float32 [1024, 3072], P(('dp', 'sp'))
- q_bias_grad: float32 [1024], P(('dp', 'sp'))
- v_bias_grad: float32 [1024], P(('dp', 'sp'))
- head_scale_grad: float32 [16], P('sp')
- attn_gain_grad: float32 [1024], P(('dp', 'sp'))
- attn_bias_grad: float32 [1024], P(('dp', 'sp'))
- out_weight_grad: float32 [1024, 1024], P(('dp', 'sp'))
- out_bias_grad: float32 [1024], P(('dp', 'sp'))
- ffn_gain_grad: float32 [1024], P(('dp', 'sp'))
- ffn_bias_grad: float32 [1024], P(('dp', 'sp'))
- fc1_weight_grad: float32 [1024, 4096], P(('dp', 'sp'))
- fc1_bias_grad: float32 [4096], P(('dp', 'sp'))
- mid_gain_grad: float32 [4096], P(('dp', 'sp'))
- mid_bias_grad: float32 [4096], P(('dp', 'sp'))
- fc2_weight_grad: float32 [4096, 1024], P(('dp', 'sp'))
- fc2_bias_grad: float32 [1024], P(('dp', 'sp'))
Inputs may be any that keep to these rules, and one draw needn't show every extreme that they name: `doc_lengths`: entries 4 w to 4 w + 3 of row [g, m] list, in order and followed by zeros, the lengths of the sequences packed into window w of 2048 tokens of group g's buffer of micro-batch m, each 512, 1024 or 2048, summing to 2048; in every micro-batch at least one group holds a single sequence of 2048 tokens in every window.
All inputs are finite; a program needn't handle non-finite values.
Results may differ from a plain program's by a relative error of at most 0.018.
Values may be sent and summed in bfloat16 or wider, within the bound.
A program may use at most 448 MiB of HBM per device.

v0:
```python
import math

import jax
import jax.numpy as jnp
from jax import lax
from jax.sharding import PartitionSpec as P

LONGEST = 2048


EPS = 1e-05


def layer_norm(values, norm_gain, norm_shift):
    center = values - jnp.mean(values, axis=-1, keepdims=True)
    spread = jnp.mean(center * center, axis=-1, keepdims=True)
    return center * lax.rsqrt(spread + EPS) * norm_gain + norm_shift


def doc_index(lengths, row_count):
    seq_ends = jnp.cumsum(lengths)
    places = jnp.arange(row_count, dtype=jnp.int32)
    return jnp.sum((places[:, None] >= seq_ends[None, :]).astype(jnp.int32), axis=1)


def block_scores(query_block, key_heads, doc_query, doc_keys, pos_query, pos_keys, score_scale):
    scores = (
        jnp.einsum("qhd,khd->hqk", query_block, key_heads, preferred_element_type=jnp.float32)
        * score_scale
    )
    allowed = (doc_query[:, None] == doc_keys[None, :]) & (pos_keys[None, :] <= pos_query[:, None])
    return jnp.where(allowed[None], scores, -1e30)


def reduce_grads(grad_set):
    return (
        lax.psum_scatter(grad_set[0], ("dp", "sp"), scatter_dimension=0, tiled=True),
        lax.psum_scatter(grad_set[1], ("dp", "sp"), scatter_dimension=0, tiled=True),
        lax.psum_scatter(grad_set[2], ("dp", "sp"), scatter_dimension=0, tiled=True),
        lax.psum_scatter(grad_set[3], ("dp", "sp"), scatter_dimension=0, tiled=True),
        lax.psum_scatter(grad_set[4], ("dp", "sp"), scatter_dimension=0, tiled=True),
        lax.psum_scatter(grad_set[5], ("dp", "sp"), scatter_dimension=0, tiled=True),
        lax.psum_scatter(grad_set[6], ("dp", "sp"), scatter_dimension=0, tiled=True),
        lax.psum_scatter(grad_set[7], ("dp", "sp"), scatter_dimension=0, tiled=True),
        lax.psum_scatter(grad_set[8], ("dp", "sp"), scatter_dimension=0, tiled=True),
        lax.psum_scatter(grad_set[9], ("dp", "sp"), scatter_dimension=0, tiled=True),
        lax.psum_scatter(grad_set[10], ("dp", "sp"), scatter_dimension=0, tiled=True),
        lax.psum_scatter(grad_set[11], ("dp", "sp"), scatter_dimension=0, tiled=True),
        lax.psum_scatter(grad_set[12], ("dp", "sp"), scatter_dimension=0, tiled=True),
        lax.psum_scatter(grad_set[13], ("dp", "sp"), scatter_dimension=0, tiled=True),
        lax.psum_scatter(grad_set[14], ("dp", "sp"), scatter_dimension=0, tiled=True),
        lax.psum_scatter(grad_set[15], ("dp", "sp"), scatter_dimension=0, tiled=True),
        lax.psum_scatter(grad_set[16], ("dp", "sp"), scatter_dimension=0, tiled=True),
    )


def shards(
    tokens,
    doc_lengths,
    out_cotangent,
    in_gain,
    in_bias,
    qkv_weight,
    q_bias,
    v_bias,
    head_scale,
    attn_gain,
    attn_bias,
    out_weight,
    out_bias,
    ffn_gain,
    ffn_bias,
    fc1_weight,
    fc1_bias,
    mid_gain,
    mid_bias,
    fc2_weight,
    fc2_bias,
):
    micro_count = tokens.shape[0]
    tok_count = tokens.shape[1]
    model_width = tokens.shape[2]
    sp_count = lax.axis_size("sp")
    group_rows = tok_count * sp_count
    local_width = model_width // sp_count
    head_local = head_scale.shape[0]
    head_dim = local_width // head_local
    score_scale = 1.0 / math.sqrt(head_dim)
    window_rows = LONGEST
    block_rows = min(512, window_rows)
    block_count = group_rows // block_rows
    head_gains = head_scale.astype(jnp.float32)
    positions = jnp.arange(group_rows, dtype=jnp.int32)
    starts = jnp.arange(block_count, dtype=jnp.int32) * block_rows

    def collect():
        return (
            lax.all_gather(in_gain, ("dp", "sp"), axis=0, tiled=True),
            lax.all_gather(in_bias, ("dp", "sp"), axis=0, tiled=True),
            lax.all_gather(qkv_weight, ("dp", "sp"), axis=0, tiled=True),
            lax.all_gather(q_bias, ("dp", "sp"), axis=0, tiled=True),
            lax.all_gather(v_bias, ("dp", "sp"), axis=0, tiled=True),
            lax.all_gather(attn_gain, ("dp", "sp"), axis=0, tiled=True),
            lax.all_gather(attn_bias, ("dp", "sp"), axis=0, tiled=True),
            lax.all_gather(out_weight, ("dp", "sp"), axis=0, tiled=True),
            lax.all_gather(out_bias, ("dp", "sp"), axis=0, tiled=True),
            lax.all_gather(ffn_gain, ("dp", "sp"), axis=0, tiled=True),
            lax.all_gather(ffn_bias, ("dp", "sp"), axis=0, tiled=True),
            lax.all_gather(fc1_weight, ("dp", "sp"), axis=0, tiled=True),
            lax.all_gather(fc1_bias, ("dp", "sp"), axis=0, tiled=True),
            lax.all_gather(mid_gain, ("dp", "sp"), axis=0, tiled=True),
            lax.all_gather(mid_bias, ("dp", "sp"), axis=0, tiled=True),
            lax.all_gather(fc2_weight, ("dp", "sp"), axis=0, tiled=True),
            lax.all_gather(fc2_bias, ("dp", "sp"), axis=0, tiled=True),
        )

    def split_heads(heads_in):
        query_heads = heads_in[:, 0].reshape(group_rows, head_local, head_dim)
        key_heads = heads_in[:, 1].reshape(group_rows, head_local, head_dim)
        value_heads = heads_in[:, 2].reshape(group_rows, head_local, head_dim)
        return (query_heads, key_heads, value_heads)

    def attend_back(heads_in, lengths, log_total, grad_mixed):
        query_heads, key_heads, value_heads = split_heads(heads_in)
        doc_ids = doc_index(lengths, group_rows)

        def one_block(block_carry, pair):
            grad_keys, grad_values = block_carry
            row_start, block_lse = pair
            query_block = lax.dynamic_slice_in_dim(query_heads, row_start, block_rows, 0)
            grad_block = lax.dynamic_slice_in_dim(grad_mixed, row_start, block_rows, 0)
            masked = block_scores(
                query_block,
                key_heads,
                lax.dynamic_slice_in_dim(doc_ids, row_start, block_rows, 0),
                doc_ids,
                lax.dynamic_slice_in_dim(positions, row_start, block_rows, 0),
                positions,
                score_scale,
            )
            prob_rows = jnp.exp(masked - block_lse[:, :, None])
            value_part = jnp.einsum(
                "hqk,qhd->khd",
                prob_rows.astype(jnp.bfloat16),
                grad_block,
                preferred_element_type=jnp.float32,
            )
            grad_probs = jnp.einsum(
                "qhd,khd->hqk", grad_block, value_heads, preferred_element_type=jnp.float32
            )
            row_inner = jnp.sum(prob_rows * grad_probs, axis=-1, keepdims=True)
            grad_scores = (prob_rows * (grad_probs - row_inner)).astype(jnp.bfloat16)
            grad_query = (
                jnp.einsum(
                    "hqk,khd->qhd", grad_scores, key_heads, preferred_element_type=jnp.float32
                )
                * score_scale
            )
            key_part = jnp.einsum(
                "hqk,qhd->khd", grad_scores, query_block, preferred_element_type=jnp.float32
            )
            grad_keys = grad_keys + key_part
            grad_values = grad_values + value_part
            return ((grad_keys, grad_values), grad_query)

        zero_heads = jnp.zeros((group_rows, head_local, head_dim), jnp.float32)
        (grad_keys, grad_values), grad_queries = lax.scan(
            one_block, (zero_heads, zero_heads), (starts, log_total)
        )
        stacked = jnp.stack(
            [
                grad_queries.reshape(group_rows, local_width),
                (grad_keys * score_scale).reshape(group_rows, local_width),
                grad_values.reshape(group_rows, local_width),
            ],
            axis=1,
        )
        return stacked.astype(jnp.bfloat16)

    outputs = []
    input_grads = []
    total_grads = None
    scale_total = jnp.zeros((head_local,), jnp.float32)
    for micro_index in range(micro_count):
        forward_set = collect()
        (
            forward_wide_in_gain,
            forward_wide_in_bias,
            forward_wide_qkv,
            forward_wide_q_bias,
            forward_wide_v_bias,
            forward_wide_attn_gain,
            forward_wide_attn_bias,
            forward_wide_out,
            forward_wide_out_bias,
            forward_wide_ffn_gain,
            forward_wide_ffn_bias,
            forward_wide_fc1,
            forward_wide_fc1_bias,
            forward_wide_mid_gain,
            forward_wide_mid_bias,
            forward_wide_fc2,
            forward_wide_fc2_bias,
        ) = forward_set
        forward_tok_rows = tokens[micro_index].astype(jnp.float32)
        forward_lengths = doc_lengths[0, micro_index]
        forward_normed = layer_norm(
            forward_tok_rows,
            forward_wide_in_gain.astype(jnp.float32),
            forward_wide_in_bias.astype(jnp.float32),
        ).astype(jnp.bfloat16)
        bias_row = jnp.concatenate(
            [forward_wide_q_bias, jnp.zeros_like(forward_wide_q_bias), forward_wide_v_bias]
        ).astype(jnp.float32)
        projected = (
            jnp.dot(forward_normed, forward_wide_qkv, preferred_element_type=jnp.float32) + bias_row
        )
        qkv_sent = projected.astype(jnp.bfloat16).reshape(tok_count, 3, model_width)
        forward_heads_in = lax.all_to_all(qkv_sent, "sp", split_axis=2, concat_axis=0, tiled=True)
        attend_query_heads, attend_key_heads, attend_value_heads = split_heads(forward_heads_in)
        attend_doc_ids = doc_index(forward_lengths, group_rows)

        def attend_one_block(row_start):
            query_block = lax.dynamic_slice_in_dim(attend_query_heads, row_start, block_rows, 0)
            masked = block_scores(
                query_block,
                attend_key_heads,
                lax.dynamic_slice_in_dim(attend_doc_ids, row_start, block_rows, 0),
                attend_doc_ids,
                lax.dynamic_slice_in_dim(positions, row_start, block_rows, 0),
                positions,
                score_scale,
            )
            row_max = jnp.max(masked, axis=-1, keepdims=True)
            raised = jnp.exp(masked - row_max)
            row_total = jnp.sum(raised, axis=-1, keepdims=True)
            prob_rows = (raised / row_total).astype(jnp.bfloat16)
            head_mixed = jnp.einsum(
                "hqk,khd->qhd", prob_rows, attend_value_heads, preferred_element_type=jnp.float32
            )
            return (head_mixed, (row_max + jnp.log(row_total))[:, :, 0])

        head_mixed, attend_log_total = lax.map(attend_one_block, starts)
        forward_head_mixed = head_mixed.reshape(group_rows, head_local, head_dim)
        scaled = (
            (forward_head_mixed * head_gains[None, :, None])
            .reshape(group_rows, local_width)
            .astype(jnp.bfloat16)
        )
        forward_attn_rows = lax.all_to_all(
            scaled, "sp", split_axis=0, concat_axis=1, tiled=True
        ).astype(jnp.float32)
        forward_post_norm = layer_norm(
            forward_attn_rows,
            forward_wide_attn_gain.astype(jnp.float32),
            forward_wide_attn_bias.astype(jnp.float32),
        ).astype(jnp.bfloat16)
        forward_hidden = (
            forward_tok_rows
            + jnp.dot(forward_post_norm, forward_wide_out, preferred_element_type=jnp.float32)
            + forward_wide_out_bias.astype(jnp.float32)
        )
        forward_ffn_in = layer_norm(
            forward_hidden,
            forward_wide_ffn_gain.astype(jnp.float32),
            forward_wide_ffn_bias.astype(jnp.float32),
        ).astype(jnp.bfloat16)
        forward_ffn_inner = jnp.dot(
            forward_ffn_in, forward_wide_fc1, preferred_element_type=jnp.float32
        ) + forward_wide_fc1_bias.astype(jnp.float32)
        forward_active = layer_norm(
            jax.nn.gelu(forward_ffn_inner),
            forward_wide_mid_gain.astype(jnp.float32),
            forward_wide_mid_bias.astype(jnp.float32),
        ).astype(jnp.bfloat16)
        output = (
            forward_hidden
            + jnp.dot(forward_active, forward_wide_fc2, preferred_element_type=jnp.float32)
            + forward_wide_fc2_bias.astype(jnp.float32)
        )
        forward_kept_values = (
            forward_normed,
            forward_heads_in,
            forward_head_mixed,
            attend_log_total,
            forward_attn_rows,
            forward_post_norm,
            forward_hidden,
            forward_ffn_in,
            forward_ffn_inner,
            forward_active,
        )
        output, kept_values = (output, forward_kept_values)
        backward_set = collect()
        (
            wide_in_gain,
            wide_in_bias,
            wide_qkv,
            wide_q_bias,
            wide_v_bias,
            wide_attn_gain,
            wide_attn_bias,
            wide_out,
            wide_out_bias,
            wide_ffn_gain,
            wide_ffn_bias,
            wide_fc1,
            wide_fc1_bias,
            wide_mid_gain,
            wide_mid_bias,
            wide_fc2,
            wide_fc2_bias,
        ) = backward_set
        (
            normed,
            backward_heads_in,
            backward_head_mixed,
            backward_log_total,
            attn_rows,
            post_norm,
            hidden,
            ffn_in,
            ffn_inner,
            active,
        ) = kept_values
        tok_rows = tokens[micro_index].astype(jnp.float32)
        backward_lengths = doc_lengths[0, micro_index]
        grad_out = out_cotangent[micro_index].astype(jnp.float32)
        fc2_bias_grad = jnp.sum(grad_out, axis=0)
        grad_low = grad_out.astype(jnp.bfloat16)
        fc2_grad = jnp.einsum("ti,tj->ij", active, grad_low, preferred_element_type=jnp.float32)
        grad_active = jnp.einsum(
            "tj,ij->ti", grad_low, wide_fc2, preferred_element_type=jnp.float32
        )
        gelu_out, gelu_back = jax.vjp(jax.nn.gelu, ffn_inner)
        _, mid_back = jax.vjp(
            layer_norm,
            gelu_out,
            wide_mid_gain.astype(jnp.float32),
            wide_mid_bias.astype(jnp.float32),
        )
        grad_gelu, mid_gain_grad, mid_bias_grad = mid_back(grad_active)
        (grad_inner,) = gelu_back(grad_gelu)
        inner_low = grad_inner.astype(jnp.bfloat16)
        fc1_bias_grad = jnp.sum(inner_low.astype(jnp.float32), axis=0)
        fc1_grad = jnp.einsum("ti,tj->ij", ffn_in, inner_low, preferred_element_type=jnp.float32)
        grad_ffn = jnp.einsum("tj,ij->ti", inner_low, wide_fc1, preferred_element_type=jnp.float32)
        _, ffn_back = jax.vjp(
            layer_norm, hidden, wide_ffn_gain.astype(jnp.float32), wide_ffn_bias.astype(jnp.float32)
        )
        grad_hid, ffn_gain_grad, ffn_bias_grad = ffn_back(grad_ffn)
        grad_hidden = grad_out + grad_hid
        out_bias_grad = jnp.sum(grad_hidden, axis=0)
        hidden_low = grad_hidden.astype(jnp.bfloat16)
        out_grad = jnp.einsum(
            "ti,tj->ij", post_norm, hidden_low, preferred_element_type=jnp.float32
        )
        grad_post = jnp.einsum(
            "tj,ij->ti", hidden_low, wide_out, preferred_element_type=jnp.float32
        )
        _, attn_back = jax.vjp(
            layer_norm,
            attn_rows,
            wide_attn_gain.astype(jnp.float32),
            wide_attn_bias.astype(jnp.float32),
        )
        grad_attn, attn_gain_grad, attn_bias_grad = attn_back(grad_post)
        grad_heads = lax.all_to_all(
            grad_attn.astype(jnp.bfloat16), "sp", split_axis=1, concat_axis=0, tiled=True
        )
        grad_scaled = grad_heads.astype(jnp.float32).reshape(group_rows, head_local, head_dim)
        scale_grad = jnp.sum(grad_scaled * backward_head_mixed, axis=(0, 2))
        backward_grad_mixed = (grad_scaled * head_gains[None, :, None]).astype(jnp.bfloat16)
        grad_qkv = attend_back(
            backward_heads_in, backward_lengths, backward_log_total, backward_grad_mixed
        )
        returned = lax.all_to_all(grad_qkv, "sp", split_axis=0, concat_axis=2, tiled=True).reshape(
            tok_count, 3 * model_width
        )
        column_sums = jnp.sum(returned.astype(jnp.float32), axis=0)
        q_bias_grad = column_sums[:model_width]
        v_bias_grad = column_sums[2 * model_width :]
        qkv_grad = jnp.einsum("ti,tj->ij", normed, returned, preferred_element_type=jnp.float32)
        grad_normed = jnp.einsum(
            "tj,ij->ti", returned, wide_qkv, preferred_element_type=jnp.float32
        )
        _, in_back = jax.vjp(
            layer_norm, tok_rows, wide_in_gain.astype(jnp.float32), wide_in_bias.astype(jnp.float32)
        )
        grad_rows, in_gain_grad, in_bias_grad = in_back(grad_normed)
        input_grad = grad_hidden + grad_rows
        grad_set = (
            in_gain_grad,
            in_bias_grad,
            qkv_grad,
            q_bias_grad,
            v_bias_grad,
            attn_gain_grad,
            attn_bias_grad,
            out_grad,
            out_bias_grad,
            ffn_gain_grad,
            ffn_bias_grad,
            fc1_grad,
            fc1_bias_grad,
            mid_gain_grad,
            mid_bias_grad,
            fc2_grad,
            fc2_bias_grad,
        )
        input_grad, grad_set, scale_grad = (input_grad, grad_set, scale_grad)
        grad_set = reduce_grads(grad_set)
        total_grads = (
            grad_set if total_grads is None else jax.tree.map(jnp.add, total_grads, grad_set)
        )
        scale_total = scale_total + scale_grad
        outputs.append(output)
        input_grads.append(input_grad)
    scale_sum = lax.psum(scale_total, "dp")
    layer_out = jnp.stack(outputs).astype(jnp.bfloat16)
    input_grad = jnp.stack(input_grads)
    return (
        layer_out,
        input_grad,
        total_grads[0],
        total_grads[1],
        total_grads[2],
        total_grads[3],
        total_grads[4],
        scale_sum,
        total_grads[5],
        total_grads[6],
        total_grads[7],
        total_grads[8],
        total_grads[9],
        total_grads[10],
        total_grads[11],
        total_grads[12],
        total_grads[13],
        total_grads[14],
        total_grads[15],
        total_grads[16],
    )


def solution(mesh):
    return jax.shard_map(
        shards,
        mesh=mesh,
        in_specs=(
            P(None, ("dp", "sp"), None),
            P("dp", None, None),
            P(None, ("dp", "sp"), None),
            P(("dp", "sp")),
            P(("dp", "sp")),
            P(("dp", "sp"), None),
            P(("dp", "sp")),
            P(("dp", "sp")),
            P("sp"),
            P(("dp", "sp")),
            P(("dp", "sp")),
            P(("dp", "sp"), None),
            P(("dp", "sp")),
            P(("dp", "sp")),
            P(("dp", "sp")),
            P(("dp", "sp"), None),
            P(("dp", "sp")),
            P(("dp", "sp")),
            P(("dp", "sp")),
            P(("dp", "sp"), None),
            P(("dp", "sp")),
        ),
        out_specs=(
            P(None, ("dp", "sp"), None),
            P(None, ("dp", "sp"), None),
            P(("dp", "sp")),
            P(("dp", "sp")),
            P(("dp", "sp"), None),
            P(("dp", "sp")),
            P(("dp", "sp")),
            P("sp"),
            P(("dp", "sp")),
            P(("dp", "sp")),
            P(("dp", "sp"), None),
            P(("dp", "sp")),
            P(("dp", "sp")),
            P(("dp", "sp")),
            P(("dp", "sp"), None),
            P(("dp", "sp")),
            P(("dp", "sp")),
            P(("dp", "sp")),
            P(("dp", "sp"), None),
            P(("dp", "sp")),
        ),
        check_vma=False,
    )
```

profile of v0, /device:TPU:0, one launch (start us, length us, event | category | flops | bytes accessed | tf_op | source)
XLA Modules:
  0.0 3681.8 jit_solution(6624119180193224921)
XLA Ops:
  18.4 43.0 %all-reduce.24 = (bf16[1024]{0:T(1024)(128)(2,1)}, bf16[1024]{0:T(1024)(128)(2,1)S(1)}, bf16[1024]{0:T(1024)(128)(2,1)S(1)}, bf16[1024]{0:T(1024)(128)(2,1)S(1)}...) all-reduce(bf16[1024]{0:T(1024)(128)(2,1)S(1)} %dynamic-update-slic, ...), channel_id=1, replica_groups=mesh['dp'=16,'sp'=2] {'dp','sp'}, use_global_device_ids=true, to_apply=%add.6 | all-reduce | flops 10240 | bytes 40960
  161.5 74.2 %all-to-all-done.2 = bf16[1024,3,1024]{0,1,2:T(4,128)(2,1)} async-done(((bf16[1024,3,1024]{0,1,2:T(4,128)(2,1)}), bf16[1024,3,1024]{0,1,2:T(4,128)(2,1)}, u32[]{:S(2)}, u32[]{:S(2)}) %all-to-all-start.2) | async-done | bytes 6291488 | tf_op jit(solution)/shard_map/all_to_all | solution.py:219
  277.6 200.6 %while.59 = (s32[]{:T(128)}, f32[4,512,8,64]{1,3,2,0:T(8,128)}, f32[4,8,512]{2,1,0:T(8,128)S(1)}, s32[4]{0:T(128)S(1)}, s32[2048]{0:T(1024)S(1)}, /*index=5*/s32...) while((s32[]{:T(128)}, f32[4,512,8,64]{1,3,2,0:T(8,128)}, ...), condition=%wide.region_21.22_spmd.clone, body=%wide.region_18.21_spmd.clone.sunk | while | flops 2251288576 | bytes 110785208 | solution.py:243
  513.6 199.2 %while.58 = (s32[]{:T(128)}, f32[4,512,8,64]{1,3,2,0:T(8,128)}, f32[4,8,512]{2,1,0:T(8,128)S(1)}, s32[4]{0:T(128)S(1)}, s32[2048]{0:T(1024)S(1)}, /*index=5*/s32...) while((s32[]{:T(128)}, f32[4,512,8,64]{1,3,2,0:T(8,128)}, ...), condition=%wide.region_7.8_spmd.clone, body=%wide.region_4.7_spmd.clone.sunk | while | flops 2251288576 | bytes 110785208 | solution.py:243
  755.1 81.3 %all-gather = bf16[32,1,128]{2,1,0:T(2,128)(2,1)S(1)} all-gather(bf16[1,1,128]{2,1,0:T(2,128)(2,1)S(1)} %bitcast.413), channel_id=1, replica_groups=mesh['dp'=16,'sp'=2] {'dp','sp'}, dimensions={0}, use_global_device_ids=true | all-gather | bytes 8448 | tf_op jit(solution)/shard_map/all_gather | solution.py:110
  836.4 64.1 %all-gather.1 = bf16[32,1,128]{2,1,0:T(2,128)(2,1)S(1)} all-gather(bf16[1,1,128]{2,1,0:T(2,128)(2,1)S(1)} %bitcast.414), channel_id=1, replica_groups=mesh['dp'=16,'sp'=2] {'dp','sp'}, dimensions={0}, use_global_device_ids=true | all-gather | bytes 8448 | tf_op jit(solution)/shard_map/all_gather | solution.py:111
  900.6 64.0 %all-gather.2 = bf16[32,1,128]{2,1,0:T(2,128)(2,1)S(1)} all-gather(bf16[1,1,128]{2,1,0:T(2,128)(2,1)S(1)} %bitcast.415), channel_id=1, replica_groups=mesh['dp'=16,'sp'=2] {'dp','sp'}, dimensions={0}, use_global_device_ids=true | all-gather | bytes 8448 | tf_op jit(solution)/shard_map/all_gather | solution.py:112
  1051.7 28.4 fusion.159
  1098.5 38.9 %multiply_reduce_fusion.3 = (f32[4096]{0:T(1024)}, f32[1024]{0:T(1024)S(1)}, f32[4096]{0:T(1024)}, f32[4096]{0:T(1024)}, f32[1024]{0:T(1024)S(1)}, /*index=5*/f32[4096]{0:T(1024)}, f32[1024,4096]{1,0:T(8,128)}) fusion(f32[1024]{0:T(1024)S(1)} %fusion.147, f32[1024]{0:T(1024)S(1)} %get-tuple-element.868, f32[1024,4096]{1,0:T(8,128)} %get-tuple-element.856, ...), kind=kOutput, calls=%fused_computation.93 | convolution fusion | flops 8732522496 | bytes 77717504 | tf_op jit(solution)/shard_map/tj,ij->ti/dot_general | solution.py:332
  1137.5 37.8 %fusion.166 = (f32[1024]{0:T(1024)S(1)}, f32[1024,4096]{1,0:T(8,128)}, bf16[1024,4096]{1,0:T(8,128)(2,1)}, f32[1024]{0:T(1024)S(1)}, f32[1024,4096]{1,0:T(8,128)}) fusion(f32[1024]{0:T(1024)S(1)} %multiply_multiply_fusion.13, f32[1024]{0:T(1024)S(1)} %get-tuple-element.868, f32[1024,4096]{1,0:T(8,128)} %get-tuple-element.856, f32[4096]{0:T(1024)S(1)} %bitcast.400, ...), kind=kLoop, calls=%fused_computation.306 | loop fusion | flops 150992896 | bytes 109133824 | tf_op jit(solution)/shard_map/transpose(jvp())/reduce_sum | solution.py:15
  1175.4 31.9 convert_reduce_fusion.1
  1365.4 445.3 %while.61 = (s32[]{:T(128)}, f32[2048,8,64]{0,2,1:T(8,128)}, f32[2048,8,64]{0,2,1:T(8,128)}, bf16[4,512,8,64]{1,3,2,0:T(8,128)(2,1)}, s32[4]{0:T(128)S(1)}, /*in...) while((s32[]{:T(128)}, f32[2048,8,64]{0,2,1:T(8,128)}, ...), condition=%wide.region_47.48_spmd.clone.clone, body=%wide.region_45.47_spmd.clone.clone.sunk | while | flops 5451804672 | bytes 347190016 | solution.py:167
  1413.7 27.4 multiply_convert_fusion.11
  1845.8 446.2 %while.60 = (s32[]{:T(128)}, f32[2048,8,64]{0,2,1:T(8,128)}, f32[2048,8,64]{0,2,1:T(8,128)}, bf16[4,512,8,64]{1,3,2,0:T(8,128)(2,1)}, s32[4]{0:T(128)S(1)}, /*in...) while((s32[]{:T(128)}, f32[2048,8,64]{0,2,1:T(8,128)}, ...), condition=%wide.region_36.37_spmd.clone.clone, body=%wide.region_34.36_spmd.clone.clone.sunk | while | flops 5451804672 | bytes 347190016 | solution.py:167
  1894.3 27.5 multiply_convert_fusion.10
  2003.9 27.5 multiply_convert_fusion.10
  2116.0 27.5 multiply_convert_fusion.10
  2228.0 27.5 multiply_convert_fusion.10
  2354.2 60.2 %all-to-all-done.5 = bf16[2048,3,512]{2,1,0:T(4,128)(2,1)} async-done(((bf16[2048,3,512]{2,1,0:T(4,128)(2,1)}), bf16[2048,3,512]{2,1,0:T(4,128)(2,1)}, u32[]{:S(2)}, u32[]{:S(2)}) %all-to-all-start.5) | async-done | bytes 6291488 | tf_op jit(solution)/shard_map/all_to_all | solution.py:377
  2672.9 41.3 %psum.7 = f32[8]{0:T(128)} all-reduce(f32[8]{0:T(128)S(1)} %add.502), channel_id=1, replica_groups=mesh['dp'=16,'sp'=2] {'dp'}, use_global_device_ids=true, to_apply=%region_68.69 | all-reduce | flops 8 | bytes 64 | tf_op jit(solution)/shard_map/psum | solution.py:419
  2747.7 47.6 %reduce-scatter.7.cloned.1.call-done = f32[32,1024]{1,0:T(8,128)} async-done(((f32[1024,1024]{1,0:T(8,128)}), f32[32,1024]{1,0:T(8,128)}) %reduce-scatter.7.cloned.1.call-update) | async-done | bytes 131088 | tf_op jit(solution)/shard_map/reduce_scatter | solution.py:44
  2795.3 158.9 %reduce-scatter.5.cloned.1.call-done = f32[32,3072]{1,0:T(8,128)} async-done(((f32[1024,3072]{1,0:T(8,128)}), f32[32,3072]{1,0:T(8,128)}) %reduce-scatter.5.cloned.1.call-update) | async-done | bytes 393232 | tf_op jit(solution)/shard_map/reduce_scatter | solution.py:39
  2954.2 359.5 %reduce-scatter.11.cloned.1.call-done = f32[128,1024]{1,0:T(8,128)} async-done(((f32[4096,1024]{1,0:T(8,128)}), f32[128,1024]{1,0:T(8,128)}) %reduce-scatter.11.cloned.1.call-update) | async-done | bytes 524304 | tf_op jit(solution)/shard_map/reduce_scatter | solution.py:52
  3313.6 361.5 %reduce-scatter.9.cloned.1.call-done = f32[32,4096]{1,0:T(8,128)} async-done(((f32[1024,4096]{1,0:T(8,128)}), f32[32,4096]{1,0:T(8,128)}) %reduce-scatter.9.cloned.1.call-update) | async-done | bytes 524304 | tf_op jit(solution)/shard_map/reduce_scatter | solution.py:48
  (710 shorter events, 2003.0 us)
Async XLA Ops:
  7.2 76.1 %all-gather.8.cloned.1.call-start = ((), (), s32[]{:S(2)}) async-start(), calls=%async_computation.12 | async-start | bytes 6488064 | tf_op jit(solution)/shard_map/all_gather | solution.py:100
  7.9 978.7 %all-gather.14.cloned.1.call-start = ((), (), s32[]{:S(2)}) async-start(), calls=%async_computation.15 | async-start | bytes 8650752 | tf_op jit(solution)/shard_map/all_gather | solution.py:113
  8.7 1010.4 %all-gather.10.cloned.1.call-start = ((), (), s32[]{:S(2)}) async-start(), calls=%async_computation.13 | async-start | bytes 2162688 | tf_op jit(solution)/shard_map/all_gather | solution.py:105
  9.4 1025.2 %all-gather.12.cloned.1.call-start = ((), (), s32[]{:S(2)}) async-start(), calls=%async_computation.14 | async-start | bytes 8650752 | tf_op jit(solution)/shard_map/all_gather | solution.py:109
  61.4 68.0 %copy-start.126 = (f32[1024]{0:T(1024)}, f32[1024]{0:T(1024)S(1)}, u32[]{:S(2)}) copy-start(f32[1024]{0:T(1024)S(1)} %convert_element_type.268) | copy-start | bytes 12292
  115.7 120.0 %all-to-all-start.2 = ((bf16[1024,3,1024]{0,1,2:T(4,128)(2,1)}), bf16[1024,3,1024]{0,1,2:T(4,128)(2,1)}, u32[]{:S(2)}, u32[]{:S(2)}) async-start(bf16[1024,3,1024]{0,1,2:T(4,128)(2,1)} %copy.325), calls=%async_computation.2 | async-start | bytes 16777216 | tf_op jit(solution)/shard_map/all_to_all | solution.py:219
  235.8 242.5 %all-to-all-start = ((bf16[1024,3,1024]{0,1,2:T(4,128)(2,1)}), bf16[1024,3,1024]{0,1,2:T(4,128)(2,1)}, u32[]{:S(2)}, u32[]{:S(2)}) async-start(bf16[1024,3,1024]{0,1,2:T(4,128)(2,1)} %copy.313), calls=%async_computation | async-start | bytes 16777216 | tf_op jit(solution)/shard_map/all_to_all | solution.py:219
  748.5 87.9 %copy-start.138 = (bf16[128]{0:T(256)(128)(2,1)S(1)}, bf16[128]{0:T(256)(128)(2,1)}, u32[]{:S(2)}) copy-start(bf16[128]{0:T(256)(128)(2,1)} %param.46) | copy-start | bytes 772
  748.5 152.1 %copy-start.139 = (bf16[128]{0:T(256)(128)(2,1)S(1)}, bf16[128]{0:T(256)(128)(2,1)}, u32[]{:S(2)}) copy-start(bf16[128]{0:T(256)(128)(2,1)} %param.47) | copy-start | bytes 772
  751.2 230.7 %all-to-all-start.3 = ((bf16[2,1024,512]{1,2,0:T(8,128)(2,1)}), bf16[2,1024,512]{1,2,0:T(8,128)(2,1)S(1)}, u32[]{:S(2)}, u32[]{:S(2)}) async-start(bf16[2,1024,512]{1,2,0:T(8,128)(2,1)} %copy.333), calls=%async_computation.3 | async-start | bytes 4194304 | tf_op jit(solution)/shard_map/all_to_all | solution.py:250
  754.9 259.5 %copy-start.62 = (f32[1024]{0:T(1024)}, f32[1024]{0:T(1024)S(1)}, u32[]{:S(2)}) copy-start(f32[1024]{0:T(1024)S(1)} %convert_element_type.278) | copy-start | bytes 12292
  755.0 296.7 %copy-start.96 = (f32[1024]{0:T(1024)}, f32[1024]{0:T(1024)S(1)}, u32[]{:S(2)}) copy-start(f32[1024]{0:T(1024)S(1)} %convert_element_type.282) | copy-start | bytes 12292
  755.0 296.7 %copy-start.128 = (f32[1024]{0:T(1024)}, f32[1024]{0:T(1024)S(1)}, u32[]{:S(2)}) copy-start(f32[1024]{0:T(1024)S(1)} %convert_element_type.283) | copy-start | bytes 12292
  836.4 339.0 %copy-start.50 = (f32[32,1,128]{2,1,0:T(1,128)}, f32[32,1,128]{2,1,0:T(1,128)S(1)}, u32[]{:S(2)}) copy-start(f32[32,1,128]{2,1,0:T(1,128)S(1)} %convert_element_type.349) | copy-start | bytes 49156
  900.6 236.9 %copy-start.68 = (f32[32,1,128]{2,1,0:T(1,128)}, f32[32,1,128]{2,1,0:T(1,128)S(1)}, u32[]{:S(2)}) copy-start(f32[32,1,128]{2,1,0:T(1,128)S(1)} %convert_element_type.350) | copy-start | bytes 49156
  981.8 27.2 all-to-all-start.1
  1314.9 24.7 all-to-all-start.4
  1838.6 481.4 %all-to-all-start.7 = ((bf16[2048,3,512]{2,1,0:T(4,128)(2,1)}), bf16[2048,3,512]{2,1,0:T(4,128)(2,1)}, u32[]{:S(2)}, u32[]{:S(2)}) async-start(bf16[2048,3,512]{2,1,0:T(4,128)(2,1)} %copy.347), calls=%async_computation.7 | async-start | bytes 16777216 | tf_op jit(solution)/shard_map/all_to_all | solution.py:377
  2320.1 94.3 %all-to-all-start.5 = ((bf16[2048,3,512]{2,1,0:T(4,128)(2,1)}), bf16[2048,3,512]{2,1,0:T(4,128)(2,1)}, u32[]{:S(2)}, u32[]{:S(2)}) async-start(bf16[2048,3,512]{2,1,0:T(4,128)(2,1)} %copy.339), calls=%async_computation.5 | async-start | bytes 16777216 | tf_op jit(solution)/shard_map/all_to_all | solution.py:377
  2327.3 404.1 %all-reduce.27.cloned.1.call-start = ((), (), s32[]{:S(2)}) async-start(), calls=%async_computation.20 | async-start | bytes 180224
  2488.4 306.8 %reduce-scatter.7.cloned.1.call-start = ((), (), s32[]{:S(2)}) async-start(), calls=%async_computation.17 | async-start | bytes 4325376 | tf_op jit(solution)/shard_map/reduce_scatter | solution.py:44
  2496.3 457.9 %reduce-scatter.5.cloned.1.call-start = ((), (), s32[]{:S(2)}) async-start(), calls=%async_computation.16 | async-start | bytes 12976128 | tf_op jit(solution)/shard_map/reduce_scatter | solution.py:39
  2524.6 789.0 %reduce-scatter.11.cloned.1.call-start = ((), (), s32[]{:S(2)}) async-start(), calls=%async_computation.19 | async-start | bytes 17301504 | tf_op jit(solution)/shard_map/reduce_scatter | solution.py:52
  2565.4 1109.7 %reduce-scatter.9.cloned.1.call-start = ((), (), s32[]{:S(2)}) async-start(), calls=%async_computation.18 | async-start | bytes 17301504 | tf_op jit(solution)/shard_map/reduce_scatter | solution.py:48
  (144 other events, 1362.6 us)
Sparse Core Ops, SparseCore 0:
  10.9 72.2 all-gather.7
  86.4 91.5 all-gather.13
  181.1 58.0 all-gather.9
  242.2 94.8 all-gather.11
  2488.6 158.9 all-reduce.26
  2652.6 142.6 reduce-scatter.6
  2801.9 152.2 reduce-scatter.4
  2957.1 356.4 reduce-scatter.10
  3316.6 358.4 reduce-scatter.8
where the time goes:
time: 3700 us; the launch traced here: 3680 us
  matrix products  1230 us (33%)
  waiting for transfers between devices  1090 us (29%)
  other arithmetic  571 us (15%)
  local copies, waits for them, and re-layouts  377 us (10%)
  blocking collectives  319 us (9%)
  starting transfers between devices  41.5 us (1%)
    reduce_scatter x1, waiting for transfers between devices, reduce_grads(): lax.psum_scatter(grad_set[11], ('dp', 'sp'), scatter_dimension=0, tiled=T...  361 us
    reduce_scatter x1, waiting for transfers between devices, reduce_grads(): lax.psum_scatter(grad_set[15], ('dp', 'sp'), scatter_dimension=0, tiled=T...  359 us
    dot_general x16, matrix products, block_scores(): jnp.einsum('qhd,khd->hqk', query_block, key_heads, preferred_element_type...  336 us
    convert_element_type x8, other arithmetic, one_block(): grad_scores = (prob_rows * (grad_probs - row_inner)).astype(jnp.bfloat16)  219 us
    reduce_scatter x1, waiting for transfers between devices, reduce_grads(): lax.psum_scatter(grad_set[2], ('dp', 'sp'), scatter_dimension=0, tiled=True)  159 us
    dot_general x8, matrix products, one_block(): jnp.einsum('qhd,khd->hqk', grad_block, value_heads, preferred_element_typ...  140 us
    dot_general x8, matrix products, one_block(): jnp.einsum('hqk,qhd->khd', prob_rows.astype(jnp.bfloat16), grad_block, pr...  134 us
    dot_general x8, matrix products, attend_one_block(): jnp.einsum('hqk,khd->qhd', prob_rows, attend_value_heads, preferred_eleme...  125 us
  transfers between devices with their start and end apart: 16, of which 9 were waited for; matrix products, arithmetic and copies ran while one was open for 37% of the time, Pallas kernels for 0%

commit v1 on v0

--- a/solution.py
+++ b/solution.py
@@ -1,14 +1,964 @@
+import functools
 import math
 
 import jax
 import jax.numpy as jnp
 from jax import lax
+from jax.experimental import pallas as pl
+from jax.experimental.pallas import tpu as pltpu
 from jax.sharding import PartitionSpec as P
 
+EPS = 1e-05
+BLOCK = 512
+LOG2E = math.log2(math.e)
+NEG = -1e30
+F32 = jnp.float32
+BF16 = jnp.bfloat16
+VMEM_CAP = 60 * 1024 * 1024
+NT = (((1,), (1,)), ((), ()))
+NN = (((1,), (0,)), ((), ()))
+FWD_STEPS = ((4, 8, 12, 16, 20), (8, 12, 16, 20, 24), (12, 17, 22, 27, 31), (16, 21, 26, 31, 31))
+BWD_STEPS = ((1, 2, 3, 4, 5), (7, 13, 18, 23, 26), (10, 16, 21, 26, 29), (14, 20, 25, 30, 32))
+
+
+def mm(a, b, dims=NN):
+    return lax.dot_general(a, b, dims, preferred_element_type=F32)
+
+
+class Place:
+    def __init__(self, depth):
+        d = lax.axis_index("dp")
+        self.depth = depth
+        self.y = lax.axis_index("sp")
+        self.c = d % 2
+        self.x = (d // 2) % 2
+        self.z = d // 4
+        self.next_y = self.device(self.z, self.x, self.c, 1 - self.y)
+        self.next_x = self.device(self.z, 1 - self.x, self.c, self.y)
+        self.twin = self.device(self.z, self.x, 1 - self.c, self.y)
+
+    def device(self, z, x, c, y):
+        return ((z * 2 + x) * 2 + c, y)
+
+    def along(self, step):
+        return (self.z + step) % self.depth
+
+    def column(self, step):
+        return self.device(self.along(step), self.x, self.c, self.y)
+
+    def greet(self):
+        barrier = pltpu.get_barrier_semaphore()
+        peers = [self.column(s) for s in range(1, self.depth)] + [self.next_x, self.next_y, self.twin]
+        for peer in peers:
+            pl.semaphore_signal(barrier, inc=1, device_id=peer, device_id_type=pl.DeviceIdType.MESH)
+        pl.semaphore_wait(barrier, len(peers))
+
+
+def remote(src, dst, send, recv, peer):
+    return pltpu.make_async_remote_copy(
+        src_ref=src, dst_ref=dst, send_sem=send, recv_sem=recv, device_id=peer, device_id_type=pl.DeviceIdType.MESH
+    )
+
+
+class Gather:
+    def __init__(self, me, shard, whole, at, count, local, send, recv):
+        self.me, self.shard, self.whole = me, shard.at[pl.ds(at, count)], whole
+        self.rows = pl.ds(at, count)
+        self.local, self.send, self.recv = local, send, recv
+
+    def own(self, z):
+        me = self.me
+        return self.whole.at[z, me.x, me.c, me.y, self.rows]
+
+    def keep(self):
+        return pltpu.make_async_copy(self.shard, self.own(self.me.z), self.local)
+
+    def depth_hop(self, s, landed):
+        me = self.me
+        z = me.along(me.depth - s) if landed else me.z
+        return remote(self.shard, self.own(z), self.send.at[6 + s], self.recv.at[6 + s], me.column(s))
+
+    def hop(self, x, y, n, peer, c=None):
+        group = self.whole.at[:, x, self.me.c if c is None else c, y, self.rows]
+        return remote(group, group, self.send.at[n], self.recv.at[n], peer)
+
+    def path(self, n, c=None):
+        me = self.me
+        x, y = me.x, me.y
+        gx = 1 - x if n in (5, 6) else x
+        gy = 1 - y if n in (2, 4, 6) else y
+        peer = me.next_y if n == 0 else me.next_x if n < 3 else me.twin
+        return self.hop(gx, gy, n, peer, c)
+
+    def begin(self):
+        self.keep().start()
+        for s in range(1, self.me.depth):
+            self.depth_hop(s, False).start()
+
+    def spread(self):
+        self.keep().wait()
+        for s in range(1, self.me.depth):
+            self.depth_hop(s, True).wait()
+        for n in (0, 1, 3):
+            self.path(n).start()
+
+    def from_y(self):
+        me = self.me
+        self.hop(me.x, 1 - me.y, 0, me.next_y).wait_recv()
+        self.path(2).start()
+        self.path(4).start()
+
+    def from_x(self):
+        me = self.me
+        self.hop(1 - me.x, me.y, 1, me.next_x).wait_recv()
+        self.path(5).start()
+
+    def from_corner(self):
+        me = self.me
+        self.hop(1 - me.x, 1 - me.y, 2, me.next_x).wait_recv()
+        self.path(6).start()
+
+    def end(self):
+        for n in range(7):
+            self.path(n).wait_send()
+        for n in range(3, 7):
+            self.path(n, 1 - self.me.c).wait_recv()
+
+
+class Swap:
+    def __init__(self, me, sent, landing, kept, place, local, send, recv):
+        self.out = remote(sent, landing(me.y), send, recv, me.next_y)
+        self.into = remote(sent, landing(1 - me.y), send, recv, me.next_y)
+        self.keep = pltpu.make_async_copy(kept, place, local)
+
+    def begin(self):
+        self.out.start()
+        self.keep.start()
+
+    def end(self):
+        self.out.wait_send()
+        self.into.wait_recv()
+        self.keep.wait()
+
+
+def add_group(own, x, y, taken):
+    def body(s, _):
+        own[s, x, y] = (own[s, x, y].astype(F32) + taken(s).astype(F32)).astype(own.dtype)
+        return 0
+
+    lax.fori_loop(0, own.shape[0], body, 0)
+
+
+class Scatter:
+    def __init__(self, me, part, at, count, own, got0, got1, got3, local, send, recv, total):
+        self.me, self.part, self.rows = me, part, pl.ds(at, count)
+        self.own, self.got0, self.got1, self.got3 = own, got0, got1, got3
+        self.local, self.send, self.recv, self.total = local, send, recv, total
+
+    def mine(self):
+        return pltpu.make_async_copy(self.part.at[:, :, self.me.c, :, self.rows], self.own, self.local)
+
+    def halves(self):
+        return remote(
+            self.part.at[:, :, 1 - self.me.c, :, self.rows], self.got0, self.send.at[0], self.recv.at[0], self.me.twin
+        )
+
+    def to_x(self, n):
+        me = self.me
+        y = me.y if n == 0 else 1 - me.y
+        return remote(self.own.at[:, 1 - me.x, y], self.got1.at[n], self.send.at[1 + n], self.recv.at[1 + n], me.next_x)
+
+    def to_y(self):
+        me = self.me
+        return remote(self.own.at[:, me.x, 1 - me.y], self.got1.at[2], self.send.at[3], self.recv.at[3], me.next_y)
+
+    def to_z(self, s):
+        me = self.me
+        return remote(
+            self.own.at[me.along(s), me.x, me.y], self.got3.at[s - 1], self.send.at[3 + s], self.recv.at[3 + s],
+            me.column(s),
+        )
+
+    def begin(self):
+        self.mine().start()
+        self.halves().start()
+
+    def across(self):
+        me, own, got = self.me, self.own, self.got0
+        self.mine().wait()
+        self.halves().wait()
+        for n, x, y in ((1, 1 - me.x, 1 - me.y), (0, 1 - me.x, me.y)):
+            add_group(own, x, y, lambda s: got[s, x, y])
+            self.to_x(n).start()
+        for x, y in ((me.x, 1 - me.y), (me.x, me.y)):
+            add_group(own, x, y, lambda s: got[s, x, y])
+
+    def along_x(self):
+        me, own, got = self.me, self.own, self.got1
+        self.to_x(1).wait_recv()
+        add_group(own, me.x, 1 - me.y, lambda s: got[1, s])
+        self.to_y().start()
+        self.to_x(0).wait_recv()
+        add_group(own, me.x, me.y, lambda s: got[0, s])
+
+    def along_y(self):
+        me, own, got = self.me, self.own, self.got1
+        self.to_y().wait_recv()
+        add_group(own, me.x, me.y, lambda s: got[2, s])
+        for s in range(1, me.depth):
+            self.to_z(s).start()
+
+    def end(self):
+        me = self.me
+        total = self.own[me.z, me.x, me.y].astype(F32)
+        for s in range(1, me.depth):
+            self.to_z(s).wait_recv()
+            total = total + self.got3[s - 1].astype(F32)
+        self.total[self.rows] = total
+        self.to_x(0).wait_send()
+        self.to_x(1).wait_send()
+        self.to_y().wait_send()
+        for s in range(1, me.depth):
+            self.to_z(s).wait_send()
+
+
+def scatter_scratch(pieces, depth):
+    out = []
+    for rows, cols, dtype in pieces:
+        for lead in ((depth, 2, 2), (depth, 2, 2), (3, depth), (depth - 1,)):
+            out.append(pltpu.VMEM(lead + (rows, cols), dtype))
+    return out
+
+
+def perform(step, plan):
+    for due in sorted(plan):
+
+        @pl.when(step == due)
+        def _(actions=plan[due]):
+            for action in actions:
+                action()
+
+
+def due(plan, step, action):
+    plan.setdefault(step, []).append(action)
+
+
+def head_pair_masks():
+    lanes = lax.broadcasted_iota(jnp.int32, (1, 128), 1)
+    return (lanes < 64, lanes >= 64)
+
+
+def attend_fwd_kernel(depth, pieces, *refs):
+    ids, hs, q_ref, k_ref, v_ref = refs[:5]
+    shards = refs[5:8]
+    cot = refs[8]
+    o_ref, mixed_ref, lse_ref = refs[9:12]
+    wholes = refs[12:15]
+    cot_whole = refs[15]
+    vt, local, send, recv = refs[16:]
+    pair = pl.program_id(0)
+    me = Place(depth)
+    half = cot.shape[1]
+    gathers = [
+        Gather(me, shards[a], wholes[a], at, count, local.at[n], send.at[n], recv.at[n])
+        for n, (a, at, count) in enumerate(pieces)
+    ]
+    n = len(pieces)
+    swap = Swap(
+        me, cot.at[1 - me.y], lambda y: cot_whole.at[y], cot.at[me.y], cot_whole.at[me.y],
+        local.at[n], send.at[n, 0], recv.at[n, 0],
+    )
+    plan = {}
+    due(plan, 0, me.greet)
+    for g in gathers:
+        due(plan, 0, g.begin)
+    due(plan, 10, swap.begin)
+    for n, g in enumerate(gathers):
+        due(plan, FWD_STEPS[0][n], g.spread)
+        due(plan, FWD_STEPS[1][n], g.from_y)
+        due(plan, FWD_STEPS[2][n], g.from_x)
+        due(plan, FWD_STEPS[3][n], g.from_corner)
+        due(plan, 31, g.end)
+    due(plan, 31, swap.end)
+    last = plan.pop(31)
+    rows = q_ref.shape[0]
+    blocks = rows // BLOCK
+    factor = LOG2E / 8.0
+    masks = head_pair_masks()
+    gains = jnp.where(masks[0], hs[2 * pair], hs[2 * pair + 1])
+    for j in range(blocks):
+        vtr = v_ref[j * BLOCK : (j + 1) * BLOCK, :].astype(F32).T.astype(BF16)
+        for h in range(2):
+            vt[j, h, 0:64, :] = vtr[h * 64 : (h + 1) * 64]
+            vt[j, h, 64:80, :] = jnp.ones((16, BLOCK), BF16)
+    key_at = lax.broadcasted_iota(jnp.int32, (BLOCK, BLOCK), 0)
+    query_at = lax.broadcasted_iota(jnp.int32, (BLOCK, BLOCK), 1)
+
+    def one_query(i, _):
+        perform(pair * blocks + i, plan)
+        q = q_ref[pl.ds(i * BLOCK, BLOCK), :]
+        qh = [jnp.where(m, q, jnp.zeros_like(q)) for m in masks]
+
+        def step(kb, carry, diag):
+            k = k_ref[pl.ds(kb * BLOCK, BLOCK), :]
+            out = []
+            for h in range(2):
+                s = mm(k, qh[h], NT)
+                if diag:
+                    s = jnp.where(key_at <= query_at, s, NEG)
+                    m = jnp.max(s, axis=0, keepdims=True)
+                    p = jnp.exp2(s * factor - m * factor).astype(BF16)
+                    out.append((m, mm(vt[kb, h], p)))
+                else:
+                    bias = jnp.where(ids[i] == ids[kb], 0.0, NEG)
+                    m_old, acc = carry[h]
+                    m = jnp.maximum(m_old, jnp.max(s, axis=0, keepdims=True) + bias)
+                    p = jnp.exp2(s * factor - (m - bias) * factor).astype(BF16)
+                    alpha = jnp.exp2((m_old - m) * factor)
+                    out.append((m, acc * alpha + mm(vt[kb, h], p)))
+            return tuple(out)
+
+        carry = step(i, None, True)
+        carry = lax.fori_loop(0, i, lambda kb, c: step(kb, c, False), carry)
+        outs = []
+        for h in range(2):
+            m, acc = carry[h]
+            total = acc[64:65]
+            outs.append(acc[:64] / total)
+            lse_ref[0, h, pl.ds(i, 1), :] = m * factor + jnp.log2(total)
+        both = jnp.concatenate(outs, axis=0).T
+        mixed_ref[pl.ds(i * BLOCK, BLOCK), :] = both
+        o_ref[pl.ds(i * BLOCK, BLOCK), :] = (both * gains).astype(BF16)
+        return 0
+
+    lax.fori_loop(0, blocks, one_query, 0)
+    perform(pair, {pl.num_programs(0) - 1: last})
+
+
+def attend_fwd(qkv, ids, hs, shards, cot, depth, collective_id):
+    rows, width3 = qkv.shape
+    width = width3 // 3
+    pairs = width // 128
+    blocks = rows // BLOCK
+    spec = lambda part: pl.BlockSpec((rows, 128), lambda p, part=part: (0, part * pairs + p))
+    smem = pl.BlockSpec(memory_space=pltpu.SMEM)
+    anywhere = pl.BlockSpec(memory_space=pl.ANY)
+    pieces = [(0, 0, shards[0].shape[0])]
+    for a in (1, 2):
+        part = shards[a].shape[0] // 2
+        pieces += [(a, 0, part), (a, part, part)]
+    count = len(pieces) + 1
+    out = pl.pallas_call(
+        functools.partial(attend_fwd_kernel, depth, pieces),
+        grid=(pairs,),
+        in_specs=[smem, smem, spec(0), spec(1), spec(2)] + [anywhere] * 4,
+        out_specs=[
+            pl.BlockSpec((rows, 128), lambda p: (0, p)),
+            pl.BlockSpec((rows, 128), lambda p: (0, p)),
+            pl.BlockSpec((1, 2, blocks, BLOCK), lambda p: (p, 0, 0, 0)),
+        ]
+        + [anywhere] * 4,
+        out_shape=[
+            jax.ShapeDtypeStruct((rows, width), BF16),
+            jax.ShapeDtypeStruct((rows, width), F32),
+            jax.ShapeDtypeStruct((pairs, 2, blocks, BLOCK), F32),
+        ]
+        + [jax.ShapeDtypeStruct((depth, 2, 2, 2) + s.shape, s.dtype) for s in shards]
+        + [jax.ShapeDtypeStruct(cot.shape, cot.dtype)],
+        scratch_shapes=[
+            pltpu.VMEM((blocks, 2, 80, BLOCK), BF16),
+            pltpu.SemaphoreType.DMA((count,)),
+            pltpu.SemaphoreType.DMA((count, 6 + depth)),
+            pltpu.SemaphoreType.DMA((count, 6 + depth)),
+        ],
+        compiler_params=pltpu.CompilerParams(
+            vmem_limit_bytes=VMEM_CAP, collective_id=collective_id, has_side_effects=True
+        ),
+        name="attend_fwd",
+    )(ids, hs, qkv, qkv, qkv, *shards, cot)
+    wholes = [w.reshape((depth * 8 * w.shape[4],) + w.shape[5:]) for w in out[3:6]]
+    return out[0], out[1], out[2], wholes, out[6].reshape(rows, width)
+
+
+def attend_bwd_kernel(depth, pieces, *refs):
+    ids, hs, q_ref, k_ref, v_ref, o_ref, g_ref, lse_ref = refs[:8]
+    parts = refs[8:11]
+    layer = refs[11]
+    dq_ref, dk_ref, dv_ref, delta_ref = refs[12:16]
+    sums = refs[16:19]
+    layer_out = refs[19]
+    kt, dk_acc, dv_acc, local, send, recv = refs[20:26]
+    scratch = refs[26:]
+    pair = pl.program_id(0)
+    me = Place(depth)
+    scatters = [
+        Scatter(
+            me, parts[a], at, count, *scratch[4 * n : 4 * n + 4], local.at[n], send.at[n], recv.at[n], sums[a]
+        )
+        for n, (a, at, count) in enumerate(pieces)
+    ]
+    n = len(pieces)
+    half = layer_out.shape[1]
+    swap = Swap(
+        me, layer.at[pl.ds((1 - me.y) * half, half)], lambda y: layer_out.at[y],
+        layer.at[pl.ds(me.y * half, half)], layer_out.at[me.y], local.at[n], send.at[n, 0], recv.at[n, 0],
+    )
+    plan = {}
+    due(plan, 0, me.greet)
+    for s in scatters:
+        due(plan, 0, s.begin)
+    for n, s in enumerate(scatters):
+        due(plan, BWD_STEPS[0][n], s.across)
+        due(plan, BWD_STEPS[1][n], s.along_x)
+        due(plan, BWD_STEPS[2][n], s.along_y)
+        due(plan, BWD_STEPS[3][n], s.end)
+    due(plan, 14, swap.begin)
+    due(plan, 32, swap.end)
+    last = plan.pop(32)
+    rows = q_ref.shape[0]
+    blocks = rows // BLOCK
+    factor = LOG2E / 8.0
+    masks = head_pair_masks()
+    for j in range(blocks):
+        kt[j] = k_ref[j * BLOCK : (j + 1) * BLOCK, :].astype(F32).T.astype(BF16)
+    key_at = lax.broadcasted_iota(jnp.int32, (BLOCK, BLOCK), 0)
+    query_at = lax.broadcasted_iota(jnp.int32, (BLOCK, BLOCK), 1)
+    gains = jnp.where(masks[0], hs[2 * pair], hs[2 * pair + 1])
+    picks = jnp.concatenate([m.astype(F32) for m in masks] + [jnp.zeros((6, 128), F32)], axis=0).astype(BF16)
+
+    def one_query(i, _):
+        perform(pair * blocks + i, plan)
+        at = pl.ds(i * BLOCK, BLOCK)
+        q = q_ref[at, :]
+        g = (g_ref[at, :].astype(F32) * gains).astype(BF16)
+        prod = g.astype(F32) * o_ref[at, :]
+        hi = prod.astype(BF16)
+        lo = (prod - hi.astype(F32)).astype(BF16)
+        deltas = mm(picks, hi, NT) + mm(picks, lo, NT)
+        qh = [jnp.where(m, q, jnp.zeros_like(q)) for m in masks]
+        gh = [jnp.where(m, g, jnp.zeros_like(g)) for m in masks]
+        delta = [deltas[h : h + 1] for h in range(2)]
+        lse = [lse_ref[0, h, pl.ds(i, 1), :] for h in range(2)]
+        for h in range(2):
+            delta_ref[0, h, pl.ds(i, 1), :] = delta[h]
+
+        def step(kb, carry, diag):
+            ks = pl.ds(kb * BLOCK, BLOCK)
+            k = k_ref[ks, :]
+            v = v_ref[ks, :]
+            out = []
+            dk_part = None
+            dv_part = None
+            for h in range(2):
+                s = mm(k, qh[h], NT)
+                dp = mm(v, gh[h], NT)
+                if diag:
+                    p = jnp.exp2(s * factor - lse[h])
+                    p = jnp.where(key_at <= query_at, p, 0.0)
+                else:
+                    bias = jnp.where(ids[i] == ids[kb], 0.0, -NEG)
+                    p = jnp.exp2(s * factor - (lse[h] + bias))
+                ds = (p * (dp - delta[h])).astype(BF16)
+                dvh = mm(p.astype(BF16), gh[h])
+                dkh = mm(ds, qh[h])
+                dk_part = dkh if dk_part is None else dk_part + dkh
+                dv_part = dvh if dv_part is None else dv_part + dvh
+                dqh = mm(kt[kb, h * 64 : (h + 1) * 64, :], ds)
+                out.append(dqh if diag else carry[h] + dqh)
+            if diag:
+                dk_acc[ks, :] = dk_part
+                dv_acc[ks, :] = dv_part
+            else:
+                dk_acc[ks, :] += dk_part
+                dv_acc[ks, :] += dv_part
+            return tuple(out)
+
+        carry = step(i, None, True)
+        carry = lax.fori_loop(0, i, lambda kb, c: step(kb, c, False), carry)
+        both = jnp.concatenate(carry, axis=0) * 0.125
+        dq_ref[at, :] = both.T.astype(BF16)
+        return 0
+
+    lax.fori_loop(0, blocks, one_query, 0)
+    dk_ref[...] = (dk_acc[...] * 0.125).astype(BF16)
+    dv_ref[...] = dv_acc[...].astype(BF16)
+    perform(pair, {pl.num_programs(0) - 1: last})
+
+
+def shard_view(part, depth):
+    return part.reshape((depth, 2, 2, 2, part.shape[0] // (depth * 8)) + part.shape[1:])
+
+
+def attend_bwd(qkv, mixed, d_scaled, lse, ids, hs, parts, layer, depth, collective_id):
+    rows, width3 = qkv.shape
+    width = width3 // 3
+    pairs = width // 128
+    blocks = rows // BLOCK
+    spec = lambda part: pl.BlockSpec((rows, 128), lambda p, part=part: (0, part * pairs + p))
+    col = pl.BlockSpec((rows, 128), lambda p: (0, p))
+    stat = pl.BlockSpec((1, 2, blocks, BLOCK), lambda p: (p, 0, 0, 0))
+    smem = pl.BlockSpec(memory_space=pltpu.SMEM)
+    anywhere = pl.BlockSpec(memory_space=pl.ANY)
+    parts = [shard_view(p, depth) for p in parts]
+    pieces = []
+    for a in (0, 1):
+        part = parts[a].shape[4] // 2
+        pieces += [(a, 0, part), (a, part, part)]
+    pieces.append((2, 0, parts[2].shape[4]))
+    count = len(pieces) + 1
+    out = pl.pallas_call(
+        functools.partial(attend_bwd_kernel, depth, pieces),
+        grid=(pairs,),
+        in_specs=[smem, smem, spec(0), spec(1), spec(2), col, col, stat] + [anywhere] * 4,
+        out_specs=[col, col, col, stat]
+        + [pl.BlockSpec(p.shape[4:], lambda p: (0, 0)) for p in parts]
+        + [anywhere],
+        out_shape=[jax.ShapeDtypeStruct((rows, width), BF16)] * 3
+        + [jax.ShapeDtypeStruct((pairs, 2, blocks, BLOCK), F32)]
+        + [jax.ShapeDtypeStruct(p.shape[4:], F32) for p in parts]
+        + [jax.ShapeDtypeStruct((2, rows // 2, width), BF16)],
+        scratch_shapes=[
+            pltpu.VMEM((blocks, 128, BLOCK), BF16),
+            pltpu.VMEM((rows, 128), F32),
+            pltpu.VMEM((rows, 128), F32),
+            pltpu.SemaphoreType.DMA((count,)),
+            pltpu.SemaphoreType.DMA((count, 3 + depth)),
+            pltpu.SemaphoreType.DMA((count, 3 + depth)),
+        ]
+        + scatter_scratch([(count, parts[a].shape[5], parts[a].dtype) for a, _, count in pieces], depth),
+        compiler_params=pltpu.CompilerParams(
+            vmem_limit_bytes=VMEM_CAP, collective_id=collective_id, has_side_effects=True
+        ),
+        name="attend_bwd",
+    )(ids, hs, qkv, qkv, qkv, mixed, d_scaled, lse, *parts, layer)
+    return out[:4], out[4:7], out[7]
+
+
+def row_norm(values):
+    center = values - jnp.mean(values, axis=-1, keepdims=True)
+    spread = jnp.mean(center * center, axis=-1, keepdims=True)
+    rstd = lax.rsqrt(spread + EPS)
+    return center * rstd, rstd
+
+
+def row_norm_back(grad, hat, rstd):
+    first = jnp.mean(grad, axis=-1, keepdims=True)
+    second = jnp.mean(grad * hat, axis=-1, keepdims=True)
+    return rstd * (grad - first - hat * second)
+
+
+def fold_rows(values):
+    return jnp.sum(values.reshape(values.shape[0] // 8, 8, values.shape[1]), axis=0)
+
+
+def resident(shape):
+    return pl.BlockSpec(shape, lambda i: (0,) * len(shape), pipeline_mode=pl.Buffered(1))
+
+
+def qkv_kernel(x_ref, w_ref, p_ref, bias_ref, normed_ref, out_ref):
+    hat, _ = row_norm(x_ref[...].astype(F32))
+    normed = (hat * p_ref[0:1] + p_ref[1:2]).astype(BF16)
+    normed_ref[...] = normed
+    cols = out_ref.shape[1]
+    for j in range(cols // 512):
+        at = slice(j * 512, (j + 1) * 512)
+        out_ref[:, at] = (mm(normed, w_ref[:, at]) + bias_ref[:, at]).astype(BF16)
+
+
+def qkv_project(x, weight, params, bias):
+    rows, width = x.shape
+    cols = weight.shape[1]
+    tile = 256
+    return pl.pallas_call(
+        qkv_kernel,
+        grid=(rows // tile,),
+        in_specs=[
+            pl.BlockSpec((tile, width), lambda i: (i, 0)),
+            resident(weight.shape),
+            resident(params.shape),
+            resident(bias.shape),
+        ],
+        out_specs=[
+            pl.BlockSpec((tile, width), lambda i: (i, 0)),
+            pl.BlockSpec((tile, cols), lambda i: (i, 0)),
+        ],
+        out_shape=[jax.ShapeDtypeStruct((rows, width), BF16), jax.ShapeDtypeStruct((rows, cols), BF16)],
+        compiler_params=pltpu.CompilerParams(vmem_limit_bytes=VMEM_CAP),
+        name="qkv_project",
+    )(x, weight, params, bias)
+
+
+GELU_A = math.sqrt(2.0 / math.pi)
+GELU_B = 0.044715
+CHUNK = 512
+
+
+def middle_kernel(
+    sc_ref, x_ref, dy_ref, wout, w1, w2, nar, wide,
+    lay_ref, post_ref, fin_ref, act_ref, din_ref, dhid_ref, dlow_ref, dsc_ref, gn_ref, gw_ref,
+    n_s, gp_s, dn_s,
+):
+    @pl.when(pl.program_id(0) == 0)
+    def _():
+        gn_ref[...] = jnp.zeros_like(gn_ref)
+        gw_ref[...] = jnp.zeros_like(gw_ref)
+
+    tile, width = x_ref.shape
+    ff = w1.shape[1]
+    chunks = ff // CHUNK
+    ahat, arstd = row_norm(sc_ref[...].astype(F32))
+    post = (ahat * nar[0:1] + nar[1:2]).astype(BF16)
+    post_ref[...] = post
+    hidden = x_ref[...].astype(F32) + mm(post, wout[...]) + nar[2:3]
+    hhat, hrstd = row_norm(hidden)
+    fin = (hhat * nar[3:4] + nar[4:5]).astype(BF16)
+    fin_ref[...] = fin
+
+    def lanes(values):
+        return jnp.sum(values.reshape(tile, CHUNK // 128, 128), axis=1)
+
+    def inner(j, total):
+        at = pl.ds(pl.multiple_of(j * CHUNK, CHUNK), CHUNK)
+        u = mm(fin, w1[:, at]) + wide[0:1, at]
+        u2 = u * u
+        t = jnp.tanh(u * (GELU_A + GELU_A * GELU_B * u2))
+        half = 0.5 * (1.0 + t)
+        n = u * half
+        gp_s[:, at] = (half + n * (1.0 - t) * (GELU_A + 3.0 * GELU_A * GELU_B * u2)).astype(BF16)
+        n_s[:, at] = n
+        for q in range(CHUNK // 128):
+            total = total + n[:, q * 128 : (q + 1) * 128]
+        return total
+
+    zero = jnp.zeros((tile, 128), F32)
+    total = lax.fori_loop(0, chunks, inner, zero, unroll=2)
+    nmean = jnp.sum(total, axis=-1, keepdims=True) / ff
+
+    def square(j, total):
+        at = pl.ds(pl.multiple_of(j * 128, 128), 128)
+        c = n_s[:, at] - nmean
+        return total + c * c
+
+    total = lax.fori_loop(0, ff // 128, square, zero, unroll=4)
+    nrstd = lax.rsqrt(jnp.sum(total, axis=-1, keepdims=True) / ff + EPS)
+    dyl = dy_ref[...]
+
+    def outer(j, carry):
+        acc, s1, s2 = carry
+        at = pl.ds(pl.multiple_of(j * CHUNK, CHUNK), CHUNK)
+        nh = (n_s[:, at] - nmean) * nrstd
+        n_s[:, at] = nh
+        act = (nh * wide[1:2, at] + wide[2:3, at]).astype(BF16)
+        act_ref[:, at] = act
+        acc = acc + mm(act, w2[at, :])
+        da = mm(dyl, w2[at, :], NT)
+        danh = da * nh
+        gw_ref[1, :, at] += fold_rows(danh)
+        gw_ref[2, :, at] += fold_rows(da)
+        gain = wide[1:2, at]
+        dg = da * gain
+        dgn = danh * gain
+        dn_s[:, at] = dg
+        for q in range(CHUNK // 128):
+            s1 = s1 + dg[:, q * 128 : (q + 1) * 128]
+            s2 = s2 + dgn[:, q * 128 : (q + 1) * 128]
+        return acc, s1, s2
+
+    acc, s1, s2 = lax.fori_loop(0, chunks, outer, (jnp.zeros((tile, width), F32), zero, zero), unroll=2)
+    lay_ref[...] = (hidden + acc + nar[5:6]).astype(BF16)
+    s1 = jnp.sum(s1, axis=-1, keepdims=True) / ff
+    s2 = jnp.sum(s2, axis=-1, keepdims=True) / ff
+
+    def inner_back(j, acc):
+        at = pl.ds(pl.multiple_of(j * CHUNK, CHUNK), CHUNK)
+        dn = nrstd * (dn_s[:, at] - s1 - n_s[:, at] * s2)
+        din = (dn * gp_s[:, at].astype(F32)).astype(BF16)
+        din_ref[:, at] = din
+        gw_ref[0, :, at] += fold_rows(din.astype(F32))
+        return acc + mm(din, w1[:, at], NT)
+
+    dffn = lax.fori_loop(0, chunks, inner_back, jnp.zeros((tile, width), F32), unroll=2)
+    dy = dyl.astype(F32)
+    gn_ref[5] += fold_rows(dy)
+    gn_ref[3] += fold_rows(dffn * hhat)
+    gn_ref[4] += fold_rows(dffn)
+    dhid = dy + row_norm_back(dffn * nar[3:4], hhat, hrstd)
+    dhid_ref[...] = dhid
+    gn_ref[2] += fold_rows(dhid)
+    dlow = dhid.astype(BF16)
+    dlow_ref[...] = dlow
+    dpost = mm(dlow, wout[...], NT)
+    gn_ref[0] += fold_rows(dpost * ahat)
+    gn_ref[1] += fold_rows(dpost)
+    dsc_ref[...] = row_norm_back(dpost * nar[0:1], ahat, arstd).astype(BF16)
+
+
+def middle(scaled, x, dy, wout, w1, w2, narrow, wide):
+    rows, width = x.shape
+    ff = w1.shape[1]
+    tile = 256
+    thin = pl.BlockSpec((tile, width), lambda i: (i, 0))
+    fat = pl.BlockSpec((tile, ff), lambda i: (i, 0))
+    keep = lambda shape: pl.BlockSpec(shape, lambda i: (0,) * len(shape))
+    return pl.pallas_call(
+        middle_kernel,
+        grid=(rows // tile,),
+        in_specs=[
+            thin, thin, thin,
+            resident(wout.shape), resident(w1.shape), resident(w2.shape),
+            resident(narrow.shape), resident(wide.shape),
+        ],
+        out_specs=[thin, thin, thin, fat, fat, thin, thin, thin, keep((6, 8, width)), keep((3, 8, ff))],
+        out_shape=[
+            jax.ShapeDtypeStruct((rows, width), BF16),
+            jax.ShapeDtypeStruct((rows, width), BF16),
+            jax.ShapeDtypeStruct((rows, width), BF16),
+            jax.ShapeDtypeStruct((rows, ff), BF16),
+            jax.ShapeDtypeStruct((rows, ff), BF16),
+            jax.ShapeDtypeStruct((rows, width), F32),
+            jax.ShapeDtypeStruct((rows, width), BF16),
+            jax.ShapeDtypeStruct((rows, width), BF16),
+            jax.ShapeDtypeStruct((6, 8, width), F32),
+            jax.ShapeDtypeStruct((3, 8, ff), F32),
+        ],
+        scratch_shapes=[
+            pltpu.VMEM((tile, ff), F32),
+            pltpu.VMEM((tile, ff), BF16),
+            pltpu.VMEM((tile, ff), F32),
+        ],
+        compiler_params=pltpu.CompilerParams(vmem_limit_bytes=VMEM_CAP),
+        name="middle",
+    )(scaled, x, dy, wout, w1, w2, narrow, wide)
+
+
+def tail_kernel(dq_ref, dk_ref, dv_ref, x_ref, dhid_ref, w_ref, p_ref, out_ref, g_ref):
+    @pl.when(pl.program_id(0) == 0)
+    def _():
+        g_ref[...] = jnp.zeros_like(g_ref)
+
+    width = x_ref.shape[1]
+    hat, rstd = row_norm(x_ref[...].astype(F32))
+    dnormed = mm(dq_ref[...], w_ref[:, 0:width], NT)
+    dnormed = dnormed + mm(dk_ref[...], w_ref[:, width : 2 * width], NT)
+    dnormed = dnormed + mm(dv_ref[...], w_ref[:, 2 * width : 3 * width], NT)
+    g_ref[0] += fold_rows(dnormed * hat)
+    g_ref[1] += fold_rows(dnormed)
+    g_ref[2] += fold_rows(dq_ref[...].astype(F32))
+    g_ref[3] += fold_rows(dv_ref[...].astype(F32))
+    out_ref[...] = dhid_ref[...] + row_norm_back(dnormed * p_ref[0:1], hat, rstd)
+
+
+def tail(dq, dk, dv, x, dhid, weight, params):
+    rows, width = x.shape
+    tile = 256
+    thin = pl.BlockSpec((tile, width), lambda i: (i, 0))
+    return pl.pallas_call(
+        tail_kernel,
+        grid=(rows // tile,),
+        in_specs=[thin] * 5 + [resident(weight.shape), resident(params.shape)],
+        out_specs=[thin, pl.BlockSpec((4, 8, width), lambda i: (0, 0, 0))],
+        out_shape=[jax.ShapeDtypeStruct((rows, width), F32), jax.ShapeDtypeStruct((4, 8, width), F32)],
+        compiler_params=pltpu.CompilerParams(vmem_limit_bytes=VMEM_CAP),
+        name="tail",
+    )(dq, dk, dv, x, dhid, weight, params)
+
+
+def enter_kernel(depth, pieces, *refs):
+    shards = refs[:2]
+    tok = refs[2]
+    wholes = refs[3:5]
+    tok_whole = refs[5]
+    local, send, recv = refs[6:]
+    me = Place(depth)
+    gathers = [
+        Gather(me, shards[a], wholes[a], at, count, local.at[n], send.at[n], recv.at[n])
+        for n, (a, at, count) in enumerate(pieces)
+    ]
+    n = len(pieces)
+    swap = Swap(
+        me, tok.at[1 - me.y], lambda y: tok_whole.at[y], tok.at[me.y], tok_whole.at[me.y],
+        local.at[n], send.at[n, 0], recv.at[n, 0],
+    )
+    me.greet()
+    for g in gathers:
+        g.begin()
+    for g in gathers:
+        g.spread()
+    swap.begin()
+    for g in gathers:
+        g.from_y()
+        g.from_x()
+    for g in gathers:
+        g.from_corner()
+    for g in gathers:
+        g.end()
+    swap.end()
+
+
+def enter(small, qkv_weight, tokens, depth, collective_id):
+    shards = [small, qkv_weight]
+    part = qkv_weight.shape[0] // 2
+    pieces = [(0, 0, small.shape[0]), (1, 0, part), (1, part, part)]
+    count = len(pieces) + 1
+    anywhere = pl.BlockSpec(memory_space=pl.ANY)
+    out = pl.pallas_call(
+        functools.partial(enter_kernel, depth, pieces),
+        in_specs=[anywhere] * 3,
+        out_specs=[anywhere] * 3,
+        out_shape=[jax.ShapeDtypeStruct((depth, 2, 2, 2) + s.shape, s.dtype) for s in shards]
+        + [jax.ShapeDtypeStruct(tokens.shape, tokens.dtype)],
+        scratch_shapes=[
+            pltpu.SemaphoreType.DMA((count,)),
+            pltpu.SemaphoreType.DMA((count, 6 + depth)),
+            pltpu.SemaphoreType.DMA((count, 6 + depth)),
+        ],
+        compiler_params=pltpu.CompilerParams(
+            collective_id=collective_id, has_side_effects=True, vmem_limit_bytes=1024 * 1024
+        ),
+        name="enter",
+    )(small, qkv_weight, tokens)
+    wholes = [w.reshape((depth * 8 * w.shape[4],) + w.shape[5:]) for w in out[:2]]
+    return wholes[0], wholes[1], out[2].reshape(-1, tokens.shape[2])
+
+
+def leave_kernel(depth, pieces, *refs):
+    arrays = len(pieces)
+    parts, sums = refs[:arrays], refs[arrays : 2 * arrays]
+    local, send, recv = refs[2 * arrays : 2 * arrays + 3]
+    scratch = refs[2 * arrays + 3 :]
+    me = Place(depth)
+    scatters = [
+        Scatter(me, parts[n], 0, piece[0], *scratch[4 * n : 4 * n + 4], local.at[n], send.at[n], recv.at[n], sums[n])
+        for n, piece in enumerate(pieces)
+    ]
+    me.greet()
+    for s in scatters:
+        s.begin()
+    for s in scatters:
+        s.across()
+    for s in scatters:
+        s.along_x()
+    for s in scatters:
+        s.along_y()
+    for s in scatters:
+        s.end()
+
+
+def leave(parts, depth, collective_id):
+    parts = [shard_view(p, depth) for p in parts]
+    pieces = [(p.shape[4], p.shape[5], p.dtype) for p in parts]
+    count = len(parts)
+    anywhere = pl.BlockSpec(memory_space=pl.ANY)
+    vmem = pl.BlockSpec(memory_space=pltpu.VMEM)
+    return pl.pallas_call(
+        functools.partial(leave_kernel, depth, pieces),
+        in_specs=[anywhere] * count,
+        out_specs=[vmem] * count,
+        out_shape=[jax.ShapeDtypeStruct(p.shape[4:], F32) for p in parts],
+        scratch_shapes=[
+            pltpu.SemaphoreType.DMA((count,)),
+            pltpu.SemaphoreType.DMA((count, 3 + depth)),
+            pltpu.SemaphoreType.DMA((count, 3 + depth)),
+        ]
+        + scatter_scratch(pieces, depth),
+        compiler_params=pltpu.CompilerParams(
+            collective_id=collective_id, has_side_effects=True, vmem_limit_bytes=VMEM_CAP
+        ),
+        name="leave",
+    )(*parts)
+
+
+def fast_shards(
+    tokens, doc_lengths, out_cotangent, in_gain, in_bias, qkv_weight, q_bias, v_bias, head_scale, attn_gain,
+    attn_bias, out_weight, out_bias, ffn_gain, ffn_bias, fc1_weight, fc1_bias, mid_gain, mid_bias, fc2_weight,
+    fc2_bias,
+):
+    depth = lax.axis_size("dp") // 4
+    devices = depth * 8
+    half = tokens.shape[1]
+    rows = 2 * half
+    width = tokens.shape[2]
+    ff = fc1_weight.shape[1]
+    me = lax.axis_index("sp")
+    swap = [(0, 1), (1, 0)]
+
+    narrow_in = [in_gain, in_bias, q_bias, v_bias, attn_gain, attn_bias, out_bias, ffn_gain, ffn_bias, fc2_bias]
+    wide_in = [fc1_bias, mid_gain, mid_bias]
+    part = width // devices
+    wide_part = ff // devices
+    small = jnp.concatenate(narrow_in + wide_in + [head_scale])
+    used = small.shape[0]
+    small_rows = 16
+    small = jnp.pad(small, (0, small_rows * 128 - used)).reshape(small_rows, 128)
+    small, wqkv, x = enter(small, qkv_weight, tokens, depth, 0)
+    small = small.reshape(devices, small_rows * 128).astype(F32)
+    nn = len(narrow_in)
+    narrow = small[:, : nn * part].reshape(devices, nn, part).transpose(1, 0, 2).reshape(nn, width)
+    base = nn * part
+    wide = small[:, base : base + 3 * wide_part].reshape(devices, 3, wide_part).transpose(1, 0, 2).reshape(3, ff)
+    base = base + 3 * wide_part
+    heads_each = head_scale.shape[0]
+    hs = small[0:2, base : base + heads_each].reshape(2 * heads_each)
+
+    lengths = lax.dynamic_index_in_dim(doc_lengths[0], me, 0, keepdims=False)
+    starts = jnp.arange(rows // BLOCK, dtype=jnp.int32) * BLOCK
+    ids = jnp.sum((starts[:, None] >= jnp.cumsum(lengths)[None, :]).astype(jnp.int32), axis=1)
+
+    in_params = narrow[0:2]
+    bias_row = jnp.concatenate([narrow[2], jnp.zeros_like(narrow[2]), narrow[3]])[None, :]
+    normed, qkv = qkv_project(x, wqkv, in_params, bias_row)
+    scaled, mixed, lse, (wout, w1, w2), dy = attend_fwd(
+        qkv, ids, hs, [out_weight, fc1_weight, fc2_weight], out_cotangent, depth, 1
+    )
+    layer, post, ffn_in, active, d_inner, d_hidden, d_low, d_scaled, grads_narrow, grads_wide = middle(
+        scaled, x, dy, wout, w1, w2, narrow[4:10], wide
+    )
+
+    def weight_grad(left, right):
+        return jnp.einsum("ti,tj->ij", left, right, preferred_element_type=F32).astype(BF16)
+
+    g_fc2 = weight_grad(active, dy)
+    g_fc1 = weight_grad(ffn_in, d_inner)
+    g_out = weight_grad(post, d_low)
+    (dq, dk, dv, delta), (s_fc2, s_fc1, s_out), layer_out = attend_bwd(
+        qkv, mixed, d_scaled, lse, ids, hs, [g_fc2, g_fc1, g_out], layer, depth, 2
+    )
+    g_q = weight_grad(normed, dq)
+    g_k = weight_grad(normed, dk)
+    g_v = weight_grad(normed, dv)
+    d_input, grads_in = tail(dq, dk, dv, x, d_hidden, wqkv, in_params)
+    d_sent = lax.dynamic_slice_in_dim(d_input, (1 - me) * half, half, 0).astype(BF16)
+    d_got = lax.ppermute(d_sent, "sp", swap).astype(F32)
+    d_kept = lax.dynamic_slice_in_dim(d_input, me * half, half, 0)
+    input_grad = jnp.stack([jnp.where(me == 0, d_kept, d_got), jnp.where(me == 0, d_got, d_kept)])
+
+    hs_grad = jnp.sum(delta, axis=(2, 3)).reshape(-1) / hs
+    narrow_grads = jnp.concatenate([jnp.sum(grads_in, axis=1), jnp.sum(grads_narrow, axis=1)], axis=0)
+    wide_grads = jnp.sum(grads_wide, axis=1)
+    packed = jnp.concatenate(
+        [
+            narrow_grads.reshape(nn, devices, part).transpose(1, 0, 2).reshape(devices, nn * part),
+            wide_grads.reshape(3, devices, wide_part).transpose(1, 0, 2).reshape(devices, 3 * wide_part),
+            jnp.tile(hs_grad.reshape(2, heads_each), (devices // 2, 1)),
+        ],
+        axis=1,
+    )
+    tiles = (used + 1023) // 1024 * 8
+    packed = jnp.pad(packed, ((0, 0), (0, tiles * 128 - used))).reshape(devices * tiles, 128)
+    s_q, s_k, s_v, s_small = leave([g_q, g_k, g_v, packed], depth, 3)
+    s_small = s_small.reshape(-1)
+    nar = [s_small[k * part : (k + 1) * part] for k in range(nn)]
+    base = nn * part
+    wid = [s_small[base + k * wide_part : base + (k + 1) * wide_part] for k in range(3)]
+    base = base + 3 * wide_part
+    s_hs = s_small[base : base + heads_each]
+    return (
+        layer_out, input_grad, nar[0], nar[1], jnp.concatenate([s_q, s_k, s_v], axis=1), nar[2], nar[3], s_hs,
+        nar[4], nar[5], s_out, nar[6], nar[7], nar[8], s_fc1, wid[0], wid[1], wid[2], s_fc2, nar[9],
+    )
+
+
 LONGEST = 2048
-
-
-EPS = 1e-05
 
 
 def layer_norm(values, norm_gain, norm_shift):
@@ -444,8 +1394,9 @@
 
 
 def solution(mesh):
+    body = fast_shards if mesh.shape["sp"] == 2 and mesh.shape["dp"] % 4 == 0 and mesh.shape["dp"] >= 8 else shards
     return jax.shard_map(
-        shards,
+        body,
         mesh=mesh,
         in_specs=(
             P(None, ("dp", "sp"), None),

time: 3700 us -> 844 us (0.23)
  matrix products: 1230 us -> 78 us
  waiting for transfers between devices: 1090 us -> 0.01 us
  Pallas kernels: 0 us -> 713 us
  other arithmetic: 571 us -> 12.1 us
  local copies, waits for them, and re-layouts: 377 us -> 33.2 us
  blocking collectives: 319 us -> 0 us
  starting transfers between devices: 41.5 us -> 1.28 us
    dot_general x80 -> x6, matrix products: 1230 us -> 78 us  [weight_grad(): jnp.einsum('ti,tj->ij', left, right, preferred_element_type=F32)]
    reduce_scatter x4 -> x0, waiting for transfers between devices: 927 us -> none  [the longest x1 361 us: reduce_grads(): lax.psum_scatter(grad_set[11], ('dp', 'sp'), scatter_dimension=0, tiled=T...]
    pallas_call x0 -> x7, Pallas kernels: none -> 713 us  [the longest x1 192 us: attend_bwd(): pl.pallas_call(functools.partial(attend_bwd_kernel, depth, pieces), grid=...]
    reduce_sum x34 -> x5, other arithmetic: 276 us -> 1.03 us  [the longest x1 0.69 us: fast_shards(): jnp.sum((starts[:, None] >= jnp.cumsum(lengths)[None, :]).astype(jnp.int3...]
    convert_element_type x29 -> x0, other arithmetic: 247 us -> none  [the longest x8 219 us: one_block(): grad_scores = (prob_rows * (grad_probs - row_inner)).astype(jnp.bfloat16)]
    all_gather x3 -> x0, blocking collectives: 209 us -> none  [the longest x1 81.3 us: collect(): lax.all_gather(fc1_bias, ('dp', 'sp'), axis=0, tiled=True)]
    all_to_all x7 -> x0, waiting for transfers between devices: 151 us -> none  [the longest x2 74.3 us: shards(): lax.all_to_all(qkv_sent, 'sp', split_axis=2, concat_axis=0, tiled=True)]
    unnamed x331 -> x45, local copies, waits for them, and re-layouts: 77.9 us -> 13.2 us
  transfers between devices with their start and end apart: 16 -> 1, of which waited for: 9 -> 0; matrix products, arithmetic and copies ran while one was open for 37% -> 4% of each run, Pallas kernels for 0% -> 7%
where the time goes in v1:
time: 844 us; the launch traced here: 839 us
  Pallas kernels  713 us (84%)
  matrix products  78 us (9%)
  local copies, waits for them, and re-layouts  33.2 us (4%)
  other arithmetic  12.1 us (1%)
    pallas_call x1, Pallas kernels, attend_bwd(): pl.pallas_call(functools.partial(attend_bwd_kernel, depth, pieces), grid=...  192 us
    pallas_call x1, Pallas kernels, middle(): pl.pallas_call(middle_kernel, grid=(rows // tile,), in_specs=[thin, thin,...  173 us
    pallas_call x1, Pallas kernels, attend_fwd(): pl.pallas_call(functools.partial(attend_fwd_kernel, depth, pieces), grid=...  162 us
    pallas_call x1, Pallas kernels, enter(): pl.pallas_call(functools.partial(enter_kernel, depth, pieces), in_specs=[...  78.3 us
    dot_general x6, matrix products, weight_grad(): jnp.einsum('ti,tj->ij', left, right, preferred_element_type=F32)  78 us
    pallas_call x1, Pallas kernels, leave(): pl.pallas_call(functools.partial(leave_kernel, depth, pieces), in_specs=[...  62 us
    pallas_call x1, Pallas kernels, tail(): pl.pallas_call(tail_kernel, grid=(rows // tile,), in_specs=[thin] * 5 + [...  25.3 us
    pallas_call x1, Pallas kernels, qkv_project(): pl.pallas_call(qkv_kernel, grid=(rows // tile,), in_specs=[pl.BlockSpec((...  20.9 us
  transfers between devices with their start and end apart: 1, of which 0 were waited for; matrix products, arithmetic and copies ran while one was open for 4% of the time, Pallas kernels for 7%

profile of v1, /device:TPU:0, one launch (start us, length us, event | category | flops | bytes accessed | tf_op | source)
XLA Modules:
  0.0 838.9 jit_solution(14496746505316452456)
XLA Ops:
  0.7 9.4 %concatenate.15 = bf16[712]{0:T(1024)(128)(2,1)S(1)} concatenate(bf16[32]{0:T(256)(128)(2,1)} %param.24, bf16[32]{0:T(256)(128)(2,1)} %param.25, bf16[32]{0:T(256)(128)(2,1)} %param.27, bf16[32]{0:T(256)(128)(2,1)} %param.28, bf16[32]{0:T(256)(128)(2,1)} %param.30, bf16[32]{0:T(256)(128)(2,1)} %param.31, bf16[32]{0:T(256)(128)(2,1)} %param.33, bf16[32]{0:T(256)(128)(2,1)} %param.34, ...), dimensions={0} | concatenate | bytes 2848 | tf_op jit(solution)/shard_map/concatenate | solution.py:889
  10.1 2.2 copy-done.4
  13.2 78.3 %enter.1 = (bf16[4,2,2,2,16,128]{5,4,3,2,1,0:T(8,128)(2,1)S(1)}, bf16[4,2,2,2,32,3072]{5,4,3,2,1,0:T(8,128)(2,1)S(1)}, bf16[2,1024,1024]{2,1,0:T(8,128)(2,1)S(1)}) custom-call(bf16[16,128]{1,0:T(8,128)(2,1)S(1)} %pad_bitcast_fusion.refs_0_, bf16[32,3072]{1,0:T(8,128)(2,1)S(1)} %copy-done.5, bf16[2,1024,1024]{2,1,0:T(8,128)(2,1)S(1)} %copy-done.4), custom_call_target="tpu_custom_call" | custom-call | tf_op jit(solution)/shard_map/enter/pallas_call | solution.py:804
  91.6 2.0 copy-done.2
  93.6 2.6 copy-done.3
  101.0 20.9 %qkv_project.1 = (bf16[2048,1024]{1,0:T(8,128)(2,1)}, bf16[2048,3072]{1,0:T(8,128)(2,1)}) custom-call(bf16[2048,1024]{1,0:T(8,128)(2,1)} %bitcast.58, bf16[1024,3072]{1,0:T(8,128)(2,1)} %bitcast.61, f32[2,1024]{1,0:T(2,128)} %slice.74.p_ref, f32[1,3072]{1,0:T(1,128)} %bitcast.88), custom_call_target="tpu_custom_call" | custom-call | tf_op jit(solution)/shard_map/qkv_project/pallas_call | solution.py:572
  121.9 161.9 %attend_fwd.1 = (bf16[2048,1024]{1,0:T(8,128)(2,1)}, f32[2048,1024]{1,0:T(8,128)}, f32[8,2,4,512]{3,2,1,0:T(4,128)}, bf16[4,2,2,2,32,1024]{5,4,3,2,1,0:T(8,128)(...) custom-call(s32[4]{0:T(128)} %convert_reduce_fusion.refs_0_, ...), custom_call_target="tpu_custom_call" | custom-call | tf_op jit(solution)/shard_map/attend_fwd/pallas_call | solution.py:351
  283.9 173.2 %middle.1 = (bf16[2048,1024]{1,0:T(8,128)(2,1)}, bf16[2048,1024]{1,0:T(8,128)(2,1)}, bf16[2048,1024]{1,0:T(8,128)(2,1)}, bf16[2048,4096]{1,0:T(8,128)(2,1)}, bf1...) custom-call(bf16[2048,1024]{1,0:T(8,128)(2,1)} %get-tuple-element.61, ...), custom_call_target="tpu_custom_call" | custom-call | tf_op jit(solution)/shard_map/middle/pallas_call | solution.py:703
  457.1 24.2 %convolution_convert_fusion.1 = bf16[4096,1024]{1,0:T(8,128)(2,1)} fusion(bf16[2048,4096]{1,0:T(8,128)(2,1)} %get-tuple-element.68, bf16[2048,1024]{1,0:T(8,128)(2,1)} %bitcast.69), kind=kOutput, calls=%fused_computation.2 | convolution fusion | flops 17184063488 | bytes 29360128 | tf_op jit(solution)/shard_map/ti,tj->ij/dot_general | solution.py:918
  481.3 9.5 %convolution_convert_fusion.5 = bf16[1024,1024]{1,0:T(8,128)(2,1)} fusion(bf16[2048,1024]{1,0:T(8,128)(2,1)} %get-tuple-element.71, bf16[2048,1024]{1,0:T(8,128)(2,1)} %get-tuple-element.72), kind=kOutput, calls=%fused_computation.11 | convolution fusion | flops 4296015872 | bytes 10485760 | tf_op jit(solution)/shard_map/ti,tj->ij/dot_general | solution.py:918
  491.3 21.0 %convolution_convert_fusion = bf16[1024,4096]{1,0:T(8,128)(2,1)} fusion(bf16[2048,1024]{1,0:T(8,128)(2,1)S(1)} %copy-done.18, bf16[2048,4096]{1,0:T(8,128)(2,1)S(1)} %copy-done.16), kind=kOutput, calls=%fused_computation.1 | convolution fusion | flops 17184063488 | bytes 29360128 | tf_op jit(solution)/shard_map/ti,tj->ij/dot_general | solution.py:918
  512.3 191.6 %attend_bwd.1 = (bf16[2048,1024]{1,0:T(8,128)(2,1)}, bf16[2048,1024]{1,0:T(8,128)(2,1)}, bf16[2048,1024]{1,0:T(8,128)(2,1)}, f32[8,2,4,512]{3,2,1,0:T(4,128)}, f...) custom-call(s32[4]{0:T(128)} %convert_reduce_fusion.refs_0_, ...), custom_call_target="tpu_custom_call" | custom-call | tf_op jit(solution)/shard_map/attend_bwd/pallas_call | solution.py:509
  703.9 25.3 %tail.1 = (f32[2048,1024]{1,0:T(8,128)}, f32[4,8,1024]{2,1,0:T(8,128)}) custom-call(bf16[2048,1024]{1,0:T(8,128)(2,1)} %get-tuple-element.75.dq_ref, bf16[2048,1024]{1,0:T(8,128)(2,1)} %get-tuple-element.76.dk_ref, bf16[2048,1024]{1,0:T(8,128)(2,1)} %get-tuple-element.77.dv_ref, bf16[2048,1024]{1,0:T(8,128)(2,1)} %bitcast.60, ...), custom_call_target="tpu_custom_call" | custom-call | tf_op jit(solution)/shard_map/tail/pallas_call | solution.py:755
  729.1 2.7 dynamic-slice_convert_fusion
  733.1 8.1 convolution_convert_fusion.4
  741.3 5.8 convolution_convert_fusion.3
  748.7 9.4 %convolution_convert_fusion.2 = bf16[1024,1024]{1,0:T(8,128)(2,1)} fusion(bf16[2048,1024]{1,0:T(8,128)(2,1)} %get-tuple-element.80, bf16[2048,1024]{1,0:T(8,128)(2,1)} %get-tuple-element.77.dv_ref), kind=kOutput, calls=%fused_computation.8 | convolution fusion | flops 4296015872 | bytes 10485760 | tf_op jit(solution)/shard_map/ti,tj->ij/dot_general | solution.py:918
  758.1 62.0 %leave.1 = (f32[32,1024]{1,0:T(8,128)}, f32[32,1024]{1,0:T(8,128)}, f32[32,1024]{1,0:T(8,128)}, f32[8,128]{1,0:T(8,128)}) custom-call(bf16[4,2,2,2,32,1024]{5,4,3,2,1,0:T(8,128)(2,1)} %bitcast.70, bf16[4,2,2,2,32,1024]{5,4,3,2,1,0:T(8,128)(2,1)} %bitcast.71, bf16[4,2,2,2,32,1024]{5,4,3,2,1,0:T(8,128)(2,1)} %bitcast.74, f32[4,2,2,2,8,128]{5,4,3,2,1,0:T(8,128)} %bitcast.79), custom_call_target="tpu_custom_call" | custom-call | tf_op jit(solution)/shard_map/leave/pallas_call | solution.py:853
  821.4 1.4 fusion.5
  822.7 1.6 fusion.4
  824.4 1.8 pad_maximum_fusion.1
  826.2 4.0 fusion
  830.2 4.3 pad_maximum_fusion
  834.5 2.0 copy.60
  (78 shorter events, 12.5 us)
Async XLA Ops:
  0.7 96.8 %copy-start = (s32[1,2,4]{2,1,0:T(2,128)S(1)}, s32[1,2,4]{2,1,0:T(2,128)}, u32[]{:S(2)}) copy-start(s32[1,2,4]{2,1,0:T(2,128)} %param.22) | copy-start | bytes 100
  10.1 2.2 copy-start.4
  12.3 0.9 copy-start.5
  91.6 2.0 copy-start.2
  93.6 2.6 copy-start.3
  481.3 9.5 %copy-start.16 = (bf16[2048,4096]{1,0:T(8,128)(2,1)S(1)}, bf16[2048,4096]{1,0:T(8,128)(2,1)}, u32[]{:S(2)}) copy-start(bf16[2048,4096]{1,0:T(8,128)(2,1)} %get-tuple-element.70) | copy-start | bytes 50331652
  481.3 10.0 %copy-start.18 = (bf16[2048,1024]{1,0:T(8,128)(2,1)S(1)}, bf16[2048,1024]{1,0:T(8,128)(2,1)}, u32[]{:S(2)}) copy-start(bf16[2048,1024]{1,0:T(8,128)(2,1)} %get-tuple-element.69) | copy-start | bytes 12582916
  729.1 4.0 copy-start.7
  731.8 94.4 %collective-permute-start = (bf16[1024,1024]{1,0:T(8,128)(2,1)S(1)}, bf16[1024,1024]{1,0:T(8,128)(2,1)}, u32[]{:S(2)}, u32[]{:S(2)}) collective-permute-start(bf16[1024,1024]{1,0:T(8,128)(2,1)S(1)} %dynamic-slice_convert_fusion), channel_id=1, source_target_pairs={{0,1},{1,0},{2,3},{3,2},{4,5},{5,4},{6,7},{7,6},{8,9},{9,8},{10,11... | collective-permute-start | bytes 6291464 | tf_op jit(solution)/shard_map/ppermute | solution.py:931
  733.1 8.2 copy-start.6
  733.1 8.2 copy-start.17
  741.3 5.8 copy-start.13
  741.3 5.8 copy-start.12
  741.3 5.9 copy-start.15
  741.3 6.5 copy-start.11
  830.2 4.3 copy-start.8
  834.5 4.3 copy-start.1
  834.5 2.0 copy-start.14
  834.5 2.7 copy-start.10
  834.5 3.5 copy-start.9

commit v2 on v1

--- a/solution.py
+++ b/solution.py
@@ -17,12 +17,24 @@
 VMEM_CAP = 60 * 1024 * 1024
 NT = (((1,), (1,)), ((), ()))
 NN = (((1,), (0,)), ((), ()))
-FWD_STEPS = ((4, 8, 12, 16, 20), (8, 12, 16, 20, 24), (12, 17, 22, 27, 31), (16, 21, 26, 31, 31))
-BWD_STEPS = ((1, 2, 3, 4, 5), (7, 13, 18, 23, 26), (10, 16, 21, 26, 29), (14, 20, 25, 30, 32))
+FWD_STEPS = ((0, 0, 10, 11), (11, 12, 28, 29), (20, 21, 30, 31), (24, 25, 32, 32))
+BWD_STEPS = ((1, 2, 3, 4, 5), (9, 15, 20, 26, 28), (14, 19, 24, 29, 30), (18, 23, 28, 32, 32))
 
 
 def mm(a, b, dims=NN):
     return lax.dot_general(a, b, dims, preferred_element_type=F32)
+
+
+def same_sequence(lengths, y):
+    ends = []
+    for k in range(lengths.shape[2]):
+        ends.append(lengths[0, y, k] + (ends[-1] if ends else 0))
+
+    def same(i, kb):
+        between = [((e > kb * BLOCK) & (e <= i * BLOCK)).astype(jnp.int32) for e in ends]
+        return sum(between) == 0
+
+    return same
 
 
 class Place:
@@ -61,8 +73,10 @@
 
 
 class Gather:
-    def __init__(self, me, shard, whole, at, count, local, send, recv):
-        self.me, self.shard, self.whole = me, shard.at[pl.ds(at, count)], whole
+    def __init__(self, me, shard, stage, whole, at, count, local, send, recv):
+        self.me, self.whole = me, whole
+        if shard is not None:
+            self.shard, self.stage = shard.at[pl.ds(at, count)], stage.at[pl.ds(at, count)]
         self.rows = pl.ds(at, count)
         self.local, self.send, self.recv = local, send, recv
 
@@ -70,13 +84,16 @@
         me = self.me
         return self.whole.at[z, me.x, me.c, me.y, self.rows]
 
+    def load(self):
+        return pltpu.make_async_copy(self.shard, self.stage, self.local)
+
     def keep(self):
-        return pltpu.make_async_copy(self.shard, self.own(self.me.z), self.local)
+        return pltpu.make_async_copy(self.stage, self.own(self.me.z), self.local)
 
     def depth_hop(self, s, landed):
         me = self.me
         z = me.along(me.depth - s) if landed else me.z
-        return remote(self.shard, self.own(z), self.send.at[6 + s], self.recv.at[6 + s], me.column(s))
+        return remote(self.stage, self.own(z), self.send.at[6 + s], self.recv.at[6 + s], me.column(s))
 
     def hop(self, x, y, n, peer, c=None):
         group = self.whole.at[:, x, self.me.c if c is None else c, y, self.rows]
@@ -90,17 +107,27 @@
         peer = me.next_y if n == 0 else me.next_x if n < 3 else me.twin
         return self.hop(gx, gy, n, peer, c)
 
+    def ready(self):
+        self.load().start()
+
     def begin(self):
+        self.load().wait()
         self.keep().start()
         for s in range(1, self.me.depth):
             self.depth_hop(s, False).start()
 
-    def spread(self):
+    def landed(self):
         self.keep().wait()
         for s in range(1, self.me.depth):
             self.depth_hop(s, True).wait()
+
+    def launch(self):
         for n in (0, 1, 3):
             self.path(n).start()
+
+    def spread(self):
+        self.landed()
+        self.launch()
 
     def from_y(self):
         me = self.me
@@ -126,13 +153,18 @@
 
 
 class Swap:
-    def __init__(self, me, sent, landing, kept, place, local, send, recv):
+    def __init__(self, me, sent, landing, kept, stage, place, local, send, recv):
         self.out = remote(sent, landing(me.y), send, recv, me.next_y)
         self.into = remote(sent, landing(1 - me.y), send, recv, me.next_y)
-        self.keep = pltpu.make_async_copy(kept, place, local)
+        self.load = pltpu.make_async_copy(kept, stage, local)
+        self.keep = pltpu.make_async_copy(stage, place, local)
+
+    def ready(self):
+        self.load.start()
 
     def begin(self):
         self.out.start()
+        self.load.wait()
         self.keep.start()
 
     def end(self):
@@ -249,43 +281,46 @@
 
 
 def attend_fwd_kernel(depth, pieces, *refs):
-    ids, hs, q_ref, k_ref, v_ref = refs[:5]
-    shards = refs[5:8]
-    cot = refs[8]
-    o_ref, mixed_ref, lse_ref = refs[9:12]
-    wholes = refs[12:15]
-    cot_whole = refs[15]
-    vt, local, send, recv = refs[16:]
+    lengths, hs, q_ref, k_ref, v_ref = refs[:5]
+    shard, cot = refs[6:8]
+    o_ref, mixed_ref, lse_ref = refs[8:11]
+    wholes = refs[11:13]
+    cot_whole = refs[13]
+    vt, local, send, recv, shard_stage, cot_stage = refs[14:]
     pair = pl.program_id(0)
     me = Place(depth)
-    half = cot.shape[1]
+    same = same_sequence(lengths, me.y)
     gathers = [
-        Gather(me, shards[a], wholes[a], at, count, local.at[n], send.at[n], recv.at[n])
+        Gather(me, shard if a else None, shard_stage, wholes[a], at, count, local.at[n], send.at[n], recv.at[n])
         for n, (a, at, count) in enumerate(pieces)
     ]
     n = len(pieces)
     swap = Swap(
-        me, cot.at[1 - me.y], lambda y: cot_whole.at[y], cot.at[me.y], cot_whole.at[me.y],
+        me, cot.at[1 - me.y], lambda y: cot_whole.at[y], cot.at[me.y], cot_stage, cot_whole.at[me.y],
         local.at[n], send.at[n, 0], recv.at[n, 0],
     )
     plan = {}
     due(plan, 0, me.greet)
-    for g in gathers:
-        due(plan, 0, g.begin)
-    due(plan, 10, swap.begin)
+    due(plan, 0, swap.ready)
     for n, g in enumerate(gathers):
-        due(plan, FWD_STEPS[0][n], g.spread)
+        if pieces[n][0]:
+            due(plan, 0, g.ready)
+    for n, g in enumerate(gathers):
+        due(plan, 0, g.begin if pieces[n][0] else g.launch)
+        if pieces[n][0]:
+            due(plan, FWD_STEPS[0][n], g.spread)
         due(plan, FWD_STEPS[1][n], g.from_y)
         due(plan, FWD_STEPS[2][n], g.from_x)
         due(plan, FWD_STEPS[3][n], g.from_corner)
-        due(plan, 31, g.end)
-    due(plan, 31, swap.end)
-    last = plan.pop(31)
+        due(plan, 32, g.end)
+    due(plan, 6, swap.begin)
+    due(plan, 32, swap.end)
+    last = plan.pop(32)
     rows = q_ref.shape[0]
     blocks = rows // BLOCK
     factor = LOG2E / 8.0
     masks = head_pair_masks()
-    gains = jnp.where(masks[0], hs[2 * pair], hs[2 * pair + 1])
+    gains = jnp.where(masks[0], hs[0, 2 * pair], hs[0, 2 * pair + 1])
     for j in range(blocks):
         vtr = v_ref[j * BLOCK : (j + 1) * BLOCK, :].astype(F32).T.astype(BF16)
         for h in range(2):
@@ -294,8 +329,8 @@
     key_at = lax.broadcasted_iota(jnp.int32, (BLOCK, BLOCK), 0)
     query_at = lax.broadcasted_iota(jnp.int32, (BLOCK, BLOCK), 1)
 
-    def one_query(i, _):
-        perform(pair * blocks + i, plan)
+    def one_query(i):
+        perform(pair, {k // blocks: plan[k] for k in plan if k % blocks == i})
         q = q_ref[pl.ds(i * BLOCK, BLOCK), :]
         qh = [jnp.where(m, q, jnp.zeros_like(q)) for m in masks]
 
@@ -310,7 +345,7 @@
                     p = jnp.exp2(s * factor - m * factor).astype(BF16)
                     out.append((m, mm(vt[kb, h], p)))
                 else:
-                    bias = jnp.where(ids[i] == ids[kb], 0.0, NEG)
+                    bias = jnp.where(same(i, kb), 0.0, NEG)
                     m_old, acc = carry[h]
                     m = jnp.maximum(m_old, jnp.max(s, axis=0, keepdims=True) + bias)
                     p = jnp.exp2(s * factor - (m - bias) * factor).astype(BF16)
@@ -319,7 +354,8 @@
             return tuple(out)
 
         carry = step(i, None, True)
-        carry = lax.fori_loop(0, i, lambda kb, c: step(kb, c, False), carry)
+        for kb in range(i):
+            carry = step(kb, carry, False)
         outs = []
         for h in range(2):
             m, acc = carry[h]
@@ -329,13 +365,13 @@
         both = jnp.concatenate(outs, axis=0).T
         mixed_ref[pl.ds(i * BLOCK, BLOCK), :] = both
         o_ref[pl.ds(i * BLOCK, BLOCK), :] = (both * gains).astype(BF16)
-        return 0
-
-    lax.fori_loop(0, blocks, one_query, 0)
+
+    for i in range(blocks):
+        one_query(i)
     perform(pair, {pl.num_programs(0) - 1: last})
 
 
-def attend_fwd(qkv, ids, hs, shards, cot, depth, collective_id):
+def attend_fwd(qkv, lengths, hs, begun, shard, cot, depth, collective_id):
     rows, width3 = qkv.shape
     width = width3 // 3
     pairs = width // 128
@@ -343,54 +379,58 @@
     spec = lambda part: pl.BlockSpec((rows, 128), lambda p, part=part: (0, part * pairs + p))
     smem = pl.BlockSpec(memory_space=pltpu.SMEM)
     anywhere = pl.BlockSpec(memory_space=pl.ANY)
-    pieces = [(0, 0, shards[0].shape[0])]
-    for a in (1, 2):
-        part = shards[a].shape[0] // 2
+    pieces = []
+    for a, count in enumerate((begun.shape[4], shard.shape[0])):
+        part = count // 2
         pieces += [(a, 0, part), (a, part, part)]
     count = len(pieces) + 1
     out = pl.pallas_call(
         functools.partial(attend_fwd_kernel, depth, pieces),
         grid=(pairs,),
-        in_specs=[smem, smem, spec(0), spec(1), spec(2)] + [anywhere] * 4,
+        in_specs=[smem, smem, spec(0), spec(1), spec(2)] + [anywhere] * 3,
         out_specs=[
             pl.BlockSpec((rows, 128), lambda p: (0, p)),
             pl.BlockSpec((rows, 128), lambda p: (0, p)),
             pl.BlockSpec((1, 2, blocks, BLOCK), lambda p: (p, 0, 0, 0)),
         ]
-        + [anywhere] * 4,
+        + [anywhere] * 3,
         out_shape=[
             jax.ShapeDtypeStruct((rows, width), BF16),
             jax.ShapeDtypeStruct((rows, width), F32),
             jax.ShapeDtypeStruct((pairs, 2, blocks, BLOCK), F32),
-        ]
-        + [jax.ShapeDtypeStruct((depth, 2, 2, 2) + s.shape, s.dtype) for s in shards]
-        + [jax.ShapeDtypeStruct(cot.shape, cot.dtype)],
+            jax.ShapeDtypeStruct(begun.shape, begun.dtype),
+            jax.ShapeDtypeStruct((depth, 2, 2, 2) + shard.shape, shard.dtype),
+            jax.ShapeDtypeStruct(cot.shape, cot.dtype),
+        ],
+        input_output_aliases={5: 3},
         scratch_shapes=[
             pltpu.VMEM((blocks, 2, 80, BLOCK), BF16),
             pltpu.SemaphoreType.DMA((count,)),
             pltpu.SemaphoreType.DMA((count, 6 + depth)),
             pltpu.SemaphoreType.DMA((count, 6 + depth)),
+            pltpu.VMEM(shard.shape, shard.dtype),
+            pltpu.VMEM(cot.shape[1:], cot.dtype),
         ],
         compiler_params=pltpu.CompilerParams(
             vmem_limit_bytes=VMEM_CAP, collective_id=collective_id, has_side_effects=True
         ),
         name="attend_fwd",
-    )(ids, hs, qkv, qkv, qkv, *shards, cot)
-    wholes = [w.reshape((depth * 8 * w.shape[4],) + w.shape[5:]) for w in out[3:6]]
-    return out[0], out[1], out[2], wholes, out[6].reshape(rows, width)
+    )(lengths, hs, qkv, qkv, qkv, begun, shard, cot)
+    return out[0], out[1], out[2], out[3], out[4], out[5].reshape(rows, width)
 
 
 def attend_bwd_kernel(depth, pieces, *refs):
-    ids, hs, q_ref, k_ref, v_ref, o_ref, g_ref, lse_ref = refs[:8]
+    lengths, hs, q_ref, k_ref, v_ref, o_ref, g_ref, lse_ref = refs[:8]
     parts = refs[8:11]
     layer = refs[11]
     dq_ref, dk_ref, dv_ref, delta_ref = refs[12:16]
     sums = refs[16:19]
     layer_out = refs[19]
-    kt, dk_acc, dv_acc, local, send, recv = refs[20:26]
-    scratch = refs[26:]
+    kt, dk_acc, dv_acc, local, send, recv, layer_stage = refs[20:27]
+    scratch = refs[27:]
     pair = pl.program_id(0)
     me = Place(depth)
+    same = same_sequence(lengths, me.y)
     scatters = [
         Scatter(
             me, parts[a], at, count, *scratch[4 * n : 4 * n + 4], local.at[n], send.at[n], recv.at[n], sums[a]
@@ -401,9 +441,10 @@
     half = layer_out.shape[1]
     swap = Swap(
         me, layer.at[pl.ds((1 - me.y) * half, half)], lambda y: layer_out.at[y],
-        layer.at[pl.ds(me.y * half, half)], layer_out.at[me.y], local.at[n], send.at[n, 0], recv.at[n, 0],
+        layer.at[pl.ds(me.y * half, half)], layer_stage, layer_out.at[me.y], local.at[n], send.at[n, 0], recv.at[n, 0],
     )
     plan = {}
+    due(plan, 0, swap.ready)
     due(plan, 0, me.greet)
     for s in scatters:
         due(plan, 0, s.begin)
@@ -412,7 +453,7 @@
         due(plan, BWD_STEPS[1][n], s.along_x)
         due(plan, BWD_STEPS[2][n], s.along_y)
         due(plan, BWD_STEPS[3][n], s.end)
-    due(plan, 14, swap.begin)
+    due(plan, 0, swap.begin)
     due(plan, 32, swap.end)
     last = plan.pop(32)
     rows = q_ref.shape[0]
@@ -423,11 +464,11 @@
         kt[j] = k_ref[j * BLOCK : (j + 1) * BLOCK, :].astype(F32).T.astype(BF16)
     key_at = lax.broadcasted_iota(jnp.int32, (BLOCK, BLOCK), 0)
     query_at = lax.broadcasted_iota(jnp.int32, (BLOCK, BLOCK), 1)
-    gains = jnp.where(masks[0], hs[2 * pair], hs[2 * pair + 1])
+    gains = jnp.where(masks[0], hs[0, 2 * pair], hs[0, 2 * pair + 1])
     picks = jnp.concatenate([m.astype(F32) for m in masks] + [jnp.zeros((6, 128), F32)], axis=0).astype(BF16)
 
-    def one_query(i, _):
-        perform(pair * blocks + i, plan)
+    def one_query(i):
+        perform(pair, {k // blocks: plan[k] for k in plan if k % blocks == i})
         at = pl.ds(i * BLOCK, BLOCK)
         q = q_ref[at, :]
         g = (g_ref[at, :].astype(F32) * gains).astype(BF16)
@@ -456,7 +497,7 @@
                     p = jnp.exp2(s * factor - lse[h])
                     p = jnp.where(key_at <= query_at, p, 0.0)
                 else:
-                    bias = jnp.where(ids[i] == ids[kb], 0.0, -NEG)
+                    bias = jnp.where(same(i, kb), 0.0, -NEG)
                     p = jnp.exp2(s * factor - (lse[h] + bias))
                 ds = (p * (dp - delta[h])).astype(BF16)
                 dvh = mm(p.astype(BF16), gh[h])
@@ -474,12 +515,13 @@
             return tuple(out)
 
         carry = step(i, None, True)
-        carry = lax.fori_loop(0, i, lambda kb, c: step(kb, c, False), carry)
+        for kb in range(i):
+            carry = step(kb, carry, False)
         both = jnp.concatenate(carry, axis=0) * 0.125
         dq_ref[at, :] = both.T.astype(BF16)
-        return 0
-
-    lax.fori_loop(0, blocks, one_query, 0)
+
+    for i in range(blocks):
+        one_query(i)
     dk_ref[...] = (dk_acc[...] * 0.125).astype(BF16)
     dv_ref[...] = dv_acc[...].astype(BF16)
     perform(pair, {pl.num_programs(0) - 1: last})
@@ -489,7 +531,7 @@
     return part.reshape((depth, 2, 2, 2, part.shape[0] // (depth * 8)) + part.shape[1:])
 
 
-def attend_bwd(qkv, mixed, d_scaled, lse, ids, hs, parts, layer, depth, collective_id):
+def attend_bwd(qkv, mixed, d_scaled, lse, lengths, hs, parts, layer, depth, collective_id):
     rows, width3 = qkv.shape
     width = width3 // 3
     pairs = width // 128
@@ -524,13 +566,14 @@
             pltpu.SemaphoreType.DMA((count,)),
             pltpu.SemaphoreType.DMA((count, 3 + depth)),
             pltpu.SemaphoreType.DMA((count, 3 + depth)),
+            pltpu.VMEM((rows // 2, width), BF16),
         ]
         + scatter_scratch([(count, parts[a].shape[5], parts[a].dtype) for a, _, count in pieces], depth),
         compiler_params=pltpu.CompilerParams(
             vmem_limit_bytes=VMEM_CAP, collective_id=collective_id, has_side_effects=True
         ),
         name="attend_bwd",
-    )(ids, hs, qkv, qkv, qkv, mixed, d_scaled, lse, *parts, layer)
+    )(lengths, hs, qkv, qkv, qkv, mixed, d_scaled, lse, *parts, layer)
     return out[:4], out[4:7], out[7]
 
 
@@ -555,17 +598,23 @@
     return pl.BlockSpec(shape, lambda i: (0,) * len(shape), pipeline_mode=pl.Buffered(1))
 
 
-def qkv_kernel(x_ref, w_ref, p_ref, bias_ref, normed_ref, out_ref):
+def qkv_kernel(x_ref, w_ref, p_ref, normed_ref, out_ref):
     hat, _ = row_norm(x_ref[...].astype(F32))
     normed = (hat * p_ref[0:1] + p_ref[1:2]).astype(BF16)
     normed_ref[...] = normed
     cols = out_ref.shape[1]
+    width = x_ref.shape[1]
     for j in range(cols // 512):
         at = slice(j * 512, (j + 1) * 512)
-        out_ref[:, at] = (mm(normed, w_ref[:, at]) + bias_ref[:, at]).astype(BF16)
-
-
-def qkv_project(x, weight, params, bias):
+        part = mm(normed, w_ref[:, at])
+        third, start = j * 512 // width, j * 512 % width
+        if third != 1:
+            row = 2 + third // 2
+            part = part + p_ref[row : row + 1, start : start + 512]
+        out_ref[:, at] = part.astype(BF16)
+
+
+def qkv_project(x, weight, params):
     rows, width = x.shape
     cols = weight.shape[1]
     tile = 256
@@ -576,7 +625,6 @@
             pl.BlockSpec((tile, width), lambda i: (i, 0)),
             resident(weight.shape),
             resident(params.shape),
-            resident(bias.shape),
         ],
         out_specs=[
             pl.BlockSpec((tile, width), lambda i: (i, 0)),
@@ -585,7 +633,7 @@
         out_shape=[jax.ShapeDtypeStruct((rows, width), BF16), jax.ShapeDtypeStruct((rows, cols), BF16)],
         compiler_params=pltpu.CompilerParams(vmem_limit_bytes=VMEM_CAP),
         name="qkv_project",
-    )(x, weight, params, bias)
+    )(x, weight, params)
 
 
 GELU_A = math.sqrt(2.0 / math.pi)
@@ -607,11 +655,11 @@
     ff = w1.shape[1]
     chunks = ff // CHUNK
     ahat, arstd = row_norm(sc_ref[...].astype(F32))
-    post = (ahat * nar[0:1] + nar[1:2]).astype(BF16)
+    post = (ahat * nar[4:5] + nar[5:6]).astype(BF16)
     post_ref[...] = post
-    hidden = x_ref[...].astype(F32) + mm(post, wout[...]) + nar[2:3]
+    hidden = x_ref[...].astype(F32) + mm(post, wout[...]) + nar[6:7]
     hhat, hrstd = row_norm(hidden)
-    fin = (hhat * nar[3:4] + nar[4:5]).astype(BF16)
+    fin = (hhat * nar[7:8] + nar[8:9]).astype(BF16)
     fin_ref[...] = fin
 
     def lanes(values):
@@ -631,7 +679,7 @@
         return total
 
     zero = jnp.zeros((tile, 128), F32)
-    total = lax.fori_loop(0, chunks, inner, zero, unroll=2)
+    total = lax.fori_loop(0, chunks, inner, zero, unroll=8)
     nmean = jnp.sum(total, axis=-1, keepdims=True) / ff
 
     def square(j, total):
@@ -664,8 +712,8 @@
             s2 = s2 + dgn[:, q * 128 : (q + 1) * 128]
         return acc, s1, s2
 
-    acc, s1, s2 = lax.fori_loop(0, chunks, outer, (jnp.zeros((tile, width), F32), zero, zero), unroll=2)
-    lay_ref[...] = (hidden + acc + nar[5:6]).astype(BF16)
+    acc, s1, s2 = lax.fori_loop(0, chunks, outer, (jnp.zeros((tile, width), F32), zero, zero), unroll=8)
+    lay_ref[...] = (hidden + acc + nar[9:10]).astype(BF16)
     s1 = jnp.sum(s1, axis=-1, keepdims=True) / ff
     s2 = jnp.sum(s2, axis=-1, keepdims=True) / ff
 
@@ -677,12 +725,12 @@
         gw_ref[0, :, at] += fold_rows(din.astype(F32))
         return acc + mm(din, w1[:, at], NT)
 
-    dffn = lax.fori_loop(0, chunks, inner_back, jnp.zeros((tile, width), F32), unroll=2)
+    dffn = lax.fori_loop(0, chunks, inner_back, jnp.zeros((tile, width), F32), unroll=8)
     dy = dyl.astype(F32)
     gn_ref[5] += fold_rows(dy)
     gn_ref[3] += fold_rows(dffn * hhat)
     gn_ref[4] += fold_rows(dffn)
-    dhid = dy + row_norm_back(dffn * nar[3:4], hhat, hrstd)
+    dhid = dy + row_norm_back(dffn * nar[7:8], hhat, hrstd)
     dhid_ref[...] = dhid
     gn_ref[2] += fold_rows(dhid)
     dlow = dhid.astype(BF16)
@@ -690,7 +738,7 @@
     dpost = mm(dlow, wout[...], NT)
     gn_ref[0] += fold_rows(dpost * ahat)
     gn_ref[1] += fold_rows(dpost)
-    dsc_ref[...] = row_norm_back(dpost * nar[0:1], ahat, arstd).astype(BF16)
+    dsc_ref[...] = row_norm_back(dpost * nar[4:5], ahat, arstd).astype(BF16)
 
 
 def middle(scaled, x, dy, wout, w1, w2, narrow, wide):
@@ -731,141 +779,292 @@
     )(scaled, x, dy, wout, w1, w2, narrow, wide)
 
 
-def tail_kernel(dq_ref, dk_ref, dv_ref, x_ref, dhid_ref, w_ref, p_ref, out_ref, g_ref):
-    @pl.when(pl.program_id(0) == 0)
+def enter_kernel(depth, pieces, counts, *refs):
+    me = Place(depth)
+    smalls = refs[: len(counts)]
+    shards = [None] + list(refs[len(counts) : len(counts) + 3])
+    tok = refs[len(counts) + 3]
+    wholes = list(refs[len(counts) + 4 : len(counts) + 7])
+    tok_whole, narrow, wide, hs = refs[len(counts) + 7 : len(counts) + 11]
+    small, small_whole, local, send, recv, small_sem, tok_stage = refs[len(counts) + 11 : len(counts) + 18]
+    stages = list(refs[len(counts) + 18 : len(counts) + 22])
+    smalls_here = refs[len(counts) + 22 :]
+    copies = [pltpu.make_async_copy(s, h, small_sem.at[n]) for n, (s, h) in enumerate(zip(smalls, smalls_here))]
+    for copy in copies:
+        copy.start()
+    for copy in copies:
+        copy.wait()
+    shards[0] = small
+    wholes = [small_whole] + wholes
+    rows = []
+    for ref, count in zip(smalls_here, counts):
+        row = ref[...].astype(F32).reshape(1, count)
+        rows.append(row if count == 128 else jnp.concatenate([row, jnp.zeros((1, 128 - count), F32)], axis=1))
+    rows.append(jnp.zeros((16 - len(counts), 128), F32))
+    small[...] = jnp.concatenate(rows, axis=0).astype(BF16)
+    gathers = [
+        Gather(me, shards[a], stages[a], wholes[a], at, count, local.at[n], send.at[n], recv.at[n])
+        for n, (a, at, count) in enumerate(pieces)
+    ]
+    first, later, begun = gathers[:3], gathers[3], gathers[4:]
+    half = tok.shape[1]
+    cut = half * 3 // 8
+    swaps = []
+    for n, (at, count) in enumerate(((0, cut), (cut, half - cut))):
+        span = pl.ds(at, count)
+        n = len(pieces) + n
+        swaps.append(
+            Swap(
+                me, tok.at[1 - me.y, span], lambda y, span=span: tok_whole.at[y, span], tok.at[me.y, span],
+                tok_stage.at[span], tok_whole.at[me.y, span], local.at[n], send.at[n, 0], recv.at[n, 0],
+            )
+        )
+    for g in gathers + swaps:
+        g.ready()
+    me.greet()
+    swaps[0].begin()
+    for g in first:
+        g.begin()
+    for g in first:
+        g.spread()
+    swaps[1].begin()
+    for g in [later] + begun:
+        g.begin()
+    for g in first:
+        g.from_y()
+    later.spread()
+    for g in first:
+        g.from_x()
+    for g in first:
+        g.from_corner()
+    first[0].end()
+    part = counts[0]
+    each = 128 // part
+    for d in range(depth * 8 // each):
+        tiles = []
+        for k in range(d * each, (d + 1) * each):
+            tile = small_whole[k // 8, k // 4 % 2, k // 2 % 2, k % 2].astype(F32)
+            tiles.append(tile[:, 0:part])
+            wide[0:3, k * 128 : (k + 1) * 128] = tile[10:13]
+        narrow[:, d * 128 : (d + 1) * 128] = jnp.concatenate(tiles, axis=1)
+    hs[...] = jnp.concatenate(
+        [small_whole[0, 0, 0, y].astype(F32)[13:14, 0 : counts[13]] for y in range(2)], axis=1
+    )
+    later.from_y()
+    later.from_x()
+    later.from_corner()
+    for g in begun:
+        g.landed()
+    for g in first[1:]:
+        g.end()
+    later.end()
+    for swap in swaps:
+        swap.end()
+
+
+def enter(smalls, qkv_weight, out_weight, fc1_weight, tokens, depth, collective_id):
+    shards = [qkv_weight, out_weight, fc1_weight]
+    counts = [s.shape[0] for s in smalls]
+    pieces = [(0, 0, 16)]
+    for a in (1, 2, 3):
+        rows = shards[a - 1].shape[0]
+        pieces += [(a, 0, rows)] if a == 2 else [(a, 0, rows // 2), (a, rows // 2, rows // 2)]
+    count = len(pieces) + 2
+    anywhere = pl.BlockSpec(memory_space=pl.ANY)
+    vmem = pl.BlockSpec(memory_space=pltpu.VMEM)
+    out = pl.pallas_call(
+        functools.partial(enter_kernel, depth, pieces, counts),
+        in_specs=[anywhere] * (len(counts) + 4),
+        out_specs=[anywhere] * 4 + [vmem] * 3,
+        out_shape=[jax.ShapeDtypeStruct((depth, 2, 2, 2) + s.shape, s.dtype) for s in shards]
+        + [
+            jax.ShapeDtypeStruct(tokens.shape, tokens.dtype),
+            jax.ShapeDtypeStruct((16, depth * 8 * counts[0]), F32),
+            jax.ShapeDtypeStruct((8, depth * 8 * counts[10]), F32),
+            jax.ShapeDtypeStruct((1, 2 * counts[13]), F32),
+        ],
+        scratch_shapes=[
+            pltpu.VMEM((16, 128), BF16),
+            pltpu.VMEM((depth, 2, 2, 2, 16, 128), BF16),
+            pltpu.SemaphoreType.DMA((count,)),
+            pltpu.SemaphoreType.DMA((count, 6 + depth)),
+            pltpu.SemaphoreType.DMA((count, 6 + depth)),
+            pltpu.SemaphoreType.DMA((len(counts),)),
+            pltpu.VMEM(tokens.shape[1:], tokens.dtype),
+        ]
+        + [pltpu.VMEM((16, 128), BF16)]
+        + [pltpu.VMEM(s.shape, s.dtype) for s in shards]
+        + [pltpu.VMEM((n,), BF16) for n in counts],
+        compiler_params=pltpu.CompilerParams(
+            collective_id=collective_id, has_side_effects=True, vmem_limit_bytes=VMEM_CAP
+        ),
+        name="enter",
+    )(*smalls, *shards, tokens)
+    return flat(out[0]), flat(out[1]), out[2], out[3].reshape(-1, tokens.shape[2]), out[4], out[5], out[6]
+
+
+def flat(whole):
+    return whole.reshape((-1,) + whole.shape[5:])
+
+
+def leave_kernel(depth, part, heads, *refs):
+    dq_ref, dk_ref, dv_ref, x_ref, dhid_ref, w_ref, p_ref = refs[:7]
+    parts = refs[7:10]
+    thin_ref, fat_ref, delta_ref, hs_ref = refs[10:14]
+    out, qkv_sum, small_sum = refs[14:17]
+    local, send, recv, go, come, store, g_acc, thin, fat, small, leaving, landing, stage = refs[17:30]
+    scratch = refs[30:]
+    me = Place(depth)
+    step = pl.program_id(0)
+    half_tiles = leaving.shape[0]
+    tile, width = x_ref.shape
+    rows = parts[0].shape[4]
+    scatters = [
+        Scatter(
+            me, parts[n], 0, rows, *scratch[4 * n : 4 * n + 4], local.at[n], send.at[n], recv.at[n],
+            qkv_sum.at[:, pl.ds(n * width, width)],
+        )
+        for n in range(3)
+    ]
+    smalls = Scatter(me, small, 0, 16, *scratch[12:16], local.at[3], send.at[3], recv.at[3], small_sum)
+
+    def trade(j):
+        return remote(leaving.at[j], landing.at[j], go.at[j], come.at[j], me.next_y)
+
+    def put(y, j):
+        return pltpu.make_async_copy(stage.at[j], out.at[y, pl.ds(j * tile, tile)], store.at[j])
+
+    @pl.when(step == 0)
     def _():
-        g_ref[...] = jnp.zeros_like(g_ref)
-
-    width = x_ref.shape[1]
+        g_acc[...] = jnp.zeros_like(g_acc)
+        me.greet()
+        for s in scatters:
+            s.begin()
+
+    @pl.when(step == 2)
+    def _():
+        for s in scatters:
+            s.across()
+
     hat, rstd = row_norm(x_ref[...].astype(F32))
     dnormed = mm(dq_ref[...], w_ref[:, 0:width], NT)
     dnormed = dnormed + mm(dk_ref[...], w_ref[:, width : 2 * width], NT)
     dnormed = dnormed + mm(dv_ref[...], w_ref[:, 2 * width : 3 * width], NT)
-    g_ref[0] += fold_rows(dnormed * hat)
-    g_ref[1] += fold_rows(dnormed)
-    g_ref[2] += fold_rows(dq_ref[...].astype(F32))
-    g_ref[3] += fold_rows(dv_ref[...].astype(F32))
-    out_ref[...] = dhid_ref[...] + row_norm_back(dnormed * p_ref[0:1], hat, rstd)
-
-
-def tail(dq, dk, dv, x, dhid, weight, params):
+    g_acc[0] += fold_rows(dnormed * hat)
+    g_acc[1] += fold_rows(dnormed)
+    g_acc[2] += fold_rows(dq_ref[...].astype(F32))
+    g_acc[3] += fold_rows(dv_ref[...].astype(F32))
+    grad = dhid_ref[...] + row_norm_back(dnormed * p_ref[0:1], hat, rstd)
+
+    @pl.when(step < half_tiles)
+    def _():
+        leaving[step] = grad.astype(BF16)
+        trade(step).start()
+
+    @pl.when(step >= half_tiles)
+    def _():
+        stage[step - half_tiles] = grad
+        put(me.y, step - half_tiles).start()
+
+    @pl.when(step == pl.num_programs(0) - 1)
+    def _():
+        thin[...] = jnp.zeros_like(thin)
+        fat[...] = jnp.zeros_like(fat)
+        for k in range(4):
+            thin[k : k + 1, :] = jnp.sum(g_acc[k], axis=0, keepdims=True)
+        for k in range(6):
+            thin[4 + k : 5 + k, :] = jnp.sum(thin_ref[k], axis=0, keepdims=True)
+        for k in range(3):
+            fat[10 + k : 11 + k, :] = jnp.sum(fat_ref[k], axis=0, keepdims=True)
+        lanes = lax.broadcasted_iota(jnp.int32, (1, 128), 1)
+        scale = jnp.zeros((1, 128), F32)
+        for p in range(delta_ref.shape[0]):
+            for h in range(2):
+                scale = jnp.where(lanes == 2 * p + h, jnp.sum(delta_ref[p, h]), scale)
+        scale = scale / jnp.concatenate([hs_ref[...], jnp.ones((1, 128 - 2 * heads), F32)], axis=1)
+        each = 128 // part
+        is_scale = lax.broadcasted_iota(jnp.int32, (16, 128), 0) == 13
+        for d in range(depth * 8):
+            block = thin[:, d // each * 128 : (d // each + 1) * 128]
+            turn = d % each * part
+            block = pltpu.roll(block, 128 - turn, 1) if turn else block
+            block = block + fat[:, d * 128 : (d + 1) * 128]
+            row = pltpu.roll(scale, 128 - heads, 1) if d % 2 else scale
+            small[d // 8, d // 4 % 2, d // 2 % 2, d % 2] = jnp.where(is_scale, row, block)
+        smalls.begin()
+        v, k, q = scatters[2], scatters[1], scatters[0]
+        v.along_x()
+        smalls.across()
+        k.along_x()
+        v.along_y()
+        smalls.along_x()
+        q.along_x()
+        k.along_y()
+        smalls.along_y()
+        v.end()
+        q.along_y()
+        for j in range(half_tiles):
+            trade(j).wait()
+            put(me.y, j).wait()
+            stage[j] = landing[j].astype(F32)
+            put(1 - me.y, j).start()
+        k.end()
+        smalls.end()
+        q.end()
+        for j in range(half_tiles):
+            put(1 - me.y, j).wait()
+
+
+def leave(dq, dk, dv, x, dhid, weight, params, parts, thin, fat, delta, hs, depth, collective_id):
     rows, width = x.shape
     tile = 256
-    thin = pl.BlockSpec((tile, width), lambda i: (i, 0))
+    tiles = rows // tile
+    parts = [shard_view(p, depth) for p in parts]
+    part = width // (depth * 8)
+    heads = hs.shape[1] // 2
+
+    def at(i):
+        return ((i + tiles // 2 * (1 - lax.axis_index("sp"))) % tiles, 0)
+
+    block = pl.BlockSpec((tile, width), at)
+    anywhere = pl.BlockSpec(memory_space=pl.ANY)
+    pieces = [(p.shape[4], p.shape[5], p.dtype) for p in parts] + [(16, 128, F32)]
+    keep = lambda shape: pl.BlockSpec(shape, lambda i: (0,) * len(shape))
+    out_shape = [
+        jax.ShapeDtypeStruct((2, rows // 2, width), F32),
+        jax.ShapeDtypeStruct((parts[0].shape[4], 3 * width), F32),
+        jax.ShapeDtypeStruct((16, 128), F32),
+    ]
     return pl.pallas_call(
-        tail_kernel,
-        grid=(rows // tile,),
-        in_specs=[thin] * 5 + [resident(weight.shape), resident(params.shape)],
-        out_specs=[thin, pl.BlockSpec((4, 8, width), lambda i: (0, 0, 0))],
-        out_shape=[jax.ShapeDtypeStruct((rows, width), F32), jax.ShapeDtypeStruct((4, 8, width), F32)],
-        compiler_params=pltpu.CompilerParams(vmem_limit_bytes=VMEM_CAP),
-        name="tail",
-    )(dq, dk, dv, x, dhid, weight, params)
-
-
-def enter_kernel(depth, pieces, *refs):
-    shards = refs[:2]
-    tok = refs[2]
-    wholes = refs[3:5]
-    tok_whole = refs[5]
-    local, send, recv = refs[6:]
-    me = Place(depth)
-    gathers = [
-        Gather(me, shards[a], wholes[a], at, count, local.at[n], send.at[n], recv.at[n])
-        for n, (a, at, count) in enumerate(pieces)
-    ]
-    n = len(pieces)
-    swap = Swap(
-        me, tok.at[1 - me.y], lambda y: tok_whole.at[y], tok.at[me.y], tok_whole.at[me.y],
-        local.at[n], send.at[n, 0], recv.at[n, 0],
-    )
-    me.greet()
-    for g in gathers:
-        g.begin()
-    for g in gathers:
-        g.spread()
-    swap.begin()
-    for g in gathers:
-        g.from_y()
-        g.from_x()
-    for g in gathers:
-        g.from_corner()
-    for g in gathers:
-        g.end()
-    swap.end()
-
-
-def enter(small, qkv_weight, tokens, depth, collective_id):
-    shards = [small, qkv_weight]
-    part = qkv_weight.shape[0] // 2
-    pieces = [(0, 0, small.shape[0]), (1, 0, part), (1, part, part)]
-    count = len(pieces) + 1
-    anywhere = pl.BlockSpec(memory_space=pl.ANY)
-    out = pl.pallas_call(
-        functools.partial(enter_kernel, depth, pieces),
-        in_specs=[anywhere] * 3,
-        out_specs=[anywhere] * 3,
-        out_shape=[jax.ShapeDtypeStruct((depth, 2, 2, 2) + s.shape, s.dtype) for s in shards]
-        + [jax.ShapeDtypeStruct(tokens.shape, tokens.dtype)],
+        functools.partial(leave_kernel, depth, part, heads),
+        grid=(tiles,),
+        in_specs=[block] * 5
+        + [resident(weight.shape), resident(params.shape)]
+        + [anywhere] * 3
+        + [resident(a.shape) for a in (thin, fat, delta, hs)],
+        out_specs=[anywhere, keep(out_shape[1].shape), keep(out_shape[2].shape)],
+        out_shape=out_shape,
         scratch_shapes=[
-            pltpu.SemaphoreType.DMA((count,)),
-            pltpu.SemaphoreType.DMA((count, 6 + depth)),
-            pltpu.SemaphoreType.DMA((count, 6 + depth)),
-        ],
-        compiler_params=pltpu.CompilerParams(
-            collective_id=collective_id, has_side_effects=True, vmem_limit_bytes=1024 * 1024
-        ),
-        name="enter",
-    )(small, qkv_weight, tokens)
-    wholes = [w.reshape((depth * 8 * w.shape[4],) + w.shape[5:]) for w in out[:2]]
-    return wholes[0], wholes[1], out[2].reshape(-1, tokens.shape[2])
-
-
-def leave_kernel(depth, pieces, *refs):
-    arrays = len(pieces)
-    parts, sums = refs[:arrays], refs[arrays : 2 * arrays]
-    local, send, recv = refs[2 * arrays : 2 * arrays + 3]
-    scratch = refs[2 * arrays + 3 :]
-    me = Place(depth)
-    scatters = [
-        Scatter(me, parts[n], 0, piece[0], *scratch[4 * n : 4 * n + 4], local.at[n], send.at[n], recv.at[n], sums[n])
-        for n, piece in enumerate(pieces)
-    ]
-    me.greet()
-    for s in scatters:
-        s.begin()
-    for s in scatters:
-        s.across()
-    for s in scatters:
-        s.along_x()
-    for s in scatters:
-        s.along_y()
-    for s in scatters:
-        s.end()
-
-
-def leave(parts, depth, collective_id):
-    parts = [shard_view(p, depth) for p in parts]
-    pieces = [(p.shape[4], p.shape[5], p.dtype) for p in parts]
-    count = len(parts)
-    anywhere = pl.BlockSpec(memory_space=pl.ANY)
-    vmem = pl.BlockSpec(memory_space=pltpu.VMEM)
-    return pl.pallas_call(
-        functools.partial(leave_kernel, depth, pieces),
-        in_specs=[anywhere] * count,
-        out_specs=[vmem] * count,
-        out_shape=[jax.ShapeDtypeStruct(p.shape[4:], F32) for p in parts],
-        scratch_shapes=[
-            pltpu.SemaphoreType.DMA((count,)),
-            pltpu.SemaphoreType.DMA((count, 3 + depth)),
-            pltpu.SemaphoreType.DMA((count, 3 + depth)),
+            pltpu.SemaphoreType.DMA((4,)),
+            pltpu.SemaphoreType.DMA((4, 3 + depth)),
+            pltpu.SemaphoreType.DMA((4, 3 + depth)),
+            pltpu.SemaphoreType.DMA((tiles // 2,)),
+            pltpu.SemaphoreType.DMA((tiles // 2,)),
+            pltpu.SemaphoreType.DMA((tiles // 2,)),
+            pltpu.VMEM((4, 8, width), F32),
+            pltpu.VMEM((16, width), F32),
+            pltpu.VMEM((16, fat.shape[2]), F32),
+            pltpu.VMEM((depth, 2, 2, 2, 16, 128), F32),
+            pltpu.VMEM((tiles // 2, tile, width), BF16),
+            pltpu.VMEM((tiles // 2, tile, width), BF16),
+            pltpu.VMEM((tiles // 2, tile, width), F32),
         ]
         + scatter_scratch(pieces, depth),
         compiler_params=pltpu.CompilerParams(
             collective_id=collective_id, has_side_effects=True, vmem_limit_bytes=VMEM_CAP
         ),
         name="leave",
-    )(*parts)
+    )(dq, dk, dv, x, dhid, weight, params, *parts, thin, fat, delta, hs)
 
 
 def fast_shards(
@@ -878,40 +1077,20 @@
     half = tokens.shape[1]
     rows = 2 * half
     width = tokens.shape[2]
-    ff = fc1_weight.shape[1]
     me = lax.axis_index("sp")
-    swap = [(0, 1), (1, 0)]
 
     narrow_in = [in_gain, in_bias, q_bias, v_bias, attn_gain, attn_bias, out_bias, ffn_gain, ffn_bias, fc2_bias]
     wide_in = [fc1_bias, mid_gain, mid_bias]
     part = width // devices
-    wide_part = ff // devices
-    small = jnp.concatenate(narrow_in + wide_in + [head_scale])
-    used = small.shape[0]
-    small_rows = 16
-    small = jnp.pad(small, (0, small_rows * 128 - used)).reshape(small_rows, 128)
-    small, wqkv, x = enter(small, qkv_weight, tokens, depth, 0)
-    small = small.reshape(devices, small_rows * 128).astype(F32)
-    nn = len(narrow_in)
-    narrow = small[:, : nn * part].reshape(devices, nn, part).transpose(1, 0, 2).reshape(nn, width)
-    base = nn * part
-    wide = small[:, base : base + 3 * wide_part].reshape(devices, 3, wide_part).transpose(1, 0, 2).reshape(3, ff)
-    base = base + 3 * wide_part
     heads_each = head_scale.shape[0]
-    hs = small[0:2, base : base + heads_each].reshape(2 * heads_each)
-
-    lengths = lax.dynamic_index_in_dim(doc_lengths[0], me, 0, keepdims=False)
-    starts = jnp.arange(rows // BLOCK, dtype=jnp.int32) * BLOCK
-    ids = jnp.sum((starts[:, None] >= jnp.cumsum(lengths)[None, :]).astype(jnp.int32), axis=1)
-
-    in_params = narrow[0:2]
-    bias_row = jnp.concatenate([narrow[2], jnp.zeros_like(narrow[2]), narrow[3]])[None, :]
-    normed, qkv = qkv_project(x, wqkv, in_params, bias_row)
-    scaled, mixed, lse, (wout, w1, w2), dy = attend_fwd(
-        qkv, ids, hs, [out_weight, fc1_weight, fc2_weight], out_cotangent, depth, 1
+    wqkv, wout, begun, x, narrow, wide, hs = enter(
+        narrow_in + wide_in + [head_scale], qkv_weight, out_weight, fc1_weight, tokens, depth, 0
     )
+    normed, qkv = qkv_project(x, wqkv, narrow)
+    scaled, mixed, lse, w1, w2, dy = attend_fwd(qkv, doc_lengths, hs, begun, fc2_weight, out_cotangent, depth, 1)
+    w1, w2 = flat(w1), flat(w2)
     layer, post, ffn_in, active, d_inner, d_hidden, d_low, d_scaled, grads_narrow, grads_wide = middle(
-        scaled, x, dy, wout, w1, w2, narrow[4:10], wide
+        scaled, x, dy, wout, w1, w2, narrow, wide
     )
 
     def weight_grad(left, right):
@@ -921,40 +1100,20 @@
     g_fc1 = weight_grad(ffn_in, d_inner)
     g_out = weight_grad(post, d_low)
     (dq, dk, dv, delta), (s_fc2, s_fc1, s_out), layer_out = attend_bwd(
-        qkv, mixed, d_scaled, lse, ids, hs, [g_fc2, g_fc1, g_out], layer, depth, 2
+        qkv, mixed, d_scaled, lse, doc_lengths, hs, [g_fc2, g_fc1, g_out], layer, depth, 2
     )
     g_q = weight_grad(normed, dq)
     g_k = weight_grad(normed, dk)
     g_v = weight_grad(normed, dv)
-    d_input, grads_in = tail(dq, dk, dv, x, d_hidden, wqkv, in_params)
-    d_sent = lax.dynamic_slice_in_dim(d_input, (1 - me) * half, half, 0).astype(BF16)
-    d_got = lax.ppermute(d_sent, "sp", swap).astype(F32)
-    d_kept = lax.dynamic_slice_in_dim(d_input, me * half, half, 0)
-    input_grad = jnp.stack([jnp.where(me == 0, d_kept, d_got), jnp.where(me == 0, d_got, d_kept)])
-
-    hs_grad = jnp.sum(delta, axis=(2, 3)).reshape(-1) / hs
-    narrow_grads = jnp.concatenate([jnp.sum(grads_in, axis=1), jnp.sum(grads_narrow, axis=1)], axis=0)
-    wide_grads = jnp.sum(grads_wide, axis=1)
-    packed = jnp.concatenate(
-        [
-            narrow_grads.reshape(nn, devices, part).transpose(1, 0, 2).reshape(devices, nn * part),
-            wide_grads.reshape(3, devices, wide_part).transpose(1, 0, 2).reshape(devices, 3 * wide_part),
-            jnp.tile(hs_grad.reshape(2, heads_each), (devices // 2, 1)),
-        ],
-        axis=1,
+    input_grad, s_qkv, s_small = leave(
+        dq, dk, dv, x, d_hidden, wqkv, narrow, [g_q, g_k, g_v], grads_narrow, grads_wide, delta, hs, depth, 3
     )
-    tiles = (used + 1023) // 1024 * 8
-    packed = jnp.pad(packed, ((0, 0), (0, tiles * 128 - used))).reshape(devices * tiles, 128)
-    s_q, s_k, s_v, s_small = leave([g_q, g_k, g_v, packed], depth, 3)
-    s_small = s_small.reshape(-1)
-    nar = [s_small[k * part : (k + 1) * part] for k in range(nn)]
-    base = nn * part
-    wid = [s_small[base + k * wide_part : base + (k + 1) * wide_part] for k in range(3)]
-    base = base + 3 * wide_part
-    s_hs = s_small[base : base + heads_each]
+    nar = [s_small[k, :part] for k in range(10)]
+    wid = [s_small[10 + k] for k in range(3)]
+    s_hs = s_small[13, :heads_each]
     return (
-        layer_out, input_grad, nar[0], nar[1], jnp.concatenate([s_q, s_k, s_v], axis=1), nar[2], nar[3], s_hs,
-        nar[4], nar[5], s_out, nar[6], nar[7], nar[8], s_fc1, wid[0], wid[1], wid[2], s_fc2, nar[9],
+        layer_out, input_grad, nar[0], nar[1], s_qkv, nar[2], nar[3], s_hs, nar[4], nar[5], s_out, nar[6], nar[7],
+        nar[8], s_fc1, wid[0], wid[1], wid[2], s_fc2, nar[9],
     )
 
 
@@ -1393,8 +1552,27 @@
     )
 
 
+def fits(args):
+    dp, sp = lax.axis_size("dp"), lax.axis_size("sp")
+    tokens, lengths, in_gain, fc1_bias = args[0], args[1], args[3], args[16]
+    return (
+        sp == 2
+        and tokens.shape[0] == 2
+        and dp % 4 == 0
+        and dp >= 8
+        and 2 * tokens.shape[1] == LONGEST
+        and lengths.shape[2] * BLOCK == LONGEST
+        and 128 % in_gain.shape[0] == 0
+        and fc1_bias.shape[0] == 128
+        and tokens.shape[2] == 128 * args[8].shape[0]
+    )
+
+
+def body(*args):
+    return fast_shards(*args) if fits(args) else shards(*args)
+
+
 def solution(mesh):
-    body = fast_shards if mesh.shape["sp"] == 2 and mesh.shape["dp"] % 4 == 0 and mesh.shape["dp"] >= 8 else shards
     return jax.shard_map(
         body,
         mesh=mesh,

time: 844 us -> 693 us (0.82)
  Pallas kernels: 713 us -> 593 us
  local copies, waits for them, and re-layouts: 33.2 us -> 16.6 us
  other arithmetic: 12.1 us -> 0.01 us
    pallas_call x1, Pallas kernels: 192 us -> 142 us  [attend_bwd(): pl.pallas_call(functools.partial(attend_bwd_kernel, depth, pieces), grid=...]
    pallas_call x1, Pallas kernels: 162 us -> 113 us  [attend_fwd(): pl.pallas_call(functools.partial(attend_fwd_kernel, depth, pieces), grid=...]
    pallas_call x1, Pallas kernels: 173 us -> 149 us  [middle(): pl.pallas_call(middle_kernel, grid=(rows // tile,), in_specs=[thin, thin,...]
    concatenate x1 -> x0, local copies, waits for them, and re-layouts: 9.43 us -> none  [fast_shards(): small = jnp.concatenate(narrow_in + wide_in + [head_scale])]
    another operation x3 -> x0, other arithmetic: 8.44 us -> none  [the longest x2 8.26 us: fast_shards(): jnp.stack([jnp.where(me == 0, d_kept, d_got), jnp.where(me == 0, d_got, d...]
    pallas_call x3 -> x2, Pallas kernels: 166 us -> 168 us  [the longest x1 87 us: enter(): pl.pallas_call(functools.partial(enter_kernel, depth, pieces, counts), in...]
  transfers between devices with their start and end apart: 1 -> 0, of which waited for: 0 -> 0; matrix products, arithmetic and copies ran while one was open for 4% -> 0% of each run, Pallas kernels for 7% -> 0%
where the time goes in v2:
time: 693 us; the launch traced here: 684 us
  Pallas kernels  593 us (86%)
  matrix products  73.3 us (11%)
  local copies, waits for them, and re-layouts  16.6 us (2%)
    pallas_call x1, Pallas kernels, middle(): pl.pallas_call(middle_kernel, grid=(rows // tile,), in_specs=[thin, thin,...  149 us
    pallas_call x1, Pallas kernels, attend_bwd(): pl.pallas_call(functools.partial(attend_bwd_kernel, depth, pieces), grid=...  142 us
    pallas_call x1, Pallas kernels, attend_fwd(): pl.pallas_call(functools.partial(attend_fwd_kernel, depth, pieces), grid=...  113 us
    pallas_call x1, Pallas kernels, enter(): pl.pallas_call(functools.partial(enter_kernel, depth, pieces, counts), in...  87 us
    pallas_call x1, Pallas kernels, leave(): pl.pallas_call(functools.partial(leave_kernel, depth, part, heads), grid=...  80.8 us
    dot_general x6, matrix products, weight_grad(): jnp.einsum('ti,tj->ij', left, right, preferred_element_type=F32)  73.3 us
    pallas_call x1, Pallas kernels, qkv_project(): pl.pallas_call(qkv_kernel, grid=(rows // tile,), in_specs=[pl.BlockSpec((...  21 us

profile of v2, /device:TPU:0, one launch (start us, length us, event | category | flops | bytes accessed | tf_op | source)
XLA Modules:
  0.0 683.9 jit_solution(623369753955106608)
XLA Ops:
  0.7 87.0 %enter.1 = (bf16[4,2,2,2,32,3072]{5,4,3,2,1,0:T(8,128)(2,1)}, bf16[4,2,2,2,32,1024]{5,4,3,2,1,0:T(8,128)(2,1)}, bf16[4,2,2,2,32,4096]{5,4,3,2,1,0:T(8,128)(2,1)}...) custom-call(bf16[32]{0:T(256)(128)(2,1)} %refs_0_.3, ...), custom_call_target="tpu_custom_call" | custom-call | tf_op jit(solution)/shard_map/enter/pallas_call | solution.py:875
  87.7 21.0 %qkv_project.1 = (bf16[2048,1024]{1,0:T(8,128)(2,1)}, bf16[2048,3072]{1,0:T(8,128)(2,1)}) custom-call(bf16[2048,1024]{1,0:T(8,128)(2,1)} %bitcast.52, bf16[1024,3072]{1,0:T(8,128)(2,1)} %bitcast.56, f32[16,1024]{1,0:T(8,128)} %get-tuple-element.59.p_ref.nar.refs_6_), custom_call_target="tpu_custom_call" | custom-call | tf_op jit(solution)/shard_map/qkv_project/pallas_call | solution.py:621
  108.6 113.2 %attend_fwd.1 = (bf16[2048,1024]{1,0:T(8,128)(2,1)}, f32[2048,1024]{1,0:T(8,128)}, f32[8,2,4,512]{3,2,1,0:T(4,128)}, bf16[4,2,2,2,32,4096]{5,4,3,2,1,0:T(8,128)(...) custom-call(s32[1,2,4]{2,1,0:T(2,128)} %refs_0_.5, ...), custom_call_target="tpu_custom_call", output_to_operand_aliasing={{3}: (5, {})} | custom-call | tf_op jit(solution)/shard_map/attend_fwd/pallas_call | solution.py:387
  221.9 149.1 %middle.1 = (bf16[2048,1024]{1,0:T(8,128)(2,1)}, bf16[2048,1024]{1,0:T(8,128)(2,1)}, bf16[2048,1024]{1,0:T(8,128)(2,1)}, bf16[2048,4096]{1,0:T(8,128)(2,1)}, bf1...) custom-call(bf16[2048,1024]{1,0:T(8,128)(2,1)} %get-tuple-element.63, ...), custom_call_target="tpu_custom_call" | custom-call | tf_op jit(solution)/shard_map/middle/pallas_call | solution.py:751
  371.0 0.0 slice-start
  371.0 9.5 %convolution_convert_fusion.5 = bf16[1024,1024]{1,0:T(8,128)(2,1)} fusion(bf16[2048,1024]{1,0:T(8,128)(2,1)} %get-tuple-element.74, bf16[2048,1024]{1,0:T(8,128)(2,1)} %get-tuple-element.75), kind=kOutput, calls=%fused_computation.5 | convolution fusion | flops 4296015872 | bytes 10485760 | tf_op jit(solution)/shard_map/ti,tj->ij/dot_general | solution.py:1097
  380.6 22.9 %convolution_convert_fusion.1 = bf16[4096,1024]{1,0:T(8,128)(2,1)} fusion(bf16[2048,4096]{1,0:T(8,128)(2,1)} %get-tuple-element.71, bf16[2048,1024]{1,0:T(8,128)(2,1)S(1)} %bitcast.62), kind=kOutput, calls=%fused_computation.1 | convolution fusion | flops 17184063488 | bytes 29360128 | tf_op jit(solution)/shard_map/ti,tj->ij/dot_general | solution.py:1097
  403.5 19.8 %convolution_convert_fusion = bf16[1024,4096]{1,0:T(8,128)(2,1)} fusion(bf16[2048,1024]{1,0:T(8,128)(2,1)S(1)} %copy-done.9, bf16[2048,4096]{1,0:T(8,128)(2,1)S(1)} %bitcast.69), kind=kOutput, calls=%fused_computation | convolution fusion | flops 17184063488 | bytes 29360128 | tf_op jit(solution)/shard_map/ti,tj->ij/dot_general | solution.py:1097
  423.3 142.0 %attend_bwd.1 = (bf16[2048,1024]{1,0:T(8,128)(2,1)}, bf16[2048,1024]{1,0:T(8,128)(2,1)}, bf16[2048,1024]{1,0:T(8,128)(2,1)}, f32[8,2,4,512]{3,2,1,0:T(4,128)}, f...) custom-call(s32[1,2,4]{2,1,0:T(2,128)} %refs_0_.5, ...), custom_call_target="tpu_custom_call" | custom-call | tf_op jit(solution)/shard_map/attend_bwd/pallas_call | solution.py:551
  565.3 0.0 copy-start.8
  565.3 9.5 %convolution_convert_fusion.4 = bf16[1024,1024]{1,0:T(8,128)(2,1)} fusion(bf16[2048,1024]{1,0:T(8,128)(2,1)} %get-tuple-element.82, bf16[2048,1024]{1,0:T(8,128)(2,1)} %get-tuple-element.78.refs_0_), kind=kOutput, calls=%fused_computation.4 | convolution fusion | flops 4296015872 | bytes 10485760 | tf_op jit(solution)/shard_map/ti,tj->ij/dot_general | solution.py:1097
  574.8 5.8 convolution_convert_fusion.3
  580.6 5.8 convolution_convert_fusion.2
  586.3 80.8 %leave.1 = (f32[2,1024,1024]{2,1,0:T(8,128)}, f32[32,3072]{1,0:T(8,128)}, f32[16,128]{1,0:T(8,128)}) custom-call(bf16[2048,1024]{1,0:T(8,128)(2,1)} %get-tuple-element.78.refs_0_, bf16[2048,1024]{1,0:T(8,128)(2,1)} %get-tuple-element.79.refs_1_, bf16[2048,1024]{1,0:T(8,128)(2,1)} %get-tuple-element.80.refs_2_, bf16[2048,1024]{1,0:T(8,128)(2,1)} %bitcast.54, ...), custom_call_target="tpu_custom_call" | custom-call | tf_op jit(solution)/shard_map/leave/pallas_call | solution.py:1038
  667.2 1.2 slice_bitcast_fusion.9
  668.3 1.3 slice_bitcast_fusion.1
  669.6 1.5 slice_bitcast_fusion
  671.2 4.9 copy.49
  676.1 1.2 copy-done
  677.3 3.4 copy.50
  680.7 0.7 copy.51
  681.5 0.7 copy.52
  682.2 0.8 copy.53
  683.0 0.8 copy.54
  (26 shorter events, 0.0 us)
Async XLA Ops:
  371.0 9.6 %copy-start.3 = (bf16[2,1024,1024]{2,1,0:T(8,128)(2,1)S(1)}, bf16[2,1024,1024]{2,1,0:T(8,128)(2,1)}, u32[]{:S(2)}) copy-start(bf16[2,1024,1024]{2,1,0:T(8,128)(2,1)} %get-tuple-element.64) | copy-start | bytes 12582916
  371.0 32.5 %slice-start = ((s8[16777216]{0:T(1024)(128)(4,1)}), s8[4194304]{0:T(1024)(128)(4,1)S(1)}, s32[]{:S(2)}) async-start(s8[16777216]{0:T(1024)(128)(4,1)} %bitcast.68), calls=%async_computation | async-start | bytes 8388608
  380.5 22.9 %slice-start.1 = ((s8[16777216]{0:T(1024)(128)(4,1)}), s8[4194304]{0:T(1024)(128)(4,1)S(1)}, s32[]{:S(2)}) async-start(s8[16777216]{0:T(1024)(128)(4,1)} %bitcast.68), calls=%async_computation.1 | async-start | bytes 8388608
  380.5 22.9 %slice-start.2 = ((s8[16777216]{0:T(1024)(128)(4,1)}), s8[4194304]{0:T(1024)(128)(4,1)S(1)}, s32[]{:S(2)}) async-start(s8[16777216]{0:T(1024)(128)(4,1)} %bitcast.68), calls=%async_computation.2 | async-start | bytes 8388608
  380.5 22.9 %slice-start.3 = ((s8[16777216]{0:T(1024)(128)(4,1)}), s8[4194304]{0:T(1024)(128)(4,1)S(1)}, s32[]{:S(2)}) async-start(s8[16777216]{0:T(1024)(128)(4,1)} %bitcast.68), calls=%async_computation.3 | async-start | bytes 8388608
  380.6 22.9 %copy-start.9 = (bf16[2048,1024]{1,0:T(8,128)(2,1)S(1)}, bf16[2048,1024]{1,0:T(8,128)(2,1)}, u32[]{:S(2)}) copy-start(bf16[2048,1024]{1,0:T(8,128)(2,1)} %get-tuple-element.72) | copy-start | bytes 12582916
  565.3 9.5 %copy-start.1 = (bf16[2048,1024]{1,0:T(8,128)(2,1)S(1)}, bf16[2048,1024]{1,0:T(8,128)(2,1)}, u32[]{:S(2)}) copy-start(bf16[2048,1024]{1,0:T(8,128)(2,1)} %get-tuple-element.79.refs_1_) | copy-start | bytes 12582916
  565.3 9.5 %copy-start.8 = (bf16[2048,1024]{1,0:T(8,128)(2,1)S(1)}, bf16[2048,1024]{1,0:T(8,128)(2,1)}, u32[]{:S(2)}) copy-start(bf16[2048,1024]{1,0:T(8,128)(2,1)} %get-tuple-element.82) | copy-start | bytes 12582916
  574.8 5.8 copy-start.2
  671.2 6.2 copy-start
  677.3 3.4 copy-start.6
  677.3 4.2 copy-start.7
  677.3 4.8 copy-start.5
  677.3 5.6 copy-start.4

commit v3 on v2

--- a/solution.py
+++ b/solution.py
@@ -150,6 +150,91 @@
             self.path(n).wait_send()
         for n in range(3, 7):
             self.path(n, 1 - self.me.c).wait_recv()
+
+
+class Gather2:
+    def __init__(self, me, shard, stage, whole, at, count, local, send, recv):
+        self.me, self.whole = me, whole
+        self.rows = pl.ds(at, count)
+        if shard is not None:
+            self.shard, self.stage = shard.at[self.rows], stage.at[self.rows]
+        self.local, self.send, self.recv = local, send, recv
+
+    def one(self, z, y):
+        me = self.me
+        return self.whole.at[z, me.x, me.c, y, self.rows]
+
+    def load(self):
+        return pltpu.make_async_copy(self.shard, self.stage, self.local)
+
+    def keep(self):
+        return pltpu.make_async_copy(self.stage, self.one(self.me.z, self.me.y), self.local)
+
+    def y_hop(self, y):
+        me = self.me
+        return remote(self.stage, self.one(me.z, y), self.send.at[0], self.recv.at[0], me.next_y)
+
+    def z_hop(self, s, n, landed):
+        me = self.me
+        z = me.along(me.depth - s) if landed else me.z
+        y = 1 - me.y if n else me.y
+        src = self.one(me.z, y) if n else self.stage
+        k = 1 + n * (me.depth - 1) + s
+        return remote(src, self.one(z, y), self.send.at[k], self.recv.at[k], me.column(s))
+
+    def plane(self, x, n, peer, c):
+        k = 2 * self.me.depth + n
+        plane = self.whole.at[:, x, c, :, self.rows]
+        return remote(plane, plane, self.send.at[k], self.recv.at[k], peer)
+
+    def x_hop(self, landed):
+        me = self.me
+        return self.plane(1 - me.x if landed else me.x, 0, me.next_x, me.c)
+
+    def twin_hop(self, n, landed):
+        me = self.me
+        return self.plane(1 - me.x if n else me.x, 1 + n, me.twin, 1 - me.c if landed else me.c)
+
+    def ready(self):
+        self.load().start()
+
+    def begin(self):
+        self.load().wait()
+        self.keep().start()
+        self.y_hop(self.me.y).start()
+        for s in range(1, self.me.depth):
+            self.z_hop(s, 0, False).start()
+
+    def pass_z(self):
+        self.y_hop(self.me.y).wait_send()
+        self.y_hop(1 - self.me.y).wait_recv()
+        for s in range(1, self.me.depth):
+            self.z_hop(s, 1, False).start()
+
+    def landed(self):
+        self.keep().wait()
+        for n in range(2):
+            for s in range(1, self.me.depth):
+                self.z_hop(s, n, True).wait()
+
+    def pass_x(self):
+        self.landed()
+        self.x_hop(False).start()
+
+    def pass_twin(self):
+        self.twin_hop(0, False).start()
+
+    def arrived(self):
+        self.x_hop(False).wait_send()
+        self.x_hop(True).wait_recv()
+
+    def pass_twin_far(self):
+        self.twin_hop(1, False).start()
+
+    def end(self):
+        for n in range(2):
+            self.twin_hop(n, False).wait_send()
+            self.twin_hop(n, True).wait_recv()
 
 
 class Swap:
@@ -598,44 +683,6 @@
     return pl.BlockSpec(shape, lambda i: (0,) * len(shape), pipeline_mode=pl.Buffered(1))
 
 
-def qkv_kernel(x_ref, w_ref, p_ref, normed_ref, out_ref):
-    hat, _ = row_norm(x_ref[...].astype(F32))
-    normed = (hat * p_ref[0:1] + p_ref[1:2]).astype(BF16)
-    normed_ref[...] = normed
-    cols = out_ref.shape[1]
-    width = x_ref.shape[1]
-    for j in range(cols // 512):
-        at = slice(j * 512, (j + 1) * 512)
-        part = mm(normed, w_ref[:, at])
-        third, start = j * 512 // width, j * 512 % width
-        if third != 1:
-            row = 2 + third // 2
-            part = part + p_ref[row : row + 1, start : start + 512]
-        out_ref[:, at] = part.astype(BF16)
-
-
-def qkv_project(x, weight, params):
-    rows, width = x.shape
-    cols = weight.shape[1]
-    tile = 256
-    return pl.pallas_call(
-        qkv_kernel,
-        grid=(rows // tile,),
-        in_specs=[
-            pl.BlockSpec((tile, width), lambda i: (i, 0)),
-            resident(weight.shape),
-            resident(params.shape),
-        ],
-        out_specs=[
-            pl.BlockSpec((tile, width), lambda i: (i, 0)),
-            pl.BlockSpec((tile, cols), lambda i: (i, 0)),
-        ],
-        out_shape=[jax.ShapeDtypeStruct((rows, width), BF16), jax.ShapeDtypeStruct((rows, cols), BF16)],
-        compiler_params=pltpu.CompilerParams(vmem_limit_bytes=VMEM_CAP),
-        name="qkv_project",
-    )(x, weight, params)
-
-
 GELU_A = math.sqrt(2.0 / math.pi)
 GELU_B = 0.044715
 CHUNK = 512
@@ -779,65 +826,65 @@
     )(scaled, x, dy, wout, w1, w2, narrow, wide)
 
 
-def enter_kernel(depth, pieces, counts, *refs):
+def enter_kernel(depth, counts, *refs):
     me = Place(depth)
-    smalls = refs[: len(counts)]
-    shards = [None] + list(refs[len(counts) : len(counts) + 3])
-    tok = refs[len(counts) + 3]
-    wholes = list(refs[len(counts) + 4 : len(counts) + 7])
-    tok_whole, narrow, wide, hs = refs[len(counts) + 7 : len(counts) + 11]
-    small, small_whole, local, send, recv, small_sem, tok_stage = refs[len(counts) + 11 : len(counts) + 18]
-    stages = list(refs[len(counts) + 18 : len(counts) + 22])
-    smalls_here = refs[len(counts) + 22 :]
+    base = len(counts)
+    smalls = refs[:base]
+    qkv_shard, out_shard, fc1_shard, tok = refs[base : base + 4]
+    qkv_whole, out_whole, fc1_whole, x_out, normed_out, qkv_out, narrow, wide, hs = refs[base + 4 : base + 13]
+    small, small_stage, small_whole, qkv_stage, out_stage, fc1_stage, weight = refs[base + 13 : base + 20]
+    tok_own, tok_got, normed_tiles, qkv_tiles = refs[base + 20 : base + 24]
+    local, send, recv, small_sem, tok_sem, go, come, put_sem, tile_sem = refs[base + 24 : base + 33]
+    smalls_here = refs[base + 33 :]
+    y = me.y
+    qrows, frows = qkv_shard.shape[0] // 2, fc1_shard.shape[0] // 2
+    sems = lambda n: (local.at[n], send.at[n], recv.at[n])
+    tiny = Gather(me, small, small_stage, small_whole, 0, 16, *sems(0))
+    q_a = Gather(me, qkv_shard, qkv_stage, weight, 0, qrows, *sems(1))
+    q_b = Gather2(me, qkv_shard, qkv_stage, weight, qrows, qrows, *sems(2))
+    w_out = Gather2(me, out_shard, out_stage, out_whole, 0, out_shard.shape[0], *sems(3))
+    f_a = Gather(me, fc1_shard, fc1_stage, fc1_whole, 0, frows, *sems(4))
+    f_b = Gather(me, fc1_shard, fc1_stage, fc1_whole, frows, frows, *sems(5))
     copies = [pltpu.make_async_copy(s, h, small_sem.at[n]) for n, (s, h) in enumerate(zip(smalls, smalls_here))]
-    for copy in copies:
+    own = pltpu.make_async_copy(tok.at[y], tok_own, tok_sem)
+    for copy in copies + [own]:
         copy.start()
+    for g in (q_a, q_b, w_out, f_a, f_b):
+        g.ready()
     for copy in copies:
         copy.wait()
-    shards[0] = small
-    wholes = [small_whole] + wholes
     rows = []
     for ref, count in zip(smalls_here, counts):
         row = ref[...].astype(F32).reshape(1, count)
         rows.append(row if count == 128 else jnp.concatenate([row, jnp.zeros((1, 128 - count), F32)], axis=1))
     rows.append(jnp.zeros((16 - len(counts), 128), F32))
     small[...] = jnp.concatenate(rows, axis=0).astype(BF16)
-    gathers = [
-        Gather(me, shards[a], stages[a], wholes[a], at, count, local.at[n], send.at[n], recv.at[n])
-        for n, (a, at, count) in enumerate(pieces)
-    ]
-    first, later, begun = gathers[:3], gathers[3], gathers[4:]
-    half = tok.shape[1]
-    cut = half * 3 // 8
-    swaps = []
-    for n, (at, count) in enumerate(((0, cut), (cut, half - cut))):
-        span = pl.ds(at, count)
-        n = len(pieces) + n
-        swaps.append(
-            Swap(
-                me, tok.at[1 - me.y, span], lambda y, span=span: tok_whole.at[y, span], tok.at[me.y, span],
-                tok_stage.at[span], tok_whole.at[me.y, span], local.at[n], send.at[n, 0], recv.at[n, 0],
-            )
-        )
-    for g in gathers + swaps:
-        g.ready()
+    tiny.ready()
+    half, width = tok_own.shape
+    cut = half // 4
+
+    def trade(n):
+        span = pl.ds(n * cut, cut if n == 0 else half - cut)
+        return remote(tok.at[1 - y, span], tok_got.at[span], go.at[n], come.at[n], me.next_y)
+
     me.greet()
-    swaps[0].begin()
-    for g in first:
-        g.begin()
-    for g in first:
-        g.spread()
-    swaps[1].begin()
-    for g in [later] + begun:
-        g.begin()
-    for g in first:
-        g.from_y()
-    later.spread()
-    for g in first:
-        g.from_x()
-    for g in first:
-        g.from_corner()
-    first[0].end()
+    tiny.begin()
+    q_a.begin()
+    q_b.begin()
+    trade(0).start()
+    tiny.spread()
+    q_b.pass_z()
+    q_a.spread()
+    tiny.from_y()
+    tiny.from_x()
+    w_out.begin()
+    tiny.from_corner()
+    q_a.from_y()
+    trade(1).start()
+    q_b.pass_x()
+    q_b.pass_twin()
+    w_out.pass_z()
+    tiny.end()
     part = counts[0]
     each = 128 // part
     for d in range(depth * 8 // each):
@@ -848,59 +895,124 @@
             wide[0:3, k * 128 : (k + 1) * 128] = tile[10:13]
         narrow[:, d * 128 : (d + 1) * 128] = jnp.concatenate(tiles, axis=1)
     hs[...] = jnp.concatenate(
-        [small_whole[0, 0, 0, y].astype(F32)[13:14, 0 : counts[13]] for y in range(2)], axis=1
+        [small_whole[0, 0, 0, k].astype(F32)[13:14, 0 : counts[13]] for k in range(2)], axis=1
     )
-    later.from_y()
-    later.from_x()
-    later.from_corner()
-    for g in begun:
-        g.landed()
-    for g in first[1:]:
-        g.end()
-    later.end()
-    for swap in swaps:
-        swap.end()
+    q_a.from_x()
+    q_a.from_corner()
+    f_a.begin()
+    f_b.begin()
+    w_out.pass_x()
+    w_out.pass_twin()
+    q_b.arrived()
+    q_b.pass_twin_far()
+    q_a.end()
+    q_b.end()
+    put_weight = pltpu.make_async_copy(weight, qkv_whole, put_sem.at[0])
+    put_weight.start()
+    own.wait()
+    put_own = pltpu.make_async_copy(tok_own, x_out.at[y], put_sem.at[1])
+    put_own.start()
+    tile_rows = normed_tiles.shape[1]
+    tiles = normed_tiles.shape[0]
+
+    def puts(i, at):
+        span = pl.ds(at * half + i * tile_rows, tile_rows)
+        return (
+            pltpu.make_async_copy(normed_tiles.at[i], normed_out.at[span], tile_sem.at[0, i]),
+            pltpu.make_async_copy(qkv_tiles.at[i], qkv_out.at[span], tile_sem.at[1, i]),
+        )
+
+    def project(source, at):
+        def body(i, _):
+            hat, _ = row_norm(source[pl.ds(i * tile_rows, tile_rows), :].astype(F32))
+            normed = (hat * narrow[0:1] + narrow[1:2]).astype(BF16)
+            normed_tiles[i] = normed
+            for j in range(3 * width // 512):
+                span = slice(j * 512, (j + 1) * 512)
+                piece = mm(normed, weight[:, :, :, :, :, span].reshape(width, 512))
+                third, start = j * 512 // width, j * 512 % width
+                if third != 1:
+                    row = 2 + third // 2
+                    piece = piece + narrow[row : row + 1, start : start + 512]
+                qkv_tiles[i, :, span] = piece.astype(BF16)
+            for put in puts(i, at):
+                put.start()
+            return 0
+
+        lax.fori_loop(0, tiles, body, 0)
+
+    project(tok_own, y)
+    w_out.arrived()
+    w_out.pass_twin_far()
+    for n in range(2):
+        trade(n).wait()
+    put_got = pltpu.make_async_copy(tok_got, x_out.at[1 - y], put_sem.at[2])
+    put_got.start()
+    for i in range(tiles):
+        for put in puts(i, y):
+            put.wait()
+    project(tok_got, 1 - y)
+    f_a.landed()
+    f_b.landed()
+    w_out.end()
+    for i in range(tiles):
+        for put in puts(i, 1 - y):
+            put.wait()
+    put_weight.wait()
+    put_own.wait()
+    put_got.wait()
 
 
 def enter(smalls, qkv_weight, out_weight, fc1_weight, tokens, depth, collective_id):
     shards = [qkv_weight, out_weight, fc1_weight]
     counts = [s.shape[0] for s in smalls]
-    pieces = [(0, 0, 16)]
-    for a in (1, 2, 3):
-        rows = shards[a - 1].shape[0]
-        pieces += [(a, 0, rows)] if a == 2 else [(a, 0, rows // 2), (a, rows // 2, rows // 2)]
-    count = len(pieces) + 2
+    _, half, width = tokens.shape
+    tile = 256
     anywhere = pl.BlockSpec(memory_space=pl.ANY)
     vmem = pl.BlockSpec(memory_space=pltpu.VMEM)
+    whole = lambda s: (depth, 2, 2, 2) + s.shape
     out = pl.pallas_call(
-        functools.partial(enter_kernel, depth, pieces, counts),
+        functools.partial(enter_kernel, depth, counts),
         in_specs=[anywhere] * (len(counts) + 4),
-        out_specs=[anywhere] * 4 + [vmem] * 3,
-        out_shape=[jax.ShapeDtypeStruct((depth, 2, 2, 2) + s.shape, s.dtype) for s in shards]
+        out_specs=[anywhere] * 6 + [vmem] * 3,
+        out_shape=[jax.ShapeDtypeStruct(whole(s), s.dtype) for s in shards]
         + [
             jax.ShapeDtypeStruct(tokens.shape, tokens.dtype),
+            jax.ShapeDtypeStruct((2 * half, width), BF16),
+            jax.ShapeDtypeStruct((2 * half, 3 * width), BF16),
             jax.ShapeDtypeStruct((16, depth * 8 * counts[0]), F32),
             jax.ShapeDtypeStruct((8, depth * 8 * counts[10]), F32),
             jax.ShapeDtypeStruct((1, 2 * counts[13]), F32),
         ],
         scratch_shapes=[
             pltpu.VMEM((16, 128), BF16),
+            pltpu.VMEM((16, 128), BF16),
             pltpu.VMEM((depth, 2, 2, 2, 16, 128), BF16),
-            pltpu.SemaphoreType.DMA((count,)),
-            pltpu.SemaphoreType.DMA((count, 6 + depth)),
-            pltpu.SemaphoreType.DMA((count, 6 + depth)),
+        ]
+        + [pltpu.VMEM(s.shape, s.dtype) for s in shards]
+        + [
+            pltpu.VMEM(whole(qkv_weight), BF16),
+            pltpu.VMEM((half, width), BF16),
+            pltpu.VMEM((half, width), BF16),
+            pltpu.VMEM((half // tile, tile, width), BF16),
+            pltpu.VMEM((half // tile, tile, 3 * width), BF16),
+            pltpu.SemaphoreType.DMA((6,)),
+            pltpu.SemaphoreType.DMA((6, 2 * depth + 3)),
+            pltpu.SemaphoreType.DMA((6, 2 * depth + 3)),
             pltpu.SemaphoreType.DMA((len(counts),)),
-            pltpu.VMEM(tokens.shape[1:], tokens.dtype),
+            pltpu.SemaphoreType.DMA,
+            pltpu.SemaphoreType.DMA((2,)),
+            pltpu.SemaphoreType.DMA((2,)),
+            pltpu.SemaphoreType.DMA((3,)),
+            pltpu.SemaphoreType.DMA((2, half // tile)),
         ]
-        + [pltpu.VMEM((16, 128), BF16)]
-        + [pltpu.VMEM(s.shape, s.dtype) for s in shards]
         + [pltpu.VMEM((n,), BF16) for n in counts],
         compiler_params=pltpu.CompilerParams(
             collective_id=collective_id, has_side_effects=True, vmem_limit_bytes=VMEM_CAP
         ),
         name="enter",
     )(*smalls, *shards, tokens)
-    return flat(out[0]), flat(out[1]), out[2], out[3].reshape(-1, tokens.shape[2]), out[4], out[5], out[6]
+    return flat(out[0]), flat(out[1]), out[2], out[3].reshape(-1, width), *out[4:]
 
 
 def flat(whole):
@@ -1083,10 +1195,9 @@
     wide_in = [fc1_bias, mid_gain, mid_bias]
     part = width // devices
     heads_each = head_scale.shape[0]
-    wqkv, wout, begun, x, narrow, wide, hs = enter(
+    wqkv, wout, begun, x, normed, qkv, narrow, wide, hs = enter(
         narrow_in + wide_in + [head_scale], qkv_weight, out_weight, fc1_weight, tokens, depth, 0
     )
-    normed, qkv = qkv_project(x, wqkv, narrow)
     scaled, mixed, lse, w1, w2, dy = attend_fwd(qkv, doc_lengths, hs, begun, fc2_weight, out_cotangent, depth, 1)
     w1, w2 = flat(w1), flat(w2)
     layer, post, ffn_in, active, d_inner, d_hidden, d_low, d_scaled, grads_narrow, grads_wide = middle(

time: 693 us -> 656 us (0.947)
  Pallas kernels: 593 us -> 561 us
    pallas_call x2 -> x1, Pallas kernels: 108 us -> 82.5 us  [enter(): pl.pallas_call(functools.partial(enter_kernel, depth, counts), in_specs=[...]
    pallas_call x1, Pallas kernels: 149 us -> 139 us  [middle(): pl.pallas_call(middle_kernel, grid=(rows // tile,), in_specs=[thin, thin,...]
where the time goes in v3:
time: 656 us; the launch traced here: 652 us
  Pallas kernels  561 us (86%)
  matrix products  73.4 us (11%)
  local copies, waits for them, and re-layouts  16.6 us (3%)
    pallas_call x1, Pallas kernels, attend_bwd(): pl.pallas_call(functools.partial(attend_bwd_kernel, depth, pieces), grid=...  142 us
    pallas_call x1, Pallas kernels, middle(): pl.pallas_call(middle_kernel, grid=(rows // tile,), in_specs=[thin, thin,...  139 us
    pallas_call x1, Pallas kernels, attend_fwd(): pl.pallas_call(functools.partial(attend_fwd_kernel, depth, pieces), grid=...  117 us
    pallas_call x1, Pallas kernels, enter(): pl.pallas_call(functools.partial(enter_kernel, depth, counts), in_specs=[...  82.5 us
    pallas_call x1, Pallas kernels, leave(): pl.pallas_call(functools.partial(leave_kernel, depth, part, heads), grid=...  80.6 us
    dot_general x6, matrix products, weight_grad(): jnp.einsum('ti,tj->ij', left, right, preferred_element_type=F32)  73.4 us

profile of v3, /device:TPU:0, one launch (start us, length us, event | category | flops | bytes accessed | tf_op | source)
XLA Modules:
  0.0 652.2 jit_solution(14727279378580317784)
XLA Ops:
  0.7 82.5 %enter.1 = (bf16[4,2,2,2,32,3072]{5,4,3,2,1,0:T(8,128)(2,1)}, bf16[4,2,2,2,32,1024]{5,4,3,2,1,0:T(8,128)(2,1)}, bf16[4,2,2,2,32,4096]{5,4,3,2,1,0:T(8,128)(2,1)}...) custom-call(bf16[32]{0:T(256)(128)(2,1)} %refs_0_.3, ...), custom_call_target="tpu_custom_call" | custom-call | tf_op jit(solution)/shard_map/enter/pallas_call | solution.py:974
  83.2 116.5 %attend_fwd.1 = (bf16[2048,1024]{1,0:T(8,128)(2,1)}, f32[2048,1024]{1,0:T(8,128)}, f32[8,2,4,512]{3,2,1,0:T(4,128)}, bf16[4,2,2,2,32,4096]{5,4,3,2,1,0:T(8,128)(...) custom-call(s32[1,2,4]{2,1,0:T(2,128)} %refs_0_.5, ...), custom_call_target="tpu_custom_call", output_to_operand_aliasing={{3}: (5, {})} | custom-call | tf_op jit(solution)/shard_map/attend_fwd/pallas_call | solution.py:472
  199.7 139.5 %middle.1 = (bf16[2048,1024]{1,0:T(8,128)(2,1)}, bf16[2048,1024]{1,0:T(8,128)(2,1)}, bf16[2048,1024]{1,0:T(8,128)(2,1)}, bf16[2048,4096]{1,0:T(8,128)(2,1)}, bf1...) custom-call(bf16[2048,1024]{1,0:T(8,128)(2,1)} %get-tuple-element.60, ...), custom_call_target="tpu_custom_call" | custom-call | tf_op jit(solution)/shard_map/middle/pallas_call | solution.py:798
  339.2 0.0 copy-start.3
  339.2 0.0 slice-start
  339.2 9.5 %convolution_convert_fusion.5 = bf16[1024,1024]{1,0:T(8,128)(2,1)} fusion(bf16[2048,1024]{1,0:T(8,128)(2,1)} %get-tuple-element.73, bf16[2048,1024]{1,0:T(8,128)(2,1)} %get-tuple-element.74), kind=kOutput, calls=%fused_computation.5 | convolution fusion | flops 4296015872 | bytes 10485760 | tf_op jit(solution)/shard_map/ti,tj->ij/dot_general | solution.py:1208
  348.7 0.0 copy-done.3
  348.8 22.9 %convolution_convert_fusion.1 = bf16[4096,1024]{1,0:T(8,128)(2,1)} fusion(bf16[2048,4096]{1,0:T(8,128)(2,1)} %get-tuple-element.70, bf16[2048,1024]{1,0:T(8,128)(2,1)S(1)} %bitcast.60), kind=kOutput, calls=%fused_computation.1 | convolution fusion | flops 17184063488 | bytes 29360128 | tf_op jit(solution)/shard_map/ti,tj->ij/dot_general | solution.py:1208
  371.7 19.8 %convolution_convert_fusion = bf16[1024,4096]{1,0:T(8,128)(2,1)} fusion(bf16[2048,1024]{1,0:T(8,128)(2,1)S(1)} %copy-done.9, bf16[2048,4096]{1,0:T(8,128)(2,1)S(1)} %bitcast.67), kind=kOutput, calls=%fused_computation | convolution fusion | flops 17184063488 | bytes 29360128 | tf_op jit(solution)/shard_map/ti,tj->ij/dot_general | solution.py:1208
  391.5 142.2 %attend_bwd.1 = (bf16[2048,1024]{1,0:T(8,128)(2,1)}, bf16[2048,1024]{1,0:T(8,128)(2,1)}, bf16[2048,1024]{1,0:T(8,128)(2,1)}, f32[8,2,4,512]{3,2,1,0:T(4,128)}, f...) custom-call(s32[1,2,4]{2,1,0:T(2,128)} %refs_0_.5, ...), custom_call_target="tpu_custom_call" | custom-call | tf_op jit(solution)/shard_map/attend_bwd/pallas_call | solution.py:636
  533.8 9.5 %convolution_convert_fusion.4 = bf16[1024,1024]{1,0:T(8,128)(2,1)} fusion(bf16[2048,1024]{1,0:T(8,128)(2,1)} %get-tuple-element.82, bf16[2048,1024]{1,0:T(8,128)(2,1)} %get-tuple-element.77.refs_0_), kind=kOutput, calls=%fused_computation.4 | convolution fusion | flops 4296015872 | bytes 10485760 | tf_op jit(solution)/shard_map/ti,tj->ij/dot_general | solution.py:1208
  543.3 5.9 convolution_convert_fusion.3
  549.1 5.7 convolution_convert_fusion.2
  554.9 80.6 %leave.1 = (f32[2,1024,1024]{2,1,0:T(8,128)}, f32[32,3072]{1,0:T(8,128)}, f32[16,128]{1,0:T(8,128)}) custom-call(bf16[2048,1024]{1,0:T(8,128)(2,1)} %get-tuple-element.77.refs_0_, bf16[2048,1024]{1,0:T(8,128)(2,1)} %get-tuple-element.78.refs_1_, bf16[2048,1024]{1,0:T(8,128)(2,1)} %get-tuple-element.79.refs_2_, bf16[2048,1024]{1,0:T(8,128)(2,1)} %bitcast.54, ...), custom_call_target="tpu_custom_call" | custom-call | tf_op jit(solution)/shard_map/leave/pallas_call | solution.py:1150
  635.5 1.2 slice_bitcast_fusion.9
  636.7 1.3 slice_bitcast_fusion.1
  638.0 1.5 slice_bitcast_fusion
  639.5 4.9 copy.49
  644.4 1.2 copy-done
  645.7 3.4 copy.50
  649.1 0.7 copy.51
  649.8 0.7 copy.52
  650.5 0.8 copy.53
  651.3 0.8 copy.54
  (25 shorter events, 0.0 us)
Async XLA Ops:
  339.2 9.5 %copy-start.3 = (bf16[2,1024,1024]{2,1,0:T(8,128)(2,1)S(1)}, bf16[2,1024,1024]{2,1,0:T(8,128)(2,1)}, u32[]{:S(2)}) copy-start(bf16[2,1024,1024]{2,1,0:T(8,128)(2,1)} %get-tuple-element.62) | copy-start | bytes 12582916
  339.2 32.5 %slice-start = ((s8[16777216]{0:T(1024)(128)(4,1)}), s8[4194304]{0:T(1024)(128)(4,1)S(1)}, s32[]{:S(2)}) async-start(s8[16777216]{0:T(1024)(128)(4,1)} %bitcast.66), calls=%async_computation | async-start | bytes 8388608
  348.7 22.9 %slice-start.1 = ((s8[16777216]{0:T(1024)(128)(4,1)}), s8[4194304]{0:T(1024)(128)(4,1)S(1)}, s32[]{:S(2)}) async-start(s8[16777216]{0:T(1024)(128)(4,1)} %bitcast.66), calls=%async_computation.1 | async-start | bytes 8388608
  348.7 22.9 %slice-start.2 = ((s8[16777216]{0:T(1024)(128)(4,1)}), s8[4194304]{0:T(1024)(128)(4,1)S(1)}, s32[]{:S(2)}) async-start(s8[16777216]{0:T(1024)(128)(4,1)} %bitcast.66), calls=%async_computation.2 | async-start | bytes 8388608
  348.7 22.9 %slice-start.3 = ((s8[16777216]{0:T(1024)(128)(4,1)}), s8[4194304]{0:T(1024)(128)(4,1)S(1)}, s32[]{:S(2)}) async-start(s8[16777216]{0:T(1024)(128)(4,1)} %bitcast.66), calls=%async_computation.3 | async-start | bytes 8388608
  348.7 22.9 %copy-start.9 = (bf16[2048,1024]{1,0:T(8,128)(2,1)S(1)}, bf16[2048,1024]{1,0:T(8,128)(2,1)}, u32[]{:S(2)}) copy-start(bf16[2048,1024]{1,0:T(8,128)(2,1)} %get-tuple-element.71) | copy-start | bytes 12582916
  533.7 9.5 %copy-start.1 = (bf16[2048,1024]{1,0:T(8,128)(2,1)S(1)}, bf16[2048,1024]{1,0:T(8,128)(2,1)}, u32[]{:S(2)}) copy-start(bf16[2048,1024]{1,0:T(8,128)(2,1)} %get-tuple-element.78.refs_1_) | copy-start | bytes 12582916
  533.7 9.5 %copy-start.8 = (bf16[2048,1024]{1,0:T(8,128)(2,1)S(1)}, bf16[2048,1024]{1,0:T(8,128)(2,1)}, u32[]{:S(2)}) copy-start(bf16[2048,1024]{1,0:T(8,128)(2,1)} %get-tuple-element.82) | copy-start | bytes 12582916
  543.3 5.9 copy-start.2
  639.5 6.2 copy-start
  645.6 3.4 copy-start.6
  645.6 4.2 copy-start.7
  645.6 4.8 copy-start.5
  645.7 5.6 copy-start.4

commit v4 on v3

--- a/solution.py
+++ b/solution.py
@@ -17,7 +17,7 @@
 VMEM_CAP = 60 * 1024 * 1024
 NT = (((1,), (1,)), ((), ()))
 NN = (((1,), (0,)), ((), ()))
-FWD_STEPS = ((0, 0, 10, 11), (11, 12, 28, 29), (20, 21, 30, 31), (24, 25, 32, 32))
+FWD_STEPS = ((0, 0, 10, 11), (9, 12, 25, 26), (20, 21, 30, 31), (24, 25, 32, 32))
 BWD_STEPS = ((1, 2, 3, 4, 5), (9, 15, 20, 26, 28), (14, 19, 24, 29, 30), (18, 23, 28, 32, 32))
 
 
@@ -73,8 +73,8 @@
 
 
 class Gather:
-    def __init__(self, me, shard, stage, whole, at, count, local, send, recv):
-        self.me, self.whole = me, whole
+    def __init__(self, me, shard, stage, whole, at, count, local, send, recv, early=False):
+        self.me, self.whole, self.early = me, whole, early
         if shard is not None:
             self.shard, self.stage = shard.at[pl.ds(at, count)], stage.at[pl.ds(at, count)]
         self.rows = pl.ds(at, count)
@@ -122,8 +122,15 @@
             self.depth_hop(s, True).wait()
 
     def launch(self):
-        for n in (0, 1, 3):
+        for n in (0, 3) if self.early else (0, 1, 3):
             self.path(n).start()
+
+    def x_begin(self):
+        self.path(1).start()
+
+    def x_end(self):
+        self.path(1).wait_send()
+        self.hop(1 - self.me.x, self.me.y, 1, self.me.next_x).wait_recv()
 
     def spread(self):
         self.landed()
@@ -137,7 +144,8 @@
 
     def from_x(self):
         me = self.me
-        self.hop(1 - me.x, me.y, 1, me.next_x).wait_recv()
+        if not self.early:
+            self.hop(1 - me.x, me.y, 1, me.next_x).wait_recv()
         self.path(5).start()
 
     def from_corner(self):
@@ -147,7 +155,8 @@
 
     def end(self):
         for n in range(7):
-            self.path(n).wait_send()
+            if n != 1 or not self.early:
+                self.path(n).wait_send()
         for n in range(3, 7):
             self.path(n, 1 - self.me.c).wait_recv()
 
@@ -367,26 +376,21 @@
 
 def attend_fwd_kernel(depth, pieces, *refs):
     lengths, hs, q_ref, k_ref, v_ref = refs[:5]
-    shard, cot = refs[6:8]
-    o_ref, mixed_ref, lse_ref = refs[8:11]
-    wholes = refs[11:13]
-    cot_whole = refs[13]
-    vt, local, send, recv, shard_stage, cot_stage = refs[14:]
+    shard = refs[6]
+    o_ref, mixed_ref, lse_ref = refs[7:10]
+    wholes = refs[10:12]
+    vt, local, send, recv, shard_stage = refs[12:]
     pair = pl.program_id(0)
     me = Place(depth)
     same = same_sequence(lengths, me.y)
     gathers = [
-        Gather(me, shard if a else None, shard_stage, wholes[a], at, count, local.at[n], send.at[n], recv.at[n])
+        Gather(
+            me, shard if a else None, shard_stage, wholes[a], at, count, local.at[n], send.at[n], recv.at[n], n == 0
+        )
         for n, (a, at, count) in enumerate(pieces)
     ]
-    n = len(pieces)
-    swap = Swap(
-        me, cot.at[1 - me.y], lambda y: cot_whole.at[y], cot.at[me.y], cot_stage, cot_whole.at[me.y],
-        local.at[n], send.at[n, 0], recv.at[n, 0],
-    )
     plan = {}
     due(plan, 0, me.greet)
-    due(plan, 0, swap.ready)
     for n, g in enumerate(gathers):
         if pieces[n][0]:
             due(plan, 0, g.ready)
@@ -398,8 +402,6 @@
         due(plan, FWD_STEPS[2][n], g.from_x)
         due(plan, FWD_STEPS[3][n], g.from_corner)
         due(plan, 32, g.end)
-    due(plan, 6, swap.begin)
-    due(plan, 32, swap.end)
     last = plan.pop(32)
     rows = q_ref.shape[0]
     blocks = rows // BLOCK
@@ -456,7 +458,7 @@
     perform(pair, {pl.num_programs(0) - 1: last})
 
 
-def attend_fwd(qkv, lengths, hs, begun, shard, cot, depth, collective_id):
+def attend_fwd(qkv, lengths, hs, begun, shard, depth, collective_id):
     rows, width3 = qkv.shape
     width = width3 // 3
     pairs = width // 128
@@ -468,24 +470,23 @@
     for a, count in enumerate((begun.shape[4], shard.shape[0])):
         part = count // 2
         pieces += [(a, 0, part), (a, part, part)]
-    count = len(pieces) + 1
+    count = len(pieces)
     out = pl.pallas_call(
         functools.partial(attend_fwd_kernel, depth, pieces),
         grid=(pairs,),
-        in_specs=[smem, smem, spec(0), spec(1), spec(2)] + [anywhere] * 3,
+        in_specs=[smem, smem, spec(0), spec(1), spec(2)] + [anywhere] * 2,
         out_specs=[
             pl.BlockSpec((rows, 128), lambda p: (0, p)),
             pl.BlockSpec((rows, 128), lambda p: (0, p)),
             pl.BlockSpec((1, 2, blocks, BLOCK), lambda p: (p, 0, 0, 0)),
         ]
-        + [anywhere] * 3,
+        + [anywhere] * 2,
         out_shape=[
             jax.ShapeDtypeStruct((rows, width), BF16),
             jax.ShapeDtypeStruct((rows, width), F32),
             jax.ShapeDtypeStruct((pairs, 2, blocks, BLOCK), F32),
             jax.ShapeDtypeStruct(begun.shape, begun.dtype),
             jax.ShapeDtypeStruct((depth, 2, 2, 2) + shard.shape, shard.dtype),
-            jax.ShapeDtypeStruct(cot.shape, cot.dtype),
         ],
         input_output_aliases={5: 3},
         scratch_shapes=[
@@ -494,14 +495,13 @@
             pltpu.SemaphoreType.DMA((count, 6 + depth)),
             pltpu.SemaphoreType.DMA((count, 6 + depth)),
             pltpu.VMEM(shard.shape, shard.dtype),
-            pltpu.VMEM(cot.shape[1:], cot.dtype),
         ],
         compiler_params=pltpu.CompilerParams(
             vmem_limit_bytes=VMEM_CAP, collective_id=collective_id, has_side_effects=True
         ),
         name="attend_fwd",
-    )(lengths, hs, qkv, qkv, qkv, begun, shard, cot)
-    return out[0], out[1], out[2], out[3], out[4], out[5].reshape(rows, width)
+    )(lengths, hs, qkv, qkv, qkv, begun, shard)
+    return out[0], out[1], out[2], out[3], out[4]
 
 
 def attend_bwd_kernel(depth, pieces, *refs):
@@ -689,11 +689,38 @@
 
 
 def middle_kernel(
-    sc_ref, x_ref, dy_ref, wout, w1, w2, nar, wide,
-    lay_ref, post_ref, fin_ref, act_ref, din_ref, dhid_ref, dlow_ref, dsc_ref, gn_ref, gw_ref,
-    n_s, gp_s, dn_s,
+    depth, sc_ref, x_ref, cot, wout, w1, w2, nar, wide,
+    lay_ref, post_ref, fin_ref, act_ref, din_ref, dhid_ref, dlow_ref, dsc_ref, gn_ref, gw_ref, dy_out,
+    n_s, gp_s, dn_s, dy_s, local, go, come,
 ):
-    @pl.when(pl.program_id(0) == 0)
+    me = Place(depth)
+    step = pl.program_id(0)
+    half_tiles = dy_s.shape[1] // x_ref.shape[0]
+    load = pltpu.make_async_copy(cot.at[me.y], dy_s.at[0], local.at[0])
+    trade = remote(cot.at[1 - me.y], dy_s.at[1], go, come, me.next_y)
+    puts = [
+        pltpu.make_async_copy(dy_s.at[n], dy_out.at[1 - me.y if n else me.y], local.at[1 + n]) for n in range(2)
+    ]
+
+    @pl.when(step == 0)
+    def _():
+        load.start()
+        me.greet()
+        trade.start()
+        load.wait()
+        puts[0].start()
+
+    @pl.when(step == half_tiles)
+    def _():
+        trade.wait()
+        puts[1].start()
+
+    @pl.when(step == pl.num_programs(0) - 1)
+    def _():
+        for put in puts:
+            put.wait()
+
+    @pl.when(step == 0)
     def _():
         gn_ref[...] = jnp.zeros_like(gn_ref)
         gw_ref[...] = jnp.zeros_like(gw_ref)
@@ -736,7 +763,7 @@
 
     total = lax.fori_loop(0, ff // 128, square, zero, unroll=4)
     nrstd = lax.rsqrt(jnp.sum(total, axis=-1, keepdims=True) / ff + EPS)
-    dyl = dy_ref[...]
+    dyl = dy_s[step // half_tiles, pl.ds(step % half_tiles * tile, tile), :]
 
     def outer(j, carry):
         acc, s1, s2 = carry
@@ -788,22 +815,28 @@
     dsc_ref[...] = row_norm_back(dpost * nar[4:5], ahat, arstd).astype(BF16)
 
 
-def middle(scaled, x, dy, wout, w1, w2, narrow, wide):
+def middle(scaled, x, cot, wout, w1, w2, narrow, wide, depth, collective_id):
     rows, width = x.shape
     ff = w1.shape[1]
     tile = 256
-    thin = pl.BlockSpec((tile, width), lambda i: (i, 0))
-    fat = pl.BlockSpec((tile, ff), lambda i: (i, 0))
+    tiles = rows // tile
+
+    def at(i):
+        return ((i + tiles // 2 * lax.axis_index("sp")) % tiles, 0)
+
+    thin = pl.BlockSpec((tile, width), at)
+    fat = pl.BlockSpec((tile, ff), at)
+    anywhere = pl.BlockSpec(memory_space=pl.ANY)
     keep = lambda shape: pl.BlockSpec(shape, lambda i: (0,) * len(shape))
-    return pl.pallas_call(
-        middle_kernel,
-        grid=(rows // tile,),
+    out = pl.pallas_call(
+        functools.partial(middle_kernel, depth),
+        grid=(tiles,),
         in_specs=[
-            thin, thin, thin,
+            thin, thin, anywhere,
             resident(wout.shape), resident(w1.shape), resident(w2.shape),
             resident(narrow.shape), resident(wide.shape),
         ],
-        out_specs=[thin, thin, thin, fat, fat, thin, thin, thin, keep((6, 8, width)), keep((3, 8, ff))],
+        out_specs=[thin, thin, thin, fat, fat, thin, thin, thin, keep((6, 8, width)), keep((3, 8, ff)), anywhere],
         out_shape=[
             jax.ShapeDtypeStruct((rows, width), BF16),
             jax.ShapeDtypeStruct((rows, width), BF16),
@@ -815,15 +848,23 @@
             jax.ShapeDtypeStruct((rows, width), BF16),
             jax.ShapeDtypeStruct((6, 8, width), F32),
             jax.ShapeDtypeStruct((3, 8, ff), F32),
+            jax.ShapeDtypeStruct(cot.shape, cot.dtype),
         ],
         scratch_shapes=[
             pltpu.VMEM((tile, ff), F32),
             pltpu.VMEM((tile, ff), BF16),
             pltpu.VMEM((tile, ff), F32),
+            pltpu.VMEM(cot.shape, cot.dtype),
+            pltpu.SemaphoreType.DMA((3,)),
+            pltpu.SemaphoreType.DMA,
+            pltpu.SemaphoreType.DMA,
         ],
-        compiler_params=pltpu.CompilerParams(vmem_limit_bytes=VMEM_CAP),
+        compiler_params=pltpu.CompilerParams(
+            vmem_limit_bytes=VMEM_CAP, collective_id=collective_id, has_side_effects=True
+        ),
         name="middle",
-    )(scaled, x, dy, wout, w1, w2, narrow, wide)
+    )(scaled, x, cot, wout, w1, w2, narrow, wide)
+    return *out[:10], out[10].reshape(rows, width)
 
 
 def enter_kernel(depth, counts, *refs):
@@ -944,6 +985,9 @@
     project(tok_own, y)
     w_out.arrived()
     w_out.pass_twin_far()
+    f_a.landed()
+    f_a.x_begin()
+    f_b.landed()
     for n in range(2):
         trade(n).wait()
     put_got = pltpu.make_async_copy(tok_got, x_out.at[1 - y], put_sem.at[2])
@@ -952,8 +996,7 @@
         for put in puts(i, y):
             put.wait()
     project(tok_got, 1 - y)
-    f_a.landed()
-    f_b.landed()
+    f_a.x_end()
     w_out.end()
     for i in range(tiles):
         for put in puts(i, 1 - y):
@@ -1198,10 +1241,10 @@
     wqkv, wout, begun, x, normed, qkv, narrow, wide, hs = enter(
         narrow_in + wide_in + [head_scale], qkv_weight, out_weight, fc1_weight, tokens, depth, 0
     )
-    scaled, mixed, lse, w1, w2, dy = attend_fwd(qkv, doc_lengths, hs, begun, fc2_weight, out_cotangent, depth, 1)
+    scaled, mixed, lse, w1, w2 = attend_fwd(qkv, doc_lengths, hs, begun, fc2_weight, depth, 1)
     w1, w2 = flat(w1), flat(w2)
-    layer, post, ffn_in, active, d_inner, d_hidden, d_low, d_scaled, grads_narrow, grads_wide = middle(
-        scaled, x, dy, wout, w1, w2, narrow, wide
+    layer, post, ffn_in, active, d_inner, d_hidden, d_low, d_scaled, grads_narrow, grads_wide, dy = middle(
+        scaled, x, out_cotangent, wout, w1, w2, narrow, wide, depth, 4
     )
 
     def weight_grad(left, right):

time: 656 us -> 649 us (0.989)
    pallas_call x1, Pallas kernels: 117 us -> 103 us  [attend_fwd(): pl.pallas_call(functools.partial(attend_fwd_kernel, depth, pieces), grid=...]
where the time goes in v4:
time: 649 us; the launch traced here: 646 us
  Pallas kernels  555 us (86%)
  matrix products  73.3 us (11%)
  local copies, waits for them, and re-layouts  16.6 us (3%)
    pallas_call x1, Pallas kernels, attend_bwd(): pl.pallas_call(functools.partial(attend_bwd_kernel, depth, pieces), grid=...  143 us
    pallas_call x1, Pallas kernels, middle(): pl.pallas_call(functools.partial(middle_kernel, depth), grid=(tiles,), in...  143 us
    pallas_call x1, Pallas kernels, attend_fwd(): pl.pallas_call(functools.partial(attend_fwd_kernel, depth, pieces), grid=...  103 us
    pallas_call x1, Pallas kernels, enter(): pl.pallas_call(functools.partial(enter_kernel, depth, counts), in_specs=[...  85.4 us
    pallas_call x1, Pallas kernels, leave(): pl.pallas_call(functools.partial(leave_kernel, depth, part, heads), grid=...  80.2 us
    dot_general x6, matrix products, weight_grad(): jnp.einsum('ti,tj->ij', left, right, preferred_element_type=F32)  73.3 us

profile of v4, /device:TPU:0, one launch (start us, length us, event | category | flops | bytes accessed | tf_op | source)
XLA Modules:
  0.0 645.6 jit_solution(1596773806997467917)
XLA Ops:
  0.7 85.4 %enter.1 = (bf16[4,2,2,2,32,3072]{5,4,3,2,1,0:T(8,128)(2,1)}, bf16[4,2,2,2,32,1024]{5,4,3,2,1,0:T(8,128)(2,1)}, bf16[4,2,2,2,32,4096]{5,4,3,2,1,0:T(8,128)(2,1)}...) custom-call(bf16[32]{0:T(256)(128)(2,1)} %refs_0_.3, ...), custom_call_target="tpu_custom_call" | custom-call | tf_op jit(solution)/shard_map/enter/pallas_call | solution.py:1017
  86.0 102.7 %attend_fwd.1 = (bf16[2048,1024]{1,0:T(8,128)(2,1)}, f32[2048,1024]{1,0:T(8,128)}, f32[8,2,4,512]{3,2,1,0:T(4,128)}, bf16[4,2,2,2,32,4096]{5,4,3,2,1,0:T(8,128)(2,1)}, bf16[4,2,2,2,128,1024]{5,4,3,2,1,0:T(8,128)(2,1)}) custom-call(s32[1,2,4]{2,1,0:T(2,128)} %refs_0_.5, f32[1,16]{1,0:T(1,128)} %get-tuple-element.56.refs_1_.refs_13_, ...), custom_call_target="tpu_custom_call", output_to_operand_aliasing={{3}: (5, {})} | custom-call | tf_op jit(solution)/shard_map/attend_fwd/pallas_call | solution.py:474
  188.7 143.0 %middle.1 = (bf16[2048,1024]{1,0:T(8,128)(2,1)}, bf16[2048,1024]{1,0:T(8,128)(2,1)}, bf16[2048,1024]{1,0:T(8,128)(2,1)}, bf16[2048,4096]{1,0:T(8,128)(2,1)}, bf1...) custom-call(bf16[2048,1024]{1,0:T(8,128)(2,1)} %get-tuple-element.60, ...), custom_call_target="tpu_custom_call" | custom-call | tf_op jit(solution)/shard_map/middle/pallas_call | solution.py:831
  331.7 0.0 slice-start
  331.8 9.5 %convolution_convert_fusion.5 = bf16[1024,1024]{1,0:T(8,128)(2,1)} fusion(bf16[2048,1024]{1,0:T(8,128)(2,1)} %get-tuple-element.73, bf16[2048,1024]{1,0:T(8,128)(2,1)} %get-tuple-element.74), kind=kOutput, calls=%fused_computation.5 | convolution fusion | flops 4296015872 | bytes 10485760 | tf_op jit(solution)/shard_map/ti,tj->ij/dot_general | solution.py:1251
  341.3 0.0 copy-start.8
  341.3 22.9 %convolution_convert_fusion.1 = bf16[4096,1024]{1,0:T(8,128)(2,1)} fusion(bf16[2048,4096]{1,0:T(8,128)(2,1)} %get-tuple-element.69, bf16[2048,1024]{1,0:T(8,128)(2,1)S(1)} %bitcast.66), kind=kOutput, calls=%fused_computation.1 | convolution fusion | flops 17184063488 | bytes 29360128 | tf_op jit(solution)/shard_map/ti,tj->ij/dot_general | solution.py:1251
  364.2 0.0 slice-done
  364.2 19.8 %convolution_convert_fusion = bf16[1024,4096]{1,0:T(8,128)(2,1)} fusion(bf16[2048,1024]{1,0:T(8,128)(2,1)S(1)} %copy-done.8, bf16[2048,4096]{1,0:T(8,128)(2,1)S(1)} %bitcast.65), kind=kOutput, calls=%fused_computation | convolution fusion | flops 17184063488 | bytes 29360128 | tf_op jit(solution)/shard_map/ti,tj->ij/dot_general | solution.py:1251
  384.1 143.4 %attend_bwd.1 = (bf16[2048,1024]{1,0:T(8,128)(2,1)}, bf16[2048,1024]{1,0:T(8,128)(2,1)}, bf16[2048,1024]{1,0:T(8,128)(2,1)}, f32[8,2,4,512]{3,2,1,0:T(4,128)}, f...) custom-call(s32[1,2,4]{2,1,0:T(2,128)} %refs_0_.5, ...), custom_call_target="tpu_custom_call" | custom-call | tf_op jit(solution)/shard_map/attend_bwd/pallas_call | solution.py:636
  527.5 9.5 %convolution_convert_fusion.4 = bf16[1024,1024]{1,0:T(8,128)(2,1)} fusion(bf16[2048,1024]{1,0:T(8,128)(2,1)} %get-tuple-element.82, bf16[2048,1024]{1,0:T(8,128)(2,1)} %get-tuple-element.77.refs_0_), kind=kOutput, calls=%fused_computation.4 | convolution fusion | flops 4296015872 | bytes 10485760 | tf_op jit(solution)/shard_map/ti,tj->ij/dot_general | solution.py:1251
  537.0 5.8 convolution_convert_fusion.3
  542.8 5.8 convolution_convert_fusion.2
  548.6 80.2 %leave.1 = (f32[2,1024,1024]{2,1,0:T(8,128)}, f32[32,3072]{1,0:T(8,128)}, f32[16,128]{1,0:T(8,128)}) custom-call(bf16[2048,1024]{1,0:T(8,128)(2,1)} %get-tuple-element.77.refs_0_, bf16[2048,1024]{1,0:T(8,128)(2,1)} %get-tuple-element.78.refs_1_, bf16[2048,1024]{1,0:T(8,128)(2,1)} %get-tuple-element.79.refs_2_, bf16[2048,1024]{1,0:T(8,128)(2,1)} %bitcast.54, ...), custom_call_target="tpu_custom_call" | custom-call | tf_op jit(solution)/shard_map/leave/pallas_call | solution.py:1193
  628.8 1.2 slice_bitcast_fusion.9
  630.0 1.3 slice_bitcast_fusion.1
  631.3 1.5 slice_bitcast_fusion
  632.8 4.9 copy.49
  637.8 1.2 copy-done
  639.0 3.4 copy.50
  642.4 0.7 copy.51
  643.1 0.7 copy.52
  643.8 0.8 copy.53
  644.6 0.8 copy.54
  (25 shorter events, 0.0 us)
Async XLA Ops:
  331.7 9.5 %copy-start.9 = (bf16[2,1024,1024]{2,1,0:T(8,128)(2,1)S(1)}, bf16[2,1024,1024]{2,1,0:T(8,128)(2,1)}, u32[]{:S(2)}) copy-start(bf16[2,1024,1024]{2,1,0:T(8,128)(2,1)} %get-tuple-element.70) | copy-start | bytes 12582916
  331.7 32.4 %slice-start = ((s8[16777216]{0:T(1024)(128)(4,1)}), s8[4194304]{0:T(1024)(128)(4,1)S(1)}, s32[]{:S(2)}) async-start(s8[16777216]{0:T(1024)(128)(4,1)} %bitcast.64), calls=%async_computation | async-start | bytes 8388608
  341.3 22.9 %slice-start.1 = ((s8[16777216]{0:T(1024)(128)(4,1)}), s8[4194304]{0:T(1024)(128)(4,1)S(1)}, s32[]{:S(2)}) async-start(s8[16777216]{0:T(1024)(128)(4,1)} %bitcast.64), calls=%async_computation.1 | async-start | bytes 8388608
  341.3 22.9 %slice-start.2 = ((s8[16777216]{0:T(1024)(128)(4,1)}), s8[4194304]{0:T(1024)(128)(4,1)S(1)}, s32[]{:S(2)}) async-start(s8[16777216]{0:T(1024)(128)(4,1)} %bitcast.64), calls=%async_computation.2 | async-start | bytes 8388608
  341.3 22.9 %slice-start.3 = ((s8[16777216]{0:T(1024)(128)(4,1)}), s8[4194304]{0:T(1024)(128)(4,1)S(1)}, s32[]{:S(2)}) async-start(s8[16777216]{0:T(1024)(128)(4,1)} %bitcast.64), calls=%async_computation.3 | async-start | bytes 8388608
  341.3 22.9 %copy-start.8 = (bf16[2048,1024]{1,0:T(8,128)(2,1)S(1)}, bf16[2048,1024]{1,0:T(8,128)(2,1)}, u32[]{:S(2)}) copy-start(bf16[2048,1024]{1,0:T(8,128)(2,1)} %get-tuple-element.71) | copy-start | bytes 12582916
  527.5 9.5 %copy-start.1 = (bf16[2048,1024]{1,0:T(8,128)(2,1)S(1)}, bf16[2048,1024]{1,0:T(8,128)(2,1)}, u32[]{:S(2)}) copy-start(bf16[2048,1024]{1,0:T(8,128)(2,1)} %get-tuple-element.78.refs_1_) | copy-start | bytes 12582916
  527.5 9.5 %copy-start.7 = (bf16[2048,1024]{1,0:T(8,128)(2,1)S(1)}, bf16[2048,1024]{1,0:T(8,128)(2,1)}, u32[]{:S(2)}) copy-start(bf16[2048,1024]{1,0:T(8,128)(2,1)} %get-tuple-element.82) | copy-start | bytes 12582916
  537.0 5.8 copy-start.2
  632.8 6.2 copy-start
  639.0 3.4 copy-start.5
  639.0 4.2 copy-start.6
  639.0 4.8 copy-start.4
  639.0 5.6 copy-start.3

commit v5 on v4

--- a/solution.py
+++ b/solution.py
@@ -685,13 +685,13 @@
 
 GELU_A = math.sqrt(2.0 / math.pi)
 GELU_B = 0.044715
-CHUNK = 512
+CHUNK = 1024
 
 
 def middle_kernel(
     depth, sc_ref, x_ref, cot, wout, w1, w2, nar, wide,
     lay_ref, post_ref, fin_ref, act_ref, din_ref, dhid_ref, dlow_ref, dsc_ref, gn_ref, gw_ref, dy_out,
-    n_s, gp_s, dn_s, dy_s, local, go, come,
+    n_s, gp_s, da_s, dy_s, local, go, come,
 ):
     me = Place(depth)
     step = pl.program_id(0)
@@ -736,70 +736,63 @@
     fin = (hhat * nar[7:8] + nar[8:9]).astype(BF16)
     fin_ref[...] = fin
 
+    dyl = dy_s[step // half_tiles, pl.ds(step % half_tiles * tile, tile), :]
+    spans = [slice(j * CHUNK, (j + 1) * CHUNK) for j in range(chunks)]
+
     def lanes(values):
-        return jnp.sum(values.reshape(tile, CHUNK // 128, 128), axis=1)
-
-    def inner(j, total):
-        at = pl.ds(pl.multiple_of(j * CHUNK, CHUNK), CHUNK)
+        total = values[:, 0:128]
+        for q in range(1, CHUNK // 128):
+            total = total + values[:, q * 128 : (q + 1) * 128]
+        return total
+
+    first = jnp.zeros((tile, 128), F32)
+    second = jnp.zeros((tile, 128), F32)
+    near = None
+    for at in spans:
         u = mm(fin, w1[:, at]) + wide[0:1, at]
+        da_s[:, at] = mm(dyl, w2[at, :], NT)
         u2 = u * u
         t = jnp.tanh(u * (GELU_A + GELU_A * GELU_B * u2))
         half = 0.5 * (1.0 + t)
         n = u * half
         gp_s[:, at] = (half + n * (1.0 - t) * (GELU_A + 3.0 * GELU_A * GELU_B * u2)).astype(BF16)
+        if near is None:
+            near = jnp.mean(n, axis=-1, keepdims=True)
+        n = n - near
         n_s[:, at] = n
-        for q in range(CHUNK // 128):
-            total = total + n[:, q * 128 : (q + 1) * 128]
-        return total
-
-    zero = jnp.zeros((tile, 128), F32)
-    total = lax.fori_loop(0, chunks, inner, zero, unroll=8)
-    nmean = jnp.sum(total, axis=-1, keepdims=True) / ff
-
-    def square(j, total):
-        at = pl.ds(pl.multiple_of(j * 128, 128), 128)
-        c = n_s[:, at] - nmean
-        return total + c * c
-
-    total = lax.fori_loop(0, ff // 128, square, zero, unroll=4)
-    nrstd = lax.rsqrt(jnp.sum(total, axis=-1, keepdims=True) / ff + EPS)
-    dyl = dy_s[step // half_tiles, pl.ds(step % half_tiles * tile, tile), :]
-
-    def outer(j, carry):
-        acc, s1, s2 = carry
-        at = pl.ds(pl.multiple_of(j * CHUNK, CHUNK), CHUNK)
+        first = first + lanes(n)
+        second = second + lanes(n * n)
+    nmean = jnp.sum(first, axis=-1, keepdims=True) / ff
+    spread = jnp.sum(second, axis=-1, keepdims=True) / ff - nmean * nmean
+    nrstd = lax.rsqrt(jnp.maximum(spread, 0.0) + EPS)
+
+    acc = jnp.zeros((tile, width), F32)
+    s1 = jnp.zeros((tile, 128), F32)
+    s2 = jnp.zeros((tile, 128), F32)
+    for at in spans:
         nh = (n_s[:, at] - nmean) * nrstd
         n_s[:, at] = nh
-        act = (nh * wide[1:2, at] + wide[2:3, at]).astype(BF16)
+        gain = wide[1:2, at]
+        act = (nh * gain + wide[2:3, at]).astype(BF16)
         act_ref[:, at] = act
         acc = acc + mm(act, w2[at, :])
-        da = mm(dyl, w2[at, :], NT)
+        da = da_s[:, at]
         danh = da * nh
         gw_ref[1, :, at] += fold_rows(danh)
         gw_ref[2, :, at] += fold_rows(da)
-        gain = wide[1:2, at]
-        dg = da * gain
-        dgn = danh * gain
-        dn_s[:, at] = dg
-        for q in range(CHUNK // 128):
-            s1 = s1 + dg[:, q * 128 : (q + 1) * 128]
-            s2 = s2 + dgn[:, q * 128 : (q + 1) * 128]
-        return acc, s1, s2
-
-    acc, s1, s2 = lax.fori_loop(0, chunks, outer, (jnp.zeros((tile, width), F32), zero, zero), unroll=8)
+        s1 = s1 + lanes(da * gain)
+        s2 = s2 + lanes(danh * gain)
     lay_ref[...] = (hidden + acc + nar[9:10]).astype(BF16)
     s1 = jnp.sum(s1, axis=-1, keepdims=True) / ff
     s2 = jnp.sum(s2, axis=-1, keepdims=True) / ff
 
-    def inner_back(j, acc):
-        at = pl.ds(pl.multiple_of(j * CHUNK, CHUNK), CHUNK)
-        dn = nrstd * (dn_s[:, at] - s1 - n_s[:, at] * s2)
+    dffn = jnp.zeros((tile, width), F32)
+    for at in spans:
+        dn = nrstd * (da_s[:, at] * wide[1:2, at] - s1 - n_s[:, at] * s2)
         din = (dn * gp_s[:, at].astype(F32)).astype(BF16)
         din_ref[:, at] = din
         gw_ref[0, :, at] += fold_rows(din.astype(F32))
-        return acc + mm(din, w1[:, at], NT)
-
-    dffn = lax.fori_loop(0, chunks, inner_back, jnp.zeros((tile, width), F32), unroll=8)
+        dffn = dffn + mm(din, w1[:, at], NT)
     dy = dyl.astype(F32)
     gn_ref[5] += fold_rows(dy)
     gn_ref[3] += fold_rows(dffn * hhat)

time: 649 us -> 646 us (level)
  no operation moved by 1% of the time
where the time goes in v5:
time: 646 us; the launch traced here: 642 us
  Pallas kernels  551 us (85%)
  matrix products  73.3 us (11%)
  local copies, waits for them, and re-layouts  16.6 us (3%)
    pallas_call x1, Pallas kernels, attend_bwd(): pl.pallas_call(functools.partial(attend_bwd_kernel, depth, pieces), grid=...  143 us
    pallas_call x1, Pallas kernels, middle(): pl.pallas_call(functools.partial(middle_kernel, depth), grid=(tiles,), in...  139 us
    pallas_call x1, Pallas kernels, attend_fwd(): pl.pallas_call(functools.partial(attend_fwd_kernel, depth, pieces), grid=...  103 us
    pallas_call x1, Pallas kernels, enter(): pl.pallas_call(functools.partial(enter_kernel, depth, counts), in_specs=[...  85.4 us
    pallas_call x1, Pallas kernels, leave(): pl.pallas_call(functools.partial(leave_kernel, depth, part, heads), grid=...  80.2 us
    dot_general x6, matrix products, weight_grad(): jnp.einsum('ti,tj->ij', left, right, preferred_element_type=F32)  73.3 us

profile of v5, /device:TPU:0, one launch (start us, length us, event | category | flops | bytes accessed | tf_op | source)
XLA Modules:
  0.0 641.7 jit_solution(5001978583803474521)
XLA Ops:
  0.7 85.4 %enter.1 = (bf16[4,2,2,2,32,3072]{5,4,3,2,1,0:T(8,128)(2,1)}, bf16[4,2,2,2,32,1024]{5,4,3,2,1,0:T(8,128)(2,1)}, bf16[4,2,2,2,32,4096]{5,4,3,2,1,0:T(8,128)(2,1)}...) custom-call(bf16[32]{0:T(256)(128)(2,1)} %refs_0_.3, ...), custom_call_target="tpu_custom_call" | custom-call | tf_op jit(solution)/shard_map/enter/pallas_call | solution.py:1010
  86.0 102.7 %attend_fwd.1 = (bf16[2048,1024]{1,0:T(8,128)(2,1)}, f32[2048,1024]{1,0:T(8,128)}, f32[8,2,4,512]{3,2,1,0:T(4,128)}, bf16[4,2,2,2,32,4096]{5,4,3,2,1,0:T(8,128)(2,1)}, bf16[4,2,2,2,128,1024]{5,4,3,2,1,0:T(8,128)(2,1)}) custom-call(s32[1,2,4]{2,1,0:T(2,128)} %refs_0_.5, f32[1,16]{1,0:T(1,128)} %get-tuple-element.56.refs_1_.refs_13_, ...), custom_call_target="tpu_custom_call", output_to_operand_aliasing={{3}: (5, {})} | custom-call | tf_op jit(solution)/shard_map/attend_fwd/pallas_call | solution.py:474
  188.7 139.2 %middle.1 = (bf16[2048,1024]{1,0:T(8,128)(2,1)}, bf16[2048,1024]{1,0:T(8,128)(2,1)}, bf16[2048,1024]{1,0:T(8,128)(2,1)}, bf16[2048,4096]{1,0:T(8,128)(2,1)}, bf1...) custom-call(bf16[2048,1024]{1,0:T(8,128)(2,1)} %get-tuple-element.60, ...), custom_call_target="tpu_custom_call" | custom-call | tf_op jit(solution)/shard_map/middle/pallas_call | solution.py:824
  327.9 0.0 copy-start.9
  327.9 0.0 slice-start
  327.9 9.5 %convolution_convert_fusion.5 = bf16[1024,1024]{1,0:T(8,128)(2,1)} fusion(bf16[2048,1024]{1,0:T(8,128)(2,1)} %get-tuple-element.73, bf16[2048,1024]{1,0:T(8,128)(2,1)} %get-tuple-element.74), kind=kOutput, calls=%fused_computation.5 | convolution fusion | flops 4296015872 | bytes 10485760 | tf_op jit(solution)/shard_map/ti,tj->ij/dot_general | solution.py:1244
  337.4 0.0 copy-done.9
  337.5 22.9 %convolution_convert_fusion.1 = bf16[4096,1024]{1,0:T(8,128)(2,1)} fusion(bf16[2048,4096]{1,0:T(8,128)(2,1)} %get-tuple-element.69, bf16[2048,1024]{1,0:T(8,128)(2,1)S(1)} %bitcast.66), kind=kOutput, calls=%fused_computation.1 | convolution fusion | flops 17184063488 | bytes 29360128 | tf_op jit(solution)/shard_map/ti,tj->ij/dot_general | solution.py:1244
  360.4 19.8 %convolution_convert_fusion = bf16[1024,4096]{1,0:T(8,128)(2,1)} fusion(bf16[2048,1024]{1,0:T(8,128)(2,1)S(1)} %copy-done.8, bf16[2048,4096]{1,0:T(8,128)(2,1)S(1)} %bitcast.65), kind=kOutput, calls=%fused_computation | convolution fusion | flops 17184063488 | bytes 29360128 | tf_op jit(solution)/shard_map/ti,tj->ij/dot_general | solution.py:1244
  380.2 143.4 %attend_bwd.1 = (bf16[2048,1024]{1,0:T(8,128)(2,1)}, bf16[2048,1024]{1,0:T(8,128)(2,1)}, bf16[2048,1024]{1,0:T(8,128)(2,1)}, f32[8,2,4,512]{3,2,1,0:T(4,128)}, f...) custom-call(s32[1,2,4]{2,1,0:T(2,128)} %refs_0_.5, ...), custom_call_target="tpu_custom_call" | custom-call | tf_op jit(solution)/shard_map/attend_bwd/pallas_call | solution.py:636
  523.7 9.5 %convolution_convert_fusion.4 = bf16[1024,1024]{1,0:T(8,128)(2,1)} fusion(bf16[2048,1024]{1,0:T(8,128)(2,1)} %get-tuple-element.82, bf16[2048,1024]{1,0:T(8,128)(2,1)} %get-tuple-element.77.refs_0_), kind=kOutput, calls=%fused_computation.4 | convolution fusion | flops 4296015872 | bytes 10485760 | tf_op jit(solution)/shard_map/ti,tj->ij/dot_general | solution.py:1244
  533.2 5.8 convolution_convert_fusion.3
  539.0 5.8 convolution_convert_fusion.2
  544.7 80.2 %leave.1 = (f32[2,1024,1024]{2,1,0:T(8,128)}, f32[32,3072]{1,0:T(8,128)}, f32[16,128]{1,0:T(8,128)}) custom-call(bf16[2048,1024]{1,0:T(8,128)(2,1)} %get-tuple-element.77.refs_0_, bf16[2048,1024]{1,0:T(8,128)(2,1)} %get-tuple-element.78.refs_1_, bf16[2048,1024]{1,0:T(8,128)(2,1)} %get-tuple-element.79.refs_2_, bf16[2048,1024]{1,0:T(8,128)(2,1)} %bitcast.54, ...), custom_call_target="tpu_custom_call" | custom-call | tf_op jit(solution)/shard_map/leave/pallas_call | solution.py:1186
  625.0 1.2 slice_bitcast_fusion.9
  626.2 1.3 slice_bitcast_fusion.1
  627.5 1.5 slice_bitcast_fusion
  629.0 4.9 copy.49
  633.9 1.2 copy-done
  635.2 3.4 copy.50
  638.6 0.7 copy.51
  639.3 0.7 copy.52
  640.0 0.8 copy.53
  640.8 0.8 copy.54
  (25 shorter events, 0.0 us)
Async XLA Ops:
  327.9 9.5 %copy-start.9 = (bf16[2,1024,1024]{2,1,0:T(8,128)(2,1)S(1)}, bf16[2,1024,1024]{2,1,0:T(8,128)(2,1)}, u32[]{:S(2)}) copy-start(bf16[2,1024,1024]{2,1,0:T(8,128)(2,1)} %get-tuple-element.70) | copy-start | bytes 12582916
  327.9 32.4 %slice-start = ((s8[16777216]{0:T(1024)(128)(4,1)}), s8[4194304]{0:T(1024)(128)(4,1)S(1)}, s32[]{:S(2)}) async-start(s8[16777216]{0:T(1024)(128)(4,1)} %bitcast.64), calls=%async_computation | async-start | bytes 8388608
  337.4 22.9 %slice-start.1 = ((s8[16777216]{0:T(1024)(128)(4,1)}), s8[4194304]{0:T(1024)(128)(4,1)S(1)}, s32[]{:S(2)}) async-start(s8[16777216]{0:T(1024)(128)(4,1)} %bitcast.64), calls=%async_computation.1 | async-start | bytes 8388608
  337.4 22.9 %slice-start.2 = ((s8[16777216]{0:T(1024)(128)(4,1)}), s8[4194304]{0:T(1024)(128)(4,1)S(1)}, s32[]{:S(2)}) async-start(s8[16777216]{0:T(1024)(128)(4,1)} %bitcast.64), calls=%async_computation.2 | async-start | bytes 8388608
  337.4 22.9 %slice-start.3 = ((s8[16777216]{0:T(1024)(128)(4,1)}), s8[4194304]{0:T(1024)(128)(4,1)S(1)}, s32[]{:S(2)}) async-start(s8[16777216]{0:T(1024)(128)(4,1)} %bitcast.64), calls=%async_computation.3 | async-start | bytes 8388608
  337.4 22.9 %copy-start.8 = (bf16[2048,1024]{1,0:T(8,128)(2,1)S(1)}, bf16[2048,1024]{1,0:T(8,128)(2,1)}, u32[]{:S(2)}) copy-start(bf16[2048,1024]{1,0:T(8,128)(2,1)} %get-tuple-element.71) | copy-start | bytes 12582916
  523.7 9.5 %copy-start.1 = (bf16[2048,1024]{1,0:T(8,128)(2,1)S(1)}, bf16[2048,1024]{1,0:T(8,128)(2,1)}, u32[]{:S(2)}) copy-start(bf16[2048,1024]{1,0:T(8,128)(2,1)} %get-tuple-element.78.refs_1_) | copy-start | bytes 12582916
  523.7 9.5 %copy-start.7 = (bf16[2048,1024]{1,0:T(8,128)(2,1)S(1)}, bf16[2048,1024]{1,0:T(8,128)(2,1)}, u32[]{:S(2)}) copy-start(bf16[2048,1024]{1,0:T(8,128)(2,1)} %get-tuple-element.82) | copy-start | bytes 12582916
  533.2 5.8 copy-start.2
  629.0 6.2 copy-start
  635.1 3.4 copy-start.5
  635.2 4.2 copy-start.6
  635.2 4.8 copy-start.4
  635.2 5.6 copy-start.3
